TPU v7x, 256 devices: a whole 4x4x8 slice. The times are simulated.
256 devices in a mesh: space: 32 (over z, y_lo, core), mem: 8 (over x, y_hi).
Axes of the slice: x: 4, y: 4 (y_hi: 2, y_lo: 2; y = y_hi * 2 + y_lo), z: 8, core: 2. Of those that a mesh axis runs over, the one named last changes fastest.
Arguments:
- members: bfloat16 [1024, 768, 2, 384], P(('space', 'mem')), may hold values from -24 to 24
- state: float32 [768, 2, 384], P('space'), may hold values from -6 to 6
- cotangent: float32 [768, 2, 384], P('space'), may hold values from -6 to 6
- conv_in: float32 [3, 3, 128, 2], replicated, may hold values from -1.5 to 1.5
- conv_out: float32 [3, 3, 2, 128], replicated, may hold values from -0.1875 to 0.1875
- bias: float32 [128], replicated, may hold values from -3 to 3
Outputs:
- increment: float32 [768, 2, 384], P('space')
- response: float32 [768, 2, 384], P('space')
All inputs are finite; a program needn't handle non-finite values.
Results may differ from a plain program's by a relative error of at most 0.0045.
Values may be sent and summed in bfloat16 or wider, within the bound.
No kernel may reach another device: no remote copies, remote signals or barrier semaphores. Data moves between devices by JAX's collectives and lax.ppermute only.
A program may use at most 64 MiB of HBM per device.

v0:
```python
import functools

import jax
import jax.numpy as jnp
import ml_dtypes
import numpy as np
from jax import lax
from jax.experimental import pallas as pl
from jax.experimental.pallas import tpu as pltpu
from jax.sharding import PartitionSpec as P

HALF = 16
GROUP = 32
BF = jnp.bfloat16
F32 = jnp.float32


def taps(distance):
    ratio = distance.astype(np.float32) / np.float32(HALF + 1.0)
    value = np.float32(1.0) - ratio * ratio
    return np.where(distance <= HALF, value, np.float32(0.0)).astype(ml_dtypes.bfloat16)


def shifted(value, step):
    if step == 1:
        return value
    lats = value.shape[-1]
    lane = lax.broadcasted_iota(jnp.int32, value.shape, value.ndim - 1)
    if step == 0:
        return jnp.where(lane == 0, 0.0, pltpu.roll(value, 1, value.ndim - 1))
    return jnp.where(lane == lats - 1, 0.0, pltpu.roll(value, lats - 1, value.ndim - 1))


def split_high_low(value):
    high = value.astype(BF)
    low = (value - high.astype(F32)).astype(BF)
    return high, low


def stack_taps(wide_ref, tap_ref):
    for tile in range(wide_ref.shape[0]):
        value = wide_ref[tile]
        rows = value.shape[0] // 8
        high = value.astype(BF).astype(F32)
        low = value - high
        high = high.reshape(rows, 1, 8, 128)
        low = low.reshape(rows, 1, 8, 128)
        both = jnp.concatenate([high, low, high, low], axis=1).reshape(rows * GROUP, 128)
        tap_ref[:, tile * 128 : (tile + 1) * 128] = both.astype(BF)


def put_taps(wide_ref, plane, first_row, var):
    rows = plane.shape[0]
    for step in range(3):
        moved = shifted(plane, step)
        for tile in range(wide_ref.shape[0]):
            start = first_row * 8 + 2 * step + var
            wide_ref[tile, pl.ds(start, rows, stride=8), :] = moved[:, tile * 128 : (tile + 1) * 128]


def put_ones(wide_ref, value):
    rows = wide_ref.shape[1] // 8
    for tile in range(wide_ref.shape[0]):
        wide_ref[tile, pl.ds(6, rows, stride=8), :] = jnp.full((rows, 128), value, F32)
        wide_ref[tile, pl.ds(7, rows, stride=8), :] = jnp.zeros((rows, 128), F32)


def fold_hidden(hidden, back_weight, fold_ref, row):
    high, low = split_high_low(hidden)
    product = jnp.dot(
        back_weight, jnp.concatenate([high, low], axis=0), preferred_element_type=F32
    )
    product = product[:24] + product[24:]
    total = product[8:16] + shifted(product[0:8], 0) + shifted(product[16:24], 2)
    for tile in range(fold_ref.shape[0]):
        fold_ref[tile, pl.ds(pl.multiple_of(row * 8, 8), 8), :] = total[:, tile * 128 : (tile + 1) * 128]


def folded(fold_ref, rows, var):
    tiles = []
    for tile in range(fold_ref.shape[0]):
        tiles.append(
            sum(
                fold_ref[tile, pl.ds(10 * step + var, rows, stride=8), :] for step in range(3)
            )
        )
    return jnp.concatenate(tiles, axis=1)


def fill_padded(main_ref, before_ref, after_ref, var_from, wide_ref):
    rows = main_ref.shape[0]
    for var in range(2):
        put_taps(wide_ref, main_ref[:, var, :], 2, var)
        for row in range(2):
            line = var_from + var
            put_taps(wide_ref, before_ref[row, line : line + 1, :], row, var)
            put_taps(wide_ref, after_ref[row, line : line + 1, :], rows + 2 + row, var)


def gradient_kernel(
    state_ref, cot_ref, before_ref, after_ref, front_ref, back_ref, out_ref, wide, state_taps, cot_taps, fold
):
    rows = state_ref.shape[0]
    put_ones(wide, 1.0)
    fill_padded(state_ref, before_ref, after_ref, 0, wide)
    stack_taps(wide, state_taps)
    fill_padded(cot_ref, before_ref, after_ref, 2, wide)
    stack_taps(wide, cot_taps)

    def step(row, carry):
        window = pl.ds(pl.multiple_of(row * GROUP, GROUP), 3 * GROUP)
        activity = jnp.tanh(jnp.dot(front_ref[0], state_taps[window, :], preferred_element_type=F32))
        slopes = 1.0 - activity * activity
        hidden = slopes * jnp.dot(front_ref[1], cot_taps[window, :], preferred_element_type=F32)
        fold_hidden(hidden, back_ref[0], fold, row)
        return carry

    lax.fori_loop(0, rows + 2, step, 0, unroll=2)
    for var in range(2):
        plane = (cot_ref[:, var, :] + folded(fold, rows, var)).astype(BF)
        for pair in range(out_ref.shape[0] // 2):
            out_ref[2 * pair + var] = plane


def slopes_kernel(state_ref, before_ref, after_ref, front_ref, out_ref, wide, state_taps):
    rows = state_ref.shape[0]
    put_ones(wide, 1.0)
    fill_padded(state_ref, before_ref, after_ref, 0, wide)
    stack_taps(wide, state_taps)

    def step(row, carry):
        window = pl.ds(pl.multiple_of(row * GROUP, GROUP), 3 * GROUP)
        activity = jnp.tanh(jnp.dot(front_ref[0], state_taps[window, :], preferred_element_type=F32))
        out_ref[row] = 1.0 - activity * activity
        return carry

    lax.fori_loop(0, rows + 2, step, 0, unroll=2)


def response_kernel(
    scale, copies_ref, slopes_ref, front_ref, back_ref, incr_out, resp_out, wide, incr_taps, fold
):
    rows = incr_out.shape[0]
    planes = []
    put_ones(wide, 0.0)
    for var in range(2):
        window = pl.ds(var * (rows + 4), rows + 4)
        plane = copies_ref[0, window, :].astype(F32)
        for group in range(1, copies_ref.shape[0]):
            plane = plane + copies_ref[group, window, :].astype(F32)
        plane = plane * scale
        planes.append(plane)
        put_taps(wide, plane, 0, var)
    stack_taps(wide, incr_taps)

    def step(row, carry):
        window = pl.ds(pl.multiple_of(row * GROUP, GROUP), 3 * GROUP)
        hidden = slopes_ref[row] * jnp.dot(
            front_ref[0], incr_taps[window, :], preferred_element_type=F32
        )
        fold_hidden(hidden, back_ref[1], fold, row)
        return carry

    lax.fori_loop(0, rows + 2, step, 0, unroll=2)
    for var in range(2):
        increment = planes[var][2 : 2 + rows]
        incr_out[:, var, :] = increment
        resp_out[:, var, :] = increment + folded(fold, rows, var)


def planes_kernel(core_ref, members_ref, keep_ref, give_ref, lines):
    core = core_ref[0]
    rows = members_ref.shape[1]
    lines[...] = members_ref.reshape(rows * 2, 128)[...].astype(F32)
    keep_ref[0] = lines[pl.ds(core, rows, stride=2), :].astype(BF)
    give_ref[0] = lines[pl.ds(1 - core, rows, stride=2), :].astype(BF)


def member_kernel(
    span, keep_ref, take_ref, field_ref, lat_ref, lon_ref, out_ref, field, banded, total
):
    step = pl.program_id(0)
    lons = field_ref.shape[0]
    blocks = out_ref.shape[0]
    rows = lons // blocks

    @pl.when(step == 0)
    def _():
        field[...] = field_ref[...].astype(F32)
        total[...] = jnp.zeros_like(total)

    for member_ref in (keep_ref, take_ref):
        for start in range(0, lons, span):
            window = pl.ds(start, span)
            product = (member_ref[0, window, :].astype(F32) * field[window, :]).astype(BF)
            banded[pl.ds(HALF + start, span), :] = jnp.dot(
                product, lat_ref[...], preferred_element_type=F32
            ).astype(BF)
        banded[pl.ds(0, HALF), :] = banded[pl.ds(lons, HALF), :]
        banded[pl.ds(HALF + lons, HALF), :] = banded[pl.ds(HALF, HALF), :]
        for start in range(0, lons, span):
            spread = jnp.dot(
                lon_ref[...], banded[pl.ds(start, span + 2 * HALF), :], preferred_element_type=F32
            )
            window = pl.ds(8 + start, span)
            total[window, :] += member_ref[0, pl.ds(start, span), :].astype(F32) * spread

    @pl.when(step == pl.num_programs(0) - 1)
    def _():
        total[pl.ds(0, 8), :] = total[pl.ds(lons, 8), :]
        total[pl.ds(lons + 8, 8), :] = total[pl.ds(8, 8), :]
        for block in range(blocks):
            out_ref[block] = total[pl.ds(6 + block * rows, rows + 4), :].astype(BF)


def sum_kernel(parts_ref, out_ref):
    for var in range(2):
        plane = parts_ref[var].astype(F32)
        for pair in range(1, parts_ref.shape[0] // 2):
            plane = plane + parts_ref[2 * pair + var].astype(F32)
        plane = plane.astype(BF)
        for group in range(out_ref.shape[0]):
            out_ref[group, pl.ds(var * plane.shape[0], plane.shape[0]), :] = plane


def weight_stacks(conv_in, conv_out, bias):
    first = jnp.transpose(conv_in, (0, 1, 3, 2))
    hidden = first.shape[-1]
    front = jnp.stack([first, conv_out[::-1, ::-1]]).reshape(2, 3, 6, hidden)
    ones = jnp.zeros((2, 3, 2, hidden), F32).at[0, 1, 0].set(bias)
    front = jnp.concatenate([front, ones], axis=2)
    back = jnp.stack([first[::-1, ::-1], conv_out])
    back = jnp.transpose(back, (0, 2, 1, 3, 4)).reshape(2, 3, 6, hidden)
    back = jnp.pad(back, ((0, 0), (0, 0), (0, 2), (0, 0))).reshape(2, 24, hidden)
    high = lax.reduce_precision(front, 8, 7)
    low = front - high
    front = jnp.stack([high, high, low, low], axis=2).reshape(2, 3 * GROUP, hidden)
    front = jnp.transpose(front, (0, 2, 1)).astype(BF)
    high = lax.reduce_precision(back, 8, 7)
    low = back - high
    back = jnp.concatenate([high, low], axis=1)
    back = jnp.concatenate([back, back], axis=2).astype(BF)
    return front, back


def per_device(members, state, cotangent, conv_in, conv_out, bias):
    blocks = lax.axis_size("space")
    groups = lax.axis_size("mem")
    held, lons, var_count, lats = members.shape
    rows = state.shape[0]
    tiles = lats // 128
    core = lax.axis_index("space") % 2
    right = [(i, (i + 1) % blocks) for i in range(blocks)]
    left = [((i + 1) % blocks, i) for i in range(blocks)]
    swap = [(i, i ^ 1) for i in range(blocks)]
    tail = jnp.concatenate([state[-2:], cotangent[-2:]], axis=1)
    head = jnp.concatenate([state[:2], cotangent[:2]], axis=1)
    before = lax.ppermute(tail, "space", right)
    after = lax.ppermute(head, "space", left)
    front, back = weight_stacks(conv_in, conv_out, bias)

    wide = pltpu.VMEM((tiles, (rows + 4) * 8, 128), F32)
    tap = pltpu.VMEM(((rows + 4) * GROUP, lats), BF)
    fold = pltpu.VMEM((tiles, (rows + 2) * 8, 128), F32)
    big = pltpu.CompilerParams(vmem_limit_bytes=48 << 20)
    outgoing = pl.pallas_call(
        gradient_kernel,
        out_shape=jax.ShapeDtypeStruct((blocks, rows, lats), BF),
        scratch_shapes=[wide, tap, tap, fold],
        compiler_params=big,
        cost_estimate=pl.CostEstimate(flops=2_000_000_000, bytes_accessed=1_500_000, transcendentals=1_200_000),
        name="gradient",
    )(state, cotangent, before, after, front, back)
    members, outgoing = lax.optimization_barrier((members, outgoing))
    gathered = lax.all_to_all(outgoing, "space", 0, 0, tiled=True)
    whole = pl.BlockSpec((1, lons, var_count, 128), lambda i, j, c: (i, 0, 0, j))
    plane_spec = pl.BlockSpec((1, lons, 128), lambda i, j, c: (i, 0, j))
    kept, given = pl.pallas_call(
        planes_kernel,
        grid_spec=pltpu.PrefetchScalarGridSpec(
            num_scalar_prefetch=1,
            grid=(held, tiles),
            in_specs=[whole],
            out_specs=[plane_spec, plane_spec],
            scratch_shapes=[pltpu.VMEM((lons * 2, 128), F32)],
        ),
        out_shape=[jax.ShapeDtypeStruct((held, lons, lats), BF)] * 2,
        compiler_params=big,
        cost_estimate=pl.CostEstimate(flops=0, bytes_accessed=20_000_000, transcendentals=0),
        name="planes",
    )(core.reshape(1), members)
    taken = lax.ppermute(given, "space", swap)
    slopes = pl.pallas_call(
        slopes_kernel,
        out_shape=jax.ShapeDtypeStruct((rows + 2, conv_in.shape[2], lats), F32),
        scratch_shapes=[wide, tap],
        compiler_params=big,
        cost_estimate=pl.CostEstimate(flops=1_000_000_000, bytes_accessed=6_000_000, transcendentals=1_200_000),
        name="slopes",
    )(state, before, after, front)

    span = 192
    offsets = np.arange(lats)
    lat_loc = jnp.asarray(taps(np.abs(offsets[:, None] - offsets[None, :])))
    lon_loc = jnp.asarray(
        taps(np.abs(np.arange(span)[:, None] + HALF - np.arange(span + 2 * HALF)[None, :]))
    )
    one = pl.BlockSpec((1, lons, lats), lambda i: (i, 0, 0))
    fixed = lambda *shape: pl.BlockSpec(shape, lambda i: (0,) * len(shape))
    parts = pl.pallas_call(
        functools.partial(member_kernel, span),
        grid=(held,),
        in_specs=[one, one, fixed(lons, lats), fixed(lats, lats), fixed(span, span + 2 * HALF)],
        out_specs=fixed(blocks, rows + 4, lats),
        out_shape=jax.ShapeDtypeStruct((blocks, rows + 4, lats), BF),
        scratch_shapes=[
            pltpu.VMEM((lons, lats), F32),
            pltpu.VMEM((lons + 2 * HALF, lats), BF),
            pltpu.VMEM((lons + 16, lats), F32),
        ],
        compiler_params=big,
        cost_estimate=pl.CostEstimate(flops=4_000_000_000, bytes_accessed=6_000_000, transcendentals=0),
        name="members",
    )(kept, taken, gathered.reshape(lons, lats), lat_loc, lon_loc)
    arrived = lax.all_to_all(parts, "space", 0, 0, tiled=True)
    spread = pl.pallas_call(
        sum_kernel,
        out_shape=jax.ShapeDtypeStruct((groups, 2 * (rows + 4), lats), BF),
        compiler_params=big,
        name="block_sum",
    )(arrived)
    copies = lax.all_to_all(spread, "mem", 0, 0, tiled=True)
    member_count = held * blocks * groups
    field = jax.ShapeDtypeStruct(state.shape, F32)
    increment, response = pl.pallas_call(
        functools.partial(response_kernel, 1.0 / (member_count - 1.0)),
        out_shape=[field, field],
        scratch_shapes=[wide, tap, fold],
        compiler_params=big,
        name="response",
    )(copies, slopes, front, back)
    return (increment, response)


def solution(mesh):
    in_specs = (
        P(("space", "mem"), None, None, None),
        P("space", None, None),
        P("space", None, None),
        P(),
        P(),
        P(),
    )
    out_specs = (P("space", None, None), P("space", None, None))
    return jax.shard_map(
        per_device, mesh=mesh, in_specs=in_specs, out_specs=out_specs, check_vma=False
    )
```

profile of v0, /device:TPU:8, one launch (start us, length us, event | category | flops | bytes accessed | tf_op | source)
XLA Modules:
  0.0 121.4 jit_solution(6137676909291223823)
XLA Ops:
  0.6 0.8 fusion.3
  1.4 0.1 collective-permute-start
  1.5 1.8 %collective-permute-start.1 = (f32[2,4,384]{2,1,0:T(4,128)S(1)}, f32[2,4,384]{2,1,0:T(4,128)S(1)}, u32[]{:S(2)}, u32[]{:S(2)}) collective-permute-start(f32[2,4,384]{2,1,0:T(4,128)S(1)} %pad_maximum_fusion.4), channel_id=1, source_target_pairs={{8,0},{16,8},{24,16},{32,24},{40,32},{48,40},{56,48},{64,56},{72,6... | collective-permute-start | bytes 36872 | tf_op jit(solution)/shard_map/ppermute | solution.py:259
  3.3 0.7 reverse_bitcast_fusion
  4.0 0.7 stack.26
  4.7 0.7 pad_bitcast_fusion.1
  5.4 0.7 rev.6
  6.1 0.7 maximum_bitcast_fusion.1
  7.0 0.1 copy.21
  7.1 0.0 collective-permute-done.before_ref
  7.1 0.0 collective-permute-done.1.after_ref
  7.1 0.0 copy-start.2
  7.1 0.9 copy-done.2
  8.0 0.0 copy-start.4
  8.0 0.9 copy-done.4
  8.9 8.7 %gradient.1 = bf16[32,24,384]{2,1,0:T(8,128)(2,1)S(1)} custom-call(f32[24,2,384]{2,1,0:T(2,128)S(1)} %copy-done.2, f32[24,2,384]{2,1,0:T(2,128)S(1)} %copy-done.4, f32[2,4,384]{2,1,0:T(4,128)S(1)} %collective-permute-done.before_ref, f32[2,4,384]{2,1,0:T(4,128)S(1)} %collective-permute-done.1.after_ref, bf16[2,128,96]{2,1,0:T(8,128)(2,1)S(1)} %bitcast.26, ...), custom_call_target="tpu_custom_call" | custom-call | flops 2000000000 | bytes 1500000 | tf_op jit(solution)/shard_map/gradient/pallas_call | solution.py:266
  17.5 0.0 copy-start.5
  17.6 0.0 copy-start.6
  17.6 10.1 %planes.1 = (bf16[4,768,384]{2,1,0:T(8,128)(2,1)S(1)}, bf16[4,768,384]{2,1,0:T(8,128)(2,1)S(1)}) custom-call(s32[1]{0:T(128)} %bitcast.core_ref, bf16[4,768,2,384]{3,2,1,0:T(2,128)(2,1)} %members_ref), custom_call_target="tpu_custom_call" | custom-call | bytes 20000000 | tf_op jit(solution)/shard_map/planes/pallas_call | solution.py:278
  27.7 0.5 collective-permute-start.2
  28.2 29.8 %all_to_all.15 = bf16[32,24,384]{2,1,0:T(8,128)(2,1)S(1)} all-to-all(bf16[32,24,384]{2,1,0:T(8,128)(2,1)S(1)} %gradient.1), channel_id=1, replica_groups=mesh['space'=32,'mem'=8] {'space'}, dimensions={0} | all-to-all | bytes 1179648 | tf_op jit(solution)/shard_map/all_to_all | solution.py:275
  57.9 0.0 collective-permute-done.2.take_ref
  58.0 0.0 copy-start.7
  58.0 1.4 %copy-done.7 = bf16[4,768,384]{2,1,0:T(8,128)(2,1)} copy-done((bf16[4,768,384]{2,1,0:T(8,128)(2,1)}, bf16[4,768,384]{2,1,0:T(8,128)(2,1)S(1)}, u32[]{:S(2)}) %copy-start.7) | copy-done | bytes 2359320
  59.4 0.0 copy-done.5
  59.4 0.0 copy-done.6
  59.4 8.3 %members.1 = bf16[32,28,384]{2,1,0:T(8,128)(2,1)S(1)} custom-call(bf16[4,768,384]{2,1,0:T(8,128)(2,1)S(1)} %get-tuple-element.19.keep_ref, bf16[4,768,384]{2,1,0:T(8,128)(2,1)} %copy-done.7, bf16[768,384]{1,0:T(8,128)(2,1)S(1)} %bitcast.29, bf16[384,384]{1,0:T(8,128)(2,1)S(1)} %copy-done.5, bf16[192,224]{1,0:T(8,128)(2,1)S(1)} %copy-done.6), custom_call_target="tpu_custom_call" | custom-call | flops 4000000000 | bytes 6000000 | tf_op jit(solution)/shard_map/members/pallas_call | solution.py:310
  67.7 0.0 copy-start.3
  67.7 26.8 %all_to_all.16.parts_ref = bf16[32,28,384]{2,1,0:T(8,128)(2,1)S(1)} all-to-all(bf16[32,28,384]{2,1,0:T(8,128)(2,1)S(1)} %members.1), channel_id=1, replica_groups=mesh['space'=32,'mem'=8] {'space'}, dimensions={0} | all-to-all | bytes 1376256 | tf_op jit(solution)/shard_map/all_to_all | solution.py:325
  94.5 0.9 block_sum.1
  95.4 6.3 %all-to-all-start.2 = ((bf16[8,56,384]{2,1,0:T(8,128)(2,1)}), bf16[8,56,384]{2,1,0:T(8,128)(2,1)S(1)}, u32[]{:S(2)}, u32[]{:S(2)}) async-start(bf16[8,56,384]{2,1,0:T(8,128)(2,1)} %block_sum.1), calls=%async_computation.2 | async-start | bytes 688128 | tf_op jit(solution)/shard_map/all_to_all | solution.py:332
  101.7 0.0 copy-done.3
  101.7 2.9 %slopes.1.slopes_ref = f32[26,128,384]{2,1,0:T(8,128)S(1)} custom-call(f32[24,2,384]{2,1,0:T(2,128)S(1)} %copy-done.3, f32[2,4,384]{2,1,0:T(4,128)S(1)} %collective-permute-done.before_ref, f32[2,4,384]{2,1,0:T(4,128)S(1)} %collective-permute-done.1.after_ref, bf16[2,128,96]{2,1,0:T(8,128)(2,1)S(1)} %bitcast.27), custom_call_target="tpu_custom_call" | custom-call | flops 1000000000 | bytes 6000000 | tf_op jit(solution)/shard_map/slopes/pallas_call | solution.py:293
  104.6 0.0 copy-start
  104.6 2.2 %copy-done = f32[26,128,384]{2,1,0:T(8,128)} copy-done((f32[26,128,384]{2,1,0:T(8,128)}, f32[26,128,384]{2,1,0:T(8,128)S(1)}, u32[]{:S(2)}) %copy-start) | copy-done | bytes 5111832
  106.9 4.0 %all-to-all-done.2.copies_ref = bf16[8,56,384]{2,1,0:T(8,128)(2,1)S(1)} async-done(((bf16[8,56,384]{2,1,0:T(8,128)(2,1)}), bf16[8,56,384]{2,1,0:T(8,128)(2,1)S(1)}, u32[]{:S(2)}, u32[]{:S(2)}) %all-to-all-start.2) | async-done | bytes 344096 | tf_op jit(solution)/shard_map/all_to_all | solution.py:332
  110.9 0.0 copy-start.1
  110.9 2.4 %copy-done.1 = f32[26,128,384]{2,1,0:T(8,128)S(1)} copy-done((f32[26,128,384]{2,1,0:T(8,128)S(1)}, f32[26,128,384]{2,1,0:T(8,128)}, u32[]{:S(2)}) %copy-start.1) | copy-done | bytes 5111832
  113.4 8.1 %response.1 = (f32[24,2,384]{2,1,0:T(2,128)}, f32[24,2,384]{2,1,0:T(2,128)}) custom-call(bf16[8,56,384]{2,1,0:T(8,128)(2,1)S(1)} %all-to-all-done.2.copies_ref, f32[26,128,384]{2,1,0:T(8,128)S(1)} %copy-done.1, bf16[2,128,96]{2,1,0:T(8,128)(2,1)S(1)} %bitcast.28, bf16[2,48,256]{2,1,0:T(8,128)(2,1)S(1)} %pad_maximum_fusion.1.back_ref), custom_call_target="tpu_custom_call" | custom-call | tf_op jit(solution)/shard_map/response/pallas_call | solution.py:335
  (11 shorter events, 0.1 us)
Async XLA Ops:
  1.4 5.7 %collective-permute-start = (f32[2,4,384]{2,1,0:T(4,128)S(1)}, f32[2,4,384]{2,1,0:T(4,128)S(1)}, u32[]{:S(2)}, u32[]{:S(2)}) collective-permute-start(f32[2,4,384]{2,1,0:T(4,128)S(1)} %pad_maximum_fusion.3), channel_id=1, source_target_pairs={{0,8},{8,16},{16,24},{24,32},{32,40},{40,48},{48,56},{56,64},{64,7... | collective-permute-start | bytes 36872 | tf_op jit(solution)/shard_map/ppermute | solution.py:258
  1.5 5.6 %collective-permute-start.1 = (f32[2,4,384]{2,1,0:T(4,128)S(1)}, f32[2,4,384]{2,1,0:T(4,128)S(1)}, u32[]{:S(2)}, u32[]{:S(2)}) collective-permute-start(f32[2,4,384]{2,1,0:T(4,128)S(1)} %pad_maximum_fusion.4), channel_id=1, source_target_pairs={{8,0},{16,8},{24,16},{32,24},{40,32},{48,40},{56,48},{64,56},{72,6... | collective-permute-start | bytes 36872 | tf_op jit(solution)/shard_map/ppermute | solution.py:259
  7.1 0.9 copy-start.2
  8.0 0.9 copy-start.4
  17.5 41.8 %copy-start.5 = (bf16[384,384]{1,0:T(8,128)(2,1)S(1)}, bf16[384,384]{1,0:T(8,128)(2,1)}, u32[]{:S(2)}) copy-start(bf16[384,384]{1,0:T(8,128)(2,1)} %constant.59.clone.lat_ref) | copy-start | bytes 884740
  17.6 41.8 %copy-start.6 = (bf16[192,224]{1,0:T(8,128)(2,1)S(1)}, bf16[192,224]{1,0:T(8,128)(2,1)}, u32[]{:S(2)}) copy-start(bf16[192,224]{1,0:T(8,128)(2,1)} %constant.60.clone.lon_ref) | copy-start | bytes 258052
  27.7 30.3 %collective-permute-start.2 = (bf16[4,768,384]{2,1,0:T(8,128)(2,1)S(1)}, bf16[4,768,384]{2,1,0:T(8,128)(2,1)S(1)}, u32[]{:S(2)}, u32[]{:S(2)}) collective-permute-start(bf16[4,768,384]{2,1,0:T(8,128)(2,1)S(1)} %get-tuple-element.20), channel_id=1, source_target_pairs={{0,8},{8,0},{16,24},{24,16},{32,40},{40,32},{48,56},{56,48},{64,72... | collective-permute-start | bytes 7077896 | tf_op jit(solution)/shard_map/ppermute | solution.py:292
  58.0 1.4 %copy-start.7 = (bf16[4,768,384]{2,1,0:T(8,128)(2,1)}, bf16[4,768,384]{2,1,0:T(8,128)(2,1)S(1)}, u32[]{:S(2)}) copy-start(bf16[4,768,384]{2,1,0:T(8,128)(2,1)S(1)} %collective-permute-done.2.take_ref) | copy-start | bytes 7077892
  67.7 34.0 %copy-start.3 = (f32[24,2,384]{2,1,0:T(2,128)S(1)}, f32[24,2,384]{2,1,0:T(2,128)}, u32[]{:S(2)}) copy-start(f32[24,2,384]{2,1,0:T(2,128)} %state_ref.3) | copy-start | bytes 221188
  95.4 15.6 %all-to-all-start.2 = ((bf16[8,56,384]{2,1,0:T(8,128)(2,1)}), bf16[8,56,384]{2,1,0:T(8,128)(2,1)S(1)}, u32[]{:S(2)}, u32[]{:S(2)}) async-start(bf16[8,56,384]{2,1,0:T(8,128)(2,1)} %block_sum.1), calls=%async_computation.2 | async-start | bytes 688128 | tf_op jit(solution)/shard_map/all_to_all | solution.py:332
  104.6 2.3 %copy-start = (f32[26,128,384]{2,1,0:T(8,128)}, f32[26,128,384]{2,1,0:T(8,128)S(1)}, u32[]{:S(2)}) copy-start(f32[26,128,384]{2,1,0:T(8,128)S(1)} %slopes.1.slopes_ref) | copy-start | bytes 15335428
  110.9 2.4 %copy-start.1 = (f32[26,128,384]{2,1,0:T(8,128)S(1)}, f32[26,128,384]{2,1,0:T(8,128)}, u32[]{:S(2)}) copy-start(f32[26,128,384]{2,1,0:T(8,128)} %copy-done) | copy-start | bytes 15335428
where the time goes:
time: 122 us; the launch traced here: 121 us
  blocking collectives  56.6 us (46%)
  Pallas kernels  38.9 us (32%)
  local copies, waits for them, and re-layouts  11.6 us (10%)
  starting transfers between devices  8.69 us (7%)
  waiting for transfers between devices  4.03 us (3%)
    all_to_all x1, blocking collectives, per_device(): gathered = lax.all_to_all(outgoing, 'space', 0, 0, tiled=True)  29.8 us
    all_to_all x1, blocking collectives, per_device(): arrived = lax.all_to_all(parts, 'space', 0, 0, tiled=True)  26.8 us
    pallas_call x1, Pallas kernels, per_device(): pl.pallas_call(planes_kernel, grid_spec=pltpu.PrefetchScalarGridSpec(num_...  10.1 us
    pallas_call x1, Pallas kernels, per_device(): pl.pallas_call(gradient_kernel, out_shape=jax.ShapeDtypeStruct((blocks, r...  8.66 us
    pallas_call x1, Pallas kernels, per_device(): pl.pallas_call(functools.partial(member_kernel, span), grid=(held,), in_s...  8.32 us
    pallas_call x1, Pallas kernels, per_device(): pl.pallas_call(functools.partial(response_kernel, 1.0 / (member_count - 1...  8.07 us
    unnamed x17, local copies, waits for them, and re-layouts  7.93 us
    all_to_all x1, starting transfers between devices, per_device(): copies = lax.all_to_all(spread, 'mem', 0, 0, tiled=True)  6.32 us
  transfers between devices with their start and end apart: 4, of which 1 were waited for; matrix products, arithmetic and copies ran while one was open for 3% of the time, Pallas kernels for 2%

commit v1 on v0

v1 whole, which is shorter than its diff:
```python
import functools

import jax
import jax.numpy as jnp
import ml_dtypes
import numpy as np
from jax import lax
from jax.experimental import pallas as pl
from jax.experimental.pallas import tpu as pltpu
from jax.sharding import PartitionSpec as P

HALF = 16
GROUP = 32
UNROLL = 2
BF = jnp.bfloat16
F32 = jnp.float32


def taps(distance):
    ratio = distance.astype(np.float32) / np.float32(HALF + 1.0)
    value = np.float32(1.0) - ratio * ratio
    return np.where(distance <= HALF, value, np.float32(0.0)).astype(ml_dtypes.bfloat16)


def shifted(value, step):
    if step == 1:
        return value
    lats = value.shape[-1]
    lane = lax.broadcasted_iota(jnp.int32, value.shape, value.ndim - 1)
    if step == 0:
        return jnp.where(lane == 0, 0.0, pltpu.roll(value, 1, value.ndim - 1))
    return jnp.where(lane == lats - 1, 0.0, pltpu.roll(value, lats - 1, value.ndim - 1))


def split_high_low(value):
    high = value.astype(BF)
    low = (value - high.astype(F32)).astype(BF)
    return high, low


def stack_taps(wide_ref, tap_ref):
    for tile in range(wide_ref.shape[0]):
        value = wide_ref[tile]
        rows = value.shape[0] // 8
        high = value.astype(BF).astype(F32)
        low = value - high
        high = high.reshape(rows, 1, 8, 128)
        low = low.reshape(rows, 1, 8, 128)
        both = jnp.concatenate([high, low, high, low], axis=1).reshape(rows * GROUP, 128)
        tap_ref[:, tile * 128 : (tile + 1) * 128] = both.astype(BF)


def put_taps(wide_ref, plane, first_row, var):
    rows = plane.shape[0]
    for step in range(3):
        moved = shifted(plane, step)
        for tile in range(wide_ref.shape[0]):
            start = first_row * 8 + 2 * step + var
            wide_ref[tile, pl.ds(start, rows, stride=8), :] = moved[:, tile * 128 : (tile + 1) * 128]


def put_ones(wide_ref, value):
    rows = wide_ref.shape[1] // 8
    for tile in range(wide_ref.shape[0]):
        wide_ref[tile, pl.ds(6, rows, stride=8), :] = jnp.full((rows, 128), value, F32)
        wide_ref[tile, pl.ds(7, rows, stride=8), :] = jnp.zeros((rows, 128), F32)


def fold_hidden(hidden, back_weight, product_ref, row):
    high, low = split_high_low(hidden)
    product = jnp.dot(
        back_weight, jnp.concatenate([high, low], axis=0), preferred_element_type=F32
    )
    product = product[:24] + product[24:]
    for step in range(3):
        product_ref[step, pl.ds(pl.multiple_of(row * 8, 8), 8), :] = product[8 * step : 8 * step + 8]


def fold_lats(product_ref, fold_ref, first, count):
    window = pl.ds(first * 8, count * 8)
    total = (
        product_ref[1, window, :]
        + shifted(product_ref[0, window, :], 0)
        + shifted(product_ref[2, window, :], 2)
    )
    for tile in range(fold_ref.shape[0]):
        fold_ref[tile, window, :] = total[:, tile * 128 : (tile + 1) * 128]


def folded(fold_ref, rows, var):
    tiles = []
    for tile in range(fold_ref.shape[0]):
        tiles.append(
            sum(
                fold_ref[tile, pl.ds(10 * step + var, rows, stride=8), :] for step in range(3)
            )
        )
    return jnp.concatenate(tiles, axis=1)


def fill_edges(before_ref, after_ref, var_from, wide_ref):
    for var in range(2):
        line = var_from + var
        for row in range(2):
            put_taps(wide_ref, before_ref[row, line : line + 1, :], row, var)
            put_taps(wide_ref, after_ref[row, line : line + 1, :], 2 + row, var)


def tap_window(row):
    return pl.ds(pl.multiple_of(row * GROUP, GROUP), 3 * GROUP)


def bands(tap_ref, edge_ref, frame_ref):
    half = 2 * GROUP
    last = tap_ref.shape[0] - half
    frame_ref[0:half, :] = edge_ref[0:half, :]
    frame_ref[half : 2 * half, :] = tap_ref[0:half, :]
    frame_ref[2 * half : 3 * half, :] = tap_ref[last : last + half, :]
    frame_ref[3 * half : 4 * half, :] = edge_ref[half : 2 * half, :]


def front_stack(rows_ref):
    value = rows_ref[...]
    high = value.astype(BF).astype(F32)
    low = value - high
    high = high.reshape(3, 1, 8, 128)
    low = low.reshape(3, 1, 8, 128)
    both = jnp.concatenate([high, high, low, low], axis=1).reshape(3 * GROUP, 128)
    return jnp.transpose(both).astype(BF)


def back_stack(rows_ref):
    value = rows_ref[...]
    high = value.astype(BF).astype(F32)
    both = jnp.concatenate([high, value - high], axis=0)
    return jnp.concatenate([both, both], axis=1).astype(BF)


def fetch(pairs, semaphores):
    copies = [
        pltpu.make_async_copy(source, target, semaphores.at[index])
        for index, (source, target) in enumerate(pairs)
    ]
    for copy in copies:
        copy.start()
    return copies


def prepare_kernel(
    state_far,
    cot_far,
    first_far,
    second_far,
    bias_far,
    front_ref,
    back_ref,
    state_taps,
    cot_taps,
    fold,
    cot_planes,
    wide,
    lines,
    product,
    state_ref,
    cot_ref,
    first_ref,
    second_ref,
    bias_ref,
    semaphores,
):
    rows = state_ref.shape[0]
    near = (first_ref, second_ref, bias_ref, state_ref, cot_ref)
    far = (first_far, second_far, bias_far, state_far, cot_far)
    copies = fetch(zip(far, near), semaphores)
    for copy in copies[:3]:
        copy.wait()
    for which in range(2):
        lines[...] = jnp.zeros_like(lines)
        for lon in range(3):
            for lat in range(3):
                start = 8 * lon + 2 * lat
                if which == 0:
                    lines[start : start + 2, :] = first_ref[lon, lat]
                else:
                    lines[start : start + 2, :] = second_ref[2 - lon, 2 - lat]
        if which == 0:
            lines[14:15, :] = bias_ref[...]
        front_ref[which] = front_stack(lines)
        lines[...] = jnp.zeros_like(lines)
        for lon in range(3):
            for lat in range(3):
                start = 8 * lat + 2 * lon
                if which == 0:
                    lines[start : start + 2, :] = first_ref[2 - lon, 2 - lat]
                else:
                    lines[start : start + 2, :] = second_ref[lon, lat]
        back_ref[which] = back_stack(lines)

    put_ones(wide, 1.0)
    for copy in copies[3:]:
        copy.wait()
    for main_ref, tap_ref in ((state_ref, state_taps), (cot_ref, cot_taps)):
        for var in range(2):
            plane = main_ref[:, var, :]
            if main_ref is cot_ref:
                cot_planes[var] = plane
            put_taps(wide, plane, 0, var)
        stack_taps(wide, tap_ref)

    def step(row, carry):
        activity = jnp.tanh(
            jnp.dot(front_ref[0], state_taps[tap_window(row), :], preferred_element_type=F32)
        )
        slopes = 1.0 - activity * activity
        hidden = slopes * jnp.dot(
            front_ref[1], cot_taps[tap_window(row), :], preferred_element_type=F32
        )
        fold_hidden(hidden, back_ref[0], product, row + 2)
        return carry

    lax.fori_loop(0, rows - 2, step, 0, unroll=UNROLL)
    fold_lats(product, fold, 2, rows - 2)


def gradient_kernel(
    cot_planes,
    before_ref,
    after_ref,
    front_ref,
    back_ref,
    state_taps,
    cot_taps,
    fold_ref,
    out_ref,
    wide,
    edge,
    state_frame,
    cot_frame,
    product,
    fold,
):
    rows = cot_planes.shape[1]
    put_ones(wide, 1.0)
    for var_from, tap_ref, frame_ref in ((0, state_taps, state_frame), (2, cot_taps, cot_frame)):
        fill_edges(before_ref, after_ref, var_from, wide)
        stack_taps(wide, edge)
        bands(tap_ref, edge, frame_ref)
    fold[...] = fold_ref[...]
    for start, row in ((0, 0), (1, 1), (4, rows), (5, rows + 1)):
        window = pl.ds(start * GROUP, 3 * GROUP)
        activity = jnp.tanh(
            jnp.dot(front_ref[0], state_frame[window, :], preferred_element_type=F32)
        )
        slopes = 1.0 - activity * activity
        hidden = slopes * jnp.dot(
            front_ref[1], cot_frame[window, :], preferred_element_type=F32
        )
        fold_hidden(hidden, back_ref[0], product, row)
    fold_lats(product, fold, 0, 2)
    fold_lats(product, fold, rows, 2)
    for var in range(2):
        plane = (cot_planes[var] + folded(fold, rows, var)).astype(BF)
        for pair in range(out_ref.shape[0] // 2):
            out_ref[2 * pair + var] = plane


def slopes_kernel(
    before_ref, after_ref, front_ref, state_taps, out_ref, wide, edge, frame
):
    rows = out_ref.shape[0] - 2
    put_ones(wide, 1.0)
    fill_edges(before_ref, after_ref, 0, wide)
    stack_taps(wide, edge)
    bands(state_taps, edge, frame)

    def slopes(window):
        activity = jnp.tanh(jnp.dot(front_ref[0], window, preferred_element_type=F32))
        return 1.0 - activity * activity

    for start, row in ((0, 0), (1, 1), (4, rows), (5, rows + 1)):
        out_ref[row] = slopes(frame[pl.ds(start * GROUP, 3 * GROUP), :])

    def step(row, carry):
        out_ref[row + 2] = slopes(state_taps[tap_window(row), :])
        return carry

    lax.fori_loop(0, rows - 2, step, 0, unroll=2)


def response_kernel(
    scale,
    copies_ref,
    slopes_far,
    front_ref,
    back_ref,
    incr_out,
    resp_out,
    wide,
    incr_taps,
    product,
    fold,
    slopes_ref,
    semaphores,
):
    rows = incr_out.shape[0]
    half = (rows + 2) // 2
    halves = [pl.ds(0, half), pl.ds(half, half)]
    copies = fetch([(slopes_far.at[part], slopes_ref.at[part]) for part in halves], semaphores)
    planes = []
    put_ones(wide, 0.0)
    for var in range(2):
        window = pl.ds(var * (rows + 4), rows + 4)
        plane = copies_ref[0, window, :].astype(F32)
        for group in range(1, copies_ref.shape[0]):
            plane = plane + copies_ref[group, window, :].astype(F32)
        plane = plane * scale
        planes.append(plane)
        put_taps(wide, plane, 0, var)
    stack_taps(wide, incr_taps)

    def step(row, carry):
        hidden = slopes_ref[row] * jnp.dot(
            front_ref[0], incr_taps[tap_window(row), :], preferred_element_type=F32
        )
        fold_hidden(hidden, back_ref[1], product, row)
        return carry

    copies[0].wait()
    lax.fori_loop(0, half, step, 0, unroll=UNROLL)
    copies[1].wait()
    lax.fori_loop(half, rows + 2, step, 0, unroll=UNROLL)
    fold_lats(product, fold, 0, rows + 2)
    for var in range(2):
        increment = planes[var][2 : 2 + rows]
        incr_out[:, var, :] = increment
        resp_out[:, var, :] = increment + folded(fold, rows, var)


def planes_kernel(core_ref, members_ref, keep_ref, give_ref, lines):
    core = core_ref[0]
    rows = members_ref.shape[1]
    lines[...] = members_ref.reshape(rows * 2, 128)[...].astype(F32)
    keep_ref[...] = lines[pl.ds(core, rows, stride=2), :].astype(BF)
    give_ref[...] = lines[pl.ds(1 - core, rows, stride=2), :].astype(BF)


def member_kernel(span, *refs):
    *far_refs, field_ref, lat_ref, lon_ref, out_ref, field, banded, total, held, semaphores = refs
    lons = field_ref.shape[0]
    member_refs = [held.at[index] for index in range(len(far_refs))]
    copies = fetch(zip(far_refs, member_refs), semaphores)
    blocks = out_ref.shape[0]
    rows = lons // blocks
    field[...] = field_ref[...].astype(F32)
    for index, member_ref in enumerate(member_refs):
        copies[index].wait()
        for start in range(0, lons, span):
            window = pl.ds(start, span)
            product = (member_ref[window, :].astype(F32) * field[window, :]).astype(BF)
            banded[pl.ds(HALF + start, span), :] = jnp.dot(
                product, lat_ref[...], preferred_element_type=F32
            ).astype(BF)
        banded[pl.ds(0, HALF), :] = banded[pl.ds(lons, HALF), :]
        banded[pl.ds(HALF + lons, HALF), :] = banded[pl.ds(HALF, HALF), :]
        for start in range(0, lons, span):
            spread = jnp.dot(
                lon_ref[...], banded[pl.ds(start, span + 2 * HALF), :], preferred_element_type=F32
            )
            window = pl.ds(8 + start, span)
            value = member_ref[pl.ds(start, span), :].astype(F32) * spread
            total[window, :] = value if index == 0 else total[window, :] + value
    total[pl.ds(0, 8), :] = total[pl.ds(lons, 8), :]
    total[pl.ds(lons + 8, 8), :] = total[pl.ds(8, 8), :]
    for block in range(blocks):
        out_ref[block] = total[pl.ds(6 + block * rows, rows + 4), :].astype(BF)


def sum_kernel(parts_ref, out_ref):
    for var in range(2):
        plane = parts_ref[var].astype(F32)
        for pair in range(1, parts_ref.shape[0] // 2):
            plane = plane + parts_ref[2 * pair + var].astype(F32)
        plane = plane.astype(BF)
        for group in range(out_ref.shape[0]):
            out_ref[group, pl.ds(var * plane.shape[0], plane.shape[0]), :] = plane


def per_device(members, state, cotangent, conv_in, conv_out, bias):
    blocks = lax.axis_size("space")
    groups = lax.axis_size("mem")
    held, lons, var_count, lats = members.shape
    rows = state.shape[0]
    tiles = lats // 128
    core = lax.axis_index("space") % 2
    small = pltpu.CompilerParams(vmem_limit_bytes=24 << 20)
    right = [(i, (i + 1) % blocks) for i in range(blocks)]
    left = [((i + 1) % blocks, i) for i in range(blocks)]
    swap = [(i, i ^ 1) for i in range(blocks)]
    tail = jnp.concatenate([state[-2:], cotangent[-2:]], axis=1)
    head = jnp.concatenate([state[:2], cotangent[:2]], axis=1)
    before = lax.ppermute(tail, "space", right)
    after = lax.ppermute(head, "space", left)
    hidden = conv_in.shape[2]
    shape = jax.ShapeDtypeStruct
    padded = lambda count: pltpu.VMEM((tiles, count * 8, 128), F32)
    tap = lambda count: pltpu.VMEM((count * GROUP, lats), BF)
    product = pltpu.VMEM((3, (rows + 2) * 8, lats), F32)
    first = jnp.transpose(conv_in, (0, 1, 3, 2))
    far = pl.BlockSpec(memory_space=pltpu.HBM)
    near = pl.BlockSpec(memory_space=pltpu.VMEM)
    remote = lambda value: pltpu.with_memory_space_constraint(value, pltpu.HBM)
    front, back, state_taps, cot_taps, partial, cot_planes = pl.pallas_call(
        prepare_kernel,
        out_shape=[
            shape((2, hidden, 3 * GROUP), BF),
            shape((2, 48, 2 * hidden), BF),
            shape((rows * GROUP, lats), BF),
            shape((rows * GROUP, lats), BF),
            shape((tiles, (rows + 2) * 8, 128), F32),
            shape((var_count, rows, lats), F32),
        ],
        in_specs=[far] * 5,
        scratch_shapes=[
            padded(rows),
            pltpu.VMEM((24, hidden), F32),
            product,
            pltpu.VMEM(state.shape, F32),
            pltpu.VMEM(state.shape, F32),
            pltpu.VMEM(first.shape, F32),
            pltpu.VMEM(conv_out.shape, F32),
            pltpu.VMEM((1, hidden), F32),
            pltpu.SemaphoreType.DMA((5,)),
        ],
        compiler_params=small,
        cost_estimate=pl.CostEstimate(flops=2_000_000_000, bytes_accessed=3_000_000, transcendentals=1_100_000),
        name="prepare",
    )(*[remote(value) for value in (state, cotangent, first, conv_out, bias.reshape(1, hidden))])
    outgoing = pl.pallas_call(
        gradient_kernel,
        out_shape=shape((blocks, rows, lats), BF),
        scratch_shapes=[
            padded(4), tap(4), tap(8), tap(8), product, padded(rows + 2)
        ],
        compiler_params=small,
        cost_estimate=pl.CostEstimate(flops=400_000_000, bytes_accessed=1_500_000, transcendentals=200_000),
        name="gradient",
    )(cot_planes, before, after, front, back, state_taps, cot_taps, partial)
    members, outgoing = lax.optimization_barrier((members, outgoing))
    gathered = lax.all_to_all(outgoing, "space", 0, 0, tiled=True)
    kept, taken = [], []
    members = remote(members)
    for member in range(held):
        keep, give = pl.pallas_call(
            planes_kernel,
            grid_spec=pltpu.PrefetchScalarGridSpec(
                num_scalar_prefetch=1,
                grid=(tiles,),
                in_specs=[
                    pl.BlockSpec((1, lons, var_count, 128), lambda j, c, member=member: (member, 0, 0, j))
                ],
                out_specs=[pl.BlockSpec((lons, 128), lambda j, c: (0, j))] * 2,
                scratch_shapes=[pltpu.VMEM((lons * 2, 128), F32)],
            ),
            out_shape=[pltpu.HBM((lons, lats), BF)] * 2,
            compiler_params=small,
            cost_estimate=pl.CostEstimate(flops=0, bytes_accessed=10_000_000, transcendentals=0),
            name="planes",
        )(core.reshape(1), members)
        kept.append(keep)
        taken.append(lax.ppermute(give, "space", swap))
    slopes = pl.pallas_call(
        slopes_kernel,
        out_shape=pltpu.HBM((rows + 2, hidden, lats), F32),
        out_specs=near,
        scratch_shapes=[padded(4), tap(4), tap(8)],
        compiler_params=small,
        cost_estimate=pl.CostEstimate(flops=1_000_000_000, bytes_accessed=6_000_000, transcendentals=1_200_000),
        name="slopes",
    )(before, after, front, state_taps)

    span = 192
    offsets = np.arange(lats)
    lat_loc = jnp.asarray(taps(np.abs(offsets[:, None] - offsets[None, :])))
    lon_loc = jnp.asarray(
        taps(np.abs(np.arange(span)[:, None] + HALF - np.arange(span + 2 * HALF)[None, :]))
    )
    parts = pl.pallas_call(
        functools.partial(member_kernel, span),
        in_specs=[far] * (2 * held) + [near] * 3,
        out_shape=jax.ShapeDtypeStruct((blocks, rows + 4, lats), BF),
        scratch_shapes=[
            pltpu.VMEM((lons, lats), F32),
            pltpu.VMEM((lons + 2 * HALF, lats), BF),
            pltpu.VMEM((lons + 16, lats), F32),
            pltpu.VMEM((2 * held, lons, lats), BF),
            pltpu.SemaphoreType.DMA((2 * held,)),
        ],
        compiler_params=small,
        cost_estimate=pl.CostEstimate(flops=4_000_000_000, bytes_accessed=6_000_000, transcendentals=0),
        name="members",
    )(*[remote(value) for value in kept + taken], gathered.reshape(lons, lats), lat_loc, lon_loc)
    arrived = lax.all_to_all(parts, "space", 0, 0, tiled=True)
    spread = pl.pallas_call(
        sum_kernel,
        out_shape=jax.ShapeDtypeStruct((groups, 2 * (rows + 4), lats), BF),
        compiler_params=small,
        name="block_sum",
    )(arrived)
    copies = lax.all_to_all(spread, "mem", 0, 0, tiled=True)
    member_count = held * blocks * groups
    field = jax.ShapeDtypeStruct(state.shape, F32)
    increment, response = pl.pallas_call(
        functools.partial(response_kernel, 1.0 / (member_count - 1.0)),
        out_shape=[field, field],
        in_specs=[near, far, near, near],
        scratch_shapes=[
            padded(rows + 4),
            tap(rows + 4),
            product,
            padded(rows + 2),
            pltpu.VMEM((rows + 2, hidden, lats), F32),
            pltpu.SemaphoreType.DMA((2,)),
        ],
        compiler_params=small,
        name="response",
    )(copies, remote(slopes), front, back)
    return (increment, response)


def solution(mesh):
    in_specs = (
        P(("space", "mem"), None, None, None),
        P("space", None, None),
        P("space", None, None),
        P(),
        P(),
        P(),
    )
    out_specs = (P("space", None, None), P("space", None, None))
    return jax.shard_map(
        per_device, mesh=mesh, in_specs=in_specs, out_specs=out_specs, check_vma=False
    )
```

time: 122 us -> 112 us (0.918)
  blocking collectives: 56.6 us -> 31.4 us
  starting transfers between devices: 8.69 us -> 20.4 us
  local copies, waits for them, and re-layouts: 11.6 us -> 1.5 us
  Pallas kernels: 38.9 us -> 48.5 us
  waiting for transfers between devices: 4.03 us -> 8.21 us
    all_to_all x1 -> x0, blocking collectives: 29.8 us -> none  [per_device(): gathered = lax.all_to_all(outgoing, 'space', 0, 0, tiled=True)]
    all_to_all x0 -> x1, starting transfers between devices: none -> 11.2 us  [per_device(): gathered = lax.all_to_all(outgoing, 'space', 0, 0, tiled=True)]
    unnamed x17 -> x14, local copies, waits for them, and re-layouts: 7.93 us -> 0.75 us
    pallas_call x1 -> x4, Pallas kernels: 10.1 us -> 15.8 us  [per_device(): pl.pallas_call(planes_kernel, grid_spec=pltpu.PrefetchScalarGridSpec(num_...]
    all_to_all x1, blocking collectives: 26.8 us -> 31.4 us  [per_device(): arrived = lax.all_to_all(parts, 'space', 0, 0, tiled=True)]
    ppermute x1 -> x4, waiting for transfers between devices: 0.01 us -> 3.84 us  [per_device(): taken.append(lax.ppermute(give, 'space', swap))]
    pallas_call x3 -> x4, Pallas kernels: 19.9 us -> 23.2 us  [the longest x1 8.6 us: per_device(): pl.pallas_call(functools.partial(member_kernel, span), in_specs=[far] * (...]
    another operation x3 -> x0, local copies, waits for them, and re-layouts: 1.42 us -> none  [the longest x2 0.72 us: weight_stacks(): front = jnp.stack([first, conv_out[::-1, ::-1]]).reshape(2, 3, 6, hidden)]
  transfers between devices with their start and end apart: 4 -> 8, of which waited for: 1 -> 5; matrix products, arithmetic and copies ran while one was open for 3% -> 0% of each run, Pallas kernels for 2% -> 25%
where the time goes in v1:
time: 112 us; the launch traced here: 111 us
  Pallas kernels  48.5 us (43%)
  blocking collectives  31.4 us (28%)
  starting transfers between devices  20.4 us (18%)
  waiting for transfers between devices  8.21 us (7%)
  local copies, waits for them, and re-layouts  1.5 us (1%)
    all_to_all x1, blocking collectives, per_device(): arrived = lax.all_to_all(parts, 'space', 0, 0, tiled=True)  31.4 us
    pallas_call x4, Pallas kernels, per_device(): pl.pallas_call(planes_kernel, grid_spec=pltpu.PrefetchScalarGridSpec(num_...  15.8 us
    all_to_all x1, starting transfers between devices, per_device(): gathered = lax.all_to_all(outgoing, 'space', 0, 0, tiled=True)  11.2 us
    pallas_call x1, Pallas kernels, per_device(): pl.pallas_call(functools.partial(response_kernel, 1.0 / (member_count - 1...  8.74 us
    pallas_call x1, Pallas kernels, per_device(): pl.pallas_call(functools.partial(member_kernel, span), in_specs=[far] * (...  8.6 us
    pallas_call x1, Pallas kernels, per_device(): pl.pallas_call(prepare_kernel, out_shape=[shape((2, hidden, 3 * GROUP), B...  7.67 us
    all_to_all x1, starting transfers between devices, per_device(): copies = lax.all_to_all(spread, 'mem', 0, 0, tiled=True)  6.32 us
    pallas_call x1, Pallas kernels, per_device(): pl.pallas_call(slopes_kernel, out_shape=pltpu.HBM((rows + 2, hidden, lats...  4.87 us
  transfers between devices with their start and end apart: 8, of which 5 were waited for; matrix products, arithmetic and copies ran while one was open for 0% of the time, Pallas kernels for 25%

profile of v1, /device:TPU:8, one launch (start us, length us, event | category | flops | bytes accessed | tf_op | source)
XLA Modules:
  0.0 111.0 jit_solution(16632486579121748118)
XLA Ops:
  0.6 0.8 fusion
  1.4 0.1 collective-permute-start
  1.5 1.8 %collective-permute-start.1 = (f32[2,4,384]{2,1,0:T(4,128)S(1)}, f32[2,4,384]{2,1,0:T(4,128)S(1)}, u32[]{:S(2)}, u32[]{:S(2)}) collective-permute-start(f32[2,4,384]{2,1,0:T(4,128)S(1)} %pad_maximum_fusion.1), channel_id=1, source_target_pairs={{8,0},{16,8},{24,16},{32,24},{40,32},{48,40},{56,48},{64,56},{72,6... | collective-permute-start | bytes 36872 | tf_op jit(solution)/shard_map/ppermute | solution.py:402
  3.3 7.7 %prepare.1 = (bf16[2,128,96]{2,1,0:T(8,128)(2,1)S(1)}, bf16[2,48,256]{2,1,0:T(8,128)(2,1)S(1)}, bf16[768,384]{1,0:T(8,128)(2,1)S(1)}, bf16[768,384]{1,0:T(8,128)...) custom-call(f32[24,2,384]{2,1,0:T(2,128)} %state_far.1, f32[24,2,384]{2,1,0:T(2,128)} %cot_far.1, ...), custom_call_target="tpu_custom_call" | custom-call | flops 2000000000 | bytes 3000000 | tf_op jit(solution)/shard_map/prepare/pallas_call | solution.py:412
  11.0 0.0 collective-permute-done.before_ref
  11.0 0.0 collective-permute-done.1.after_ref
  11.0 2.0 %gradient.1 = bf16[32,24,384]{2,1,0:T(8,128)(2,1)} custom-call(f32[2,24,384]{2,1,0:T(8,128)S(1)} %get-tuple-element.18.cot_planes, f32[2,4,384]{2,1,0:T(4,128)S(1)} %collective-permute-done.before_ref, f32[2,4,384]{2,1,0:T(4,128)S(1)} %collective-permute-done.1.after_ref, bf16[2,128,96]{2,1,0:T(8,128)(2,1)S(1)} %get-tuple-element.19.front_ref, ...), custom_call_target="tpu_custom_call" | custom-call | flops 400000000 | bytes 1500000 | tf_op jit(solution)/shard_map/gradient/pallas_call | solution.py:438
  13.0 11.2 %all-to-all-start = ((bf16[32,24,384]{2,1,0:T(8,128)(2,1)}), bf16[32,24,384]{2,1,0:T(8,128)(2,1)S(1)}, u32[]{:S(2)}, u32[]{:S(2)}) async-start(bf16[32,24,384]{2,1,0:T(8,128)(2,1)} %gradient.1), calls=%async_computation | async-start | bytes 1179648 | tf_op jit(solution)/shard_map/all_to_all | solution.py:449
  24.2 3.9 %planes.7 = (bf16[768,384]{1,0:T(8,128)(2,1)}, bf16[768,384]{1,0:T(8,128)(2,1)}) custom-call(s32[1]{0:T(128)} %bitcast.core_ref, bf16[4,768,2,384]{3,2,1,0:T(2,128)(2,1)} %members_ref.3), custom_call_target="tpu_custom_call" | custom-call | bytes 10000000 | tf_op jit(solution)/shard_map/planes/pallas_call | solution.py:453
  28.1 3.9 %planes.6 = (bf16[768,384]{1,0:T(8,128)(2,1)}, bf16[768,384]{1,0:T(8,128)(2,1)}) custom-call(s32[1]{0:T(128)} %bitcast.core_ref, bf16[4,768,2,384]{3,2,1,0:T(2,128)(2,1)} %members_ref.3), custom_call_target="tpu_custom_call" | custom-call | bytes 10000000 | tf_op jit(solution)/shard_map/planes/pallas_call | solution.py:453
  32.0 0.0 copy-start.6
  32.0 0.0 copy-start.5
  32.0 0.0 copy-start
  32.0 0.0 copy-start.1
  32.0 4.0 %planes.5 = (bf16[768,384]{1,0:T(8,128)(2,1)}, bf16[768,384]{1,0:T(8,128)(2,1)}) custom-call(s32[1]{0:T(128)} %bitcast.core_ref, bf16[4,768,2,384]{3,2,1,0:T(2,128)(2,1)} %members_ref.3), custom_call_target="tpu_custom_call" | custom-call | bytes 10000000 | tf_op jit(solution)/shard_map/planes/pallas_call | solution.py:453
  36.1 3.9 %planes.4 = (bf16[768,384]{1,0:T(8,128)(2,1)}, bf16[768,384]{1,0:T(8,128)(2,1)}) custom-call(s32[1]{0:T(128)} %bitcast.core_ref, bf16[4,768,2,384]{3,2,1,0:T(2,128)(2,1)} %members_ref.3), custom_call_target="tpu_custom_call" | custom-call | bytes 10000000 | tf_op jit(solution)/shard_map/planes/pallas_call | solution.py:453
  40.0 0.0 copy-done.6
  40.0 0.1 collective-permute-start.5
  40.2 0.0 copy-done.5
  40.2 0.4 collective-permute-start.4
  40.5 0.1 collective-permute-start.3
  40.7 0.4 collective-permute-start.2
  41.0 1.0 collective-permute-done.5.refs_7_
  42.0 0.0 copy-start.2
  42.0 2.5 %collective-permute-done.4.refs_6_ = bf16[768,384]{1,0:T(8,128)(2,1)S(1)} collective-permute-done((bf16[768,384]{1,0:T(8,128)(2,1)S(1)}, bf16[768,384]{1,0:T(8,128)(2,1)S(1)}, u32[]{:S(2)}, u32[]{:S(2)}) %collective-permute-start.4) | collective-permute-done | bytes 589856 | tf_op jit(solution)/shard_map/ppermute | solution.py:470
  44.5 0.0 copy-start.3
  44.5 0.2 collective-permute-done.3.refs_5_
  44.7 0.0 copy-start.4
  44.8 0.1 collective-permute-done.2.refs_4_
  44.9 0.0 all-to-all-done
  44.9 0.0 copy-done.2
  44.9 0.5 copy-done.3
  45.4 0.3 copy-done.4
  45.6 0.0 copy-done
  45.6 0.0 copy-done.1
  45.6 8.6 %members.1 = bf16[32,28,384]{2,1,0:T(8,128)(2,1)S(1)} custom-call(bf16[768,384]{1,0:T(8,128)(2,1)} %get-tuple-element.25.refs_0_, bf16[768,384]{1,0:T(8,128)(2,1)} %get-tuple-element.26.refs_1_, bf16[768,384]{1,0:T(8,128)(2,1)} %get-tuple-element.27.refs_2_, bf16[768,384]{1,0:T(8,128)(2,1)} %get-tuple-element.28.refs_3_, ...), custom_call_target="tpu_custom_call" | custom-call | flops 4000000000 | bytes 6000000 | tf_op jit(solution)/shard_map/members/pallas_call | solution.py:487
  54.2 31.4 %all_to_all.15.parts_ref = bf16[32,28,384]{2,1,0:T(8,128)(2,1)S(1)} all-to-all(bf16[32,28,384]{2,1,0:T(8,128)(2,1)S(1)} %members.1), channel_id=1, replica_groups=mesh['space'=32,'mem'=8] {'space'}, dimensions={0} | all-to-all | bytes 1376256 | tf_op jit(solution)/shard_map/all_to_all | solution.py:502
  85.7 0.9 block_sum.1
  86.5 6.3 %all-to-all-start.2 = ((bf16[8,56,384]{2,1,0:T(8,128)(2,1)}), bf16[8,56,384]{2,1,0:T(8,128)(2,1)S(1)}, u32[]{:S(2)}, u32[]{:S(2)}) async-start(bf16[8,56,384]{2,1,0:T(8,128)(2,1)} %block_sum.1), calls=%async_computation.2 | async-start | bytes 688128 | tf_op jit(solution)/shard_map/all_to_all | solution.py:509
  92.9 4.9 %slopes.1.slopes_far = f32[26,128,384]{2,1,0:T(8,128)} custom-call(f32[2,4,384]{2,1,0:T(4,128)S(1)} %collective-permute-done.before_ref, f32[2,4,384]{2,1,0:T(4,128)S(1)} %collective-permute-done.1.after_ref, bf16[2,128,96]{2,1,0:T(8,128)(2,1)S(1)} %get-tuple-element.19.front_ref, bf16[768,384]{1,0:T(8,128)(2,1)S(1)} %get-tuple-element.21.state_taps), custom_call_target="tpu_custom_call" | custom-call | flops 1000000000 | bytes 6000000 | tf_op jit(solution)/shard_map/slopes/pallas_call | solution.py:471
  97.7 4.4 %all-to-all-done.2.copies_ref = bf16[8,56,384]{2,1,0:T(8,128)(2,1)S(1)} async-done(((bf16[8,56,384]{2,1,0:T(8,128)(2,1)}), bf16[8,56,384]{2,1,0:T(8,128)(2,1)S(1)}, u32[]{:S(2)}, u32[]{:S(2)}) %all-to-all-start.2) | async-done | bytes 344096 | tf_op jit(solution)/shard_map/all_to_all | solution.py:509
  102.1 8.7 %response.1 = (f32[24,2,384]{2,1,0:T(2,128)}, f32[24,2,384]{2,1,0:T(2,128)}) custom-call(bf16[8,56,384]{2,1,0:T(8,128)(2,1)S(1)} %all-to-all-done.2.copies_ref, f32[26,128,384]{2,1,0:T(8,128)} %slopes.1.slopes_far, bf16[2,128,96]{2,1,0:T(8,128)(2,1)S(1)} %get-tuple-element.19.front_ref, bf16[2,48,256]{2,1,0:T(8,128)(2,1)S(1)} %get-tuple-element.20.back_ref), custom_call_target="tpu_custom_call" | custom-call | tf_op jit(solution)/shard_map/response/pallas_call | solution.py:512
  (2 shorter events, 0.0 us)
Async XLA Ops:
  1.4 9.6 %collective-permute-start = (f32[2,4,384]{2,1,0:T(4,128)S(1)}, f32[2,4,384]{2,1,0:T(4,128)S(1)}, u32[]{:S(2)}, u32[]{:S(2)}) collective-permute-start(f32[2,4,384]{2,1,0:T(4,128)S(1)} %pad_maximum_fusion), channel_id=1, source_target_pairs={{0,8},{8,16},{16,24},{24,32},{32,40},{40,48},{48,56},{56,64},{64,7... | collective-permute-start | bytes 36872 | tf_op jit(solution)/shard_map/ppermute | solution.py:401
  1.5 9.5 %collective-permute-start.1 = (f32[2,4,384]{2,1,0:T(4,128)S(1)}, f32[2,4,384]{2,1,0:T(4,128)S(1)}, u32[]{:S(2)}, u32[]{:S(2)}) collective-permute-start(f32[2,4,384]{2,1,0:T(4,128)S(1)} %pad_maximum_fusion.1), channel_id=1, source_target_pairs={{8,0},{16,8},{24,16},{32,24},{40,32},{48,40},{56,48},{64,56},{72,6... | collective-permute-start | bytes 36872 | tf_op jit(solution)/shard_map/ppermute | solution.py:402
  13.0 31.9 %all-to-all-start = ((bf16[32,24,384]{2,1,0:T(8,128)(2,1)}), bf16[32,24,384]{2,1,0:T(8,128)(2,1)S(1)}, u32[]{:S(2)}, u32[]{:S(2)}) async-start(bf16[32,24,384]{2,1,0:T(8,128)(2,1)} %gradient.1), calls=%async_computation | async-start | bytes 1179648 | tf_op jit(solution)/shard_map/all_to_all | solution.py:449
  32.0 8.0 %copy-start.6 = (bf16[768,384]{1,0:T(8,128)(2,1)S(1)}, bf16[768,384]{1,0:T(8,128)(2,1)}, u32[]{:S(2)}) copy-start(bf16[768,384]{1,0:T(8,128)(2,1)} %get-tuple-element.32) | copy-start | bytes 1769476
  32.0 8.1 %copy-start.5 = (bf16[768,384]{1,0:T(8,128)(2,1)S(1)}, bf16[768,384]{1,0:T(8,128)(2,1)}, u32[]{:S(2)}) copy-start(bf16[768,384]{1,0:T(8,128)(2,1)} %get-tuple-element.31) | copy-start | bytes 1769476
  32.0 13.6 %copy-start = (bf16[384,384]{1,0:T(8,128)(2,1)S(1)}, bf16[384,384]{1,0:T(8,128)(2,1)}, u32[]{:S(2)}) copy-start(bf16[384,384]{1,0:T(8,128)(2,1)} %constant.23.clone.refs_9_) | copy-start | bytes 884740
  32.0 13.6 %copy-start.1 = (bf16[192,224]{1,0:T(8,128)(2,1)S(1)}, bf16[192,224]{1,0:T(8,128)(2,1)}, u32[]{:S(2)}) copy-start(bf16[192,224]{1,0:T(8,128)(2,1)} %constant.24.clone.refs_10_) | copy-start | bytes 258052
  40.0 2.0 %collective-permute-start.5 = (bf16[768,384]{1,0:T(8,128)(2,1)S(1)}, bf16[768,384]{1,0:T(8,128)(2,1)S(1)}, u32[]{:S(2)}, u32[]{:S(2)}) collective-permute-start(bf16[768,384]{1,0:T(8,128)(2,1)S(1)} %copy-done.6), channel_id=1, source_target_pairs={{0,8},{8,0},{16,24},{24,16},{32,40},{40,32},{48,56},{56,48},{64,72... | collective-permute-start | bytes 1769480 | tf_op jit(solution)/shard_map/ppermute | solution.py:470
  40.2 4.4 %collective-permute-start.4 = (bf16[768,384]{1,0:T(8,128)(2,1)S(1)}, bf16[768,384]{1,0:T(8,128)(2,1)S(1)}, u32[]{:S(2)}, u32[]{:S(2)}) collective-permute-start(bf16[768,384]{1,0:T(8,128)(2,1)S(1)} %copy-done.5), channel_id=1, source_target_pairs={{0,8},{8,0},{16,24},{24,16},{32,40},{40,32},{48,56},{56,48},{64,72... | collective-permute-start | bytes 1769480 | tf_op jit(solution)/shard_map/ppermute | solution.py:470
  40.5 4.2 %collective-permute-start.3 = (bf16[768,384]{1,0:T(8,128)(2,1)}, bf16[768,384]{1,0:T(8,128)(2,1)S(1)}, u32[]{:S(2)}, u32[]{:S(2)}) collective-permute-start(bf16[768,384]{1,0:T(8,128)(2,1)} %get-tuple-element.30), channel_id=1, source_target_pairs={{0,8},{8,0},{16,24},{24,16},{32,40},{40,32},{48,56},{56,48},{64,72... | collective-permute-start | bytes 1769480 | tf_op jit(solution)/shard_map/ppermute | solution.py:470
  40.7 4.2 %collective-permute-start.2 = (bf16[768,384]{1,0:T(8,128)(2,1)}, bf16[768,384]{1,0:T(8,128)(2,1)}, u32[]{:S(2)}, u32[]{:S(2)}) collective-permute-start(bf16[768,384]{1,0:T(8,128)(2,1)} %get-tuple-element.29), channel_id=1, source_target_pairs={{0,8},{8,0},{16,24},{24,16},{32,40},{40,32},{48,56},{56,48},{64,72... | collective-permute-start | bytes 1769480 | tf_op jit(solution)/shard_map/ppermute | solution.py:470
  42.0 2.9 %copy-start.2 = (bf16[768,384]{1,0:T(8,128)(2,1)}, bf16[768,384]{1,0:T(8,128)(2,1)S(1)}, u32[]{:S(2)}) copy-start(bf16[768,384]{1,0:T(8,128)(2,1)S(1)} %collective-permute-done.5.refs_7_) | copy-start | bytes 1769476
  44.5 0.8 copy-start.3
  44.7 0.9 copy-start.4
  86.5 15.6 %all-to-all-start.2 = ((bf16[8,56,384]{2,1,0:T(8,128)(2,1)}), bf16[8,56,384]{2,1,0:T(8,128)(2,1)S(1)}, u32[]{:S(2)}, u32[]{:S(2)}) async-start(bf16[8,56,384]{2,1,0:T(8,128)(2,1)} %block_sum.1), calls=%async_computation.2 | async-start | bytes 688128 | tf_op jit(solution)/shard_map/all_to_all | solution.py:509

commit v2 on v1

--- a/solution.py
+++ b/solution.py
@@ -11,7 +11,7 @@
 
 HALF = 16
 GROUP = 32
-UNROLL = 2
+UNROLL = True
 BF = jnp.bfloat16
 F32 = jnp.float32
 
@@ -96,6 +96,12 @@
             )
         )
     return jnp.concatenate(tiles, axis=1)
+
+
+def edges(core_ref, partner_ref, neighbour_ref):
+    partner, neighbour = partner_ref[...], neighbour_ref[...]
+    first = core_ref[0] == 0
+    return jnp.where(first, neighbour, partner), jnp.where(first, partner, neighbour)
 
 
 def fill_edges(before_ref, after_ref, var_from, wide_ref):
@@ -223,9 +229,10 @@
 
 
 def gradient_kernel(
+    core_ref,
     cot_planes,
-    before_ref,
-    after_ref,
+    partner_ref,
+    neighbour_ref,
     front_ref,
     back_ref,
     state_taps,
@@ -240,6 +247,7 @@
     fold,
 ):
     rows = cot_planes.shape[1]
+    before_ref, after_ref = edges(core_ref, partner_ref, neighbour_ref)
     put_ones(wide, 1.0)
     for var_from, tap_ref, frame_ref in ((0, state_taps, state_frame), (2, cot_taps, cot_frame)):
         fill_edges(before_ref, after_ref, var_from, wide)
@@ -265,9 +273,10 @@
 
 
 def slopes_kernel(
-    before_ref, after_ref, front_ref, state_taps, out_ref, wide, edge, frame
+    core_ref, partner_ref, neighbour_ref, front_ref, state_taps, out_ref, wide, edge, frame
 ):
     rows = out_ref.shape[0] - 2
+    before_ref, after_ref = edges(core_ref, partner_ref, neighbour_ref)
     put_ones(wide, 1.0)
     fill_edges(before_ref, after_ref, 0, wide)
     stack_taps(wide, edge)
@@ -336,30 +345,51 @@
         resp_out[:, var, :] = increment + folded(fold, rows, var)
 
 
-def planes_kernel(core_ref, members_ref, keep_ref, give_ref, lines):
+def planes_kernel(core_ref, members_far, *refs):
+    *outs, near, lines, planes, in_semaphores, out_semaphores = refs
     core = core_ref[0]
-    rows = members_ref.shape[1]
-    lines[...] = members_ref.reshape(rows * 2, 128)[...].astype(F32)
-    keep_ref[...] = lines[pl.ds(core, rows, stride=2), :].astype(BF)
-    give_ref[...] = lines[pl.ds(1 - core, rows, stride=2), :].astype(BF)
-
-
-def member_kernel(span, *refs):
+    count, tiles, lines_count = near.shape[:3]
+    rows = lines_count // 2
+    merged = members_far.reshape(count, lines_count, tiles * 128)
+    pairs = [
+        (merged.at[member, :, pl.ds(tile * 128, 128)], near.at[member, tile])
+        for member in range(count)
+        for tile in range(tiles)
+    ]
+    arrivals = fetch(pairs, in_semaphores)
+    departures = []
+    for member in range(count):
+        for tile in range(tiles):
+            arrivals[member * tiles + tile].wait()
+            lines[...] = near[member, tile].astype(F32)
+            window = pl.ds(tile * 128, 128)
+            planes[member, :, window] = lines[pl.ds(core, rows, stride=2), :].astype(BF)
+            planes[count + member, :, window] = lines[pl.ds(1 - core, rows, stride=2), :].astype(BF)
+        for slot in (count + member, member):
+            copy = pltpu.make_async_copy(planes.at[slot], outs[slot], out_semaphores.at[slot])
+            copy.start()
+            departures.append(copy)
+    for copy in departures:
+        copy.wait()
+
+
+def member_kernel(span, reaches, *refs):
     *far_refs, field_ref, lat_ref, lon_ref, out_ref, field, banded, total, held, semaphores = refs
     lons = field_ref.shape[0]
+    blocks = out_ref.shape[0]
+    rows = lons // blocks
     member_refs = [held.at[index] for index in range(len(far_refs))]
     copies = fetch(zip(far_refs, member_refs), semaphores)
-    blocks = out_ref.shape[0]
-    rows = lons // blocks
     field[...] = field_ref[...].astype(F32)
     for index, member_ref in enumerate(member_refs):
         copies[index].wait()
         for start in range(0, lons, span):
             window = pl.ds(start, span)
             product = (member_ref[window, :].astype(F32) * field[window, :]).astype(BF)
-            banded[pl.ds(HALF + start, span), :] = jnp.dot(
-                product, lat_ref[...], preferred_element_type=F32
-            ).astype(BF)
+            for (first, last), (low, high) in reaches:
+                banded[pl.ds(HALF + start, span), first:last] = jnp.dot(
+                    product[:, low:high], lat_ref[low:high, first:last], preferred_element_type=F32
+                ).astype(BF)
         banded[pl.ds(0, HALF), :] = banded[pl.ds(lons, HALF), :]
         banded[pl.ds(HALF + lons, HALF), :] = banded[pl.ds(HALF, HALF), :]
         for start in range(0, lons, span):
@@ -375,155 +405,234 @@
         out_ref[block] = total[pl.ds(6 + block * rows, rows + 4), :].astype(BF)
 
 
-def sum_kernel(parts_ref, out_ref):
-    for var in range(2):
-        plane = parts_ref[var].astype(F32)
-        for pair in range(1, parts_ref.shape[0] // 2):
-            plane = plane + parts_ref[2 * pair + var].astype(F32)
-        plane = plane.astype(BF)
-        for group in range(out_ref.shape[0]):
-            out_ref[group, pl.ds(var * plane.shape[0], plane.shape[0]), :] = plane
+def sum_kernel(*refs):
+    *parts_refs, out_ref = refs
+    start = 0
+    for parts_ref in parts_refs:
+        lines, lats = parts_ref.shape[1:]
+        for var in range(2):
+            plane = parts_ref[var].astype(F32)
+            for pair in range(1, parts_ref.shape[0] // 2):
+                plane = plane + parts_ref[2 * pair + var].astype(F32)
+            plane = plane.astype(BF)
+            for group in range(out_ref.shape[0]):
+                out_ref[group, pl.ds(var * lines, lines), pl.ds(start, lats)] = plane
+        start += lats
+
+
+def shape_of(*dims):
+    return jax.ShapeDtypeStruct(dims, BF)
+
+
+def wide_of(*dims):
+    return jax.ShapeDtypeStruct(dims, F32)
+
+
+FAR = pl.BlockSpec(memory_space=pltpu.HBM)
+SCALAR = pl.BlockSpec(memory_space=pltpu.SMEM)
+NEAR = pl.BlockSpec(memory_space=pltpu.VMEM)
+PARAMS = pltpu.CompilerParams(vmem_limit_bytes=24 << 20)
+
+
+def remote(value):
+    return pltpu.with_memory_space_constraint(value, pltpu.HBM)
+
+
+def padded_scratch(count, lats):
+    return pltpu.VMEM((lats // 128, count * 8, 128), F32)
+
+
+def tap_scratch(count, lats):
+    return pltpu.VMEM((count * GROUP, lats), BF)
+
+
+def prepare(state, cotangent, first, second, bias):
+    rows, var_count, lats = state.shape
+    hidden = first.shape[-1]
+    operands = (state, cotangent, first, second, bias.reshape(1, hidden))
+    return pl.pallas_call(
+        prepare_kernel,
+        out_shape=[
+            shape_of(2, hidden, 3 * GROUP),
+            shape_of(2, 48, 2 * hidden),
+            shape_of(rows * GROUP, lats),
+            shape_of(rows * GROUP, lats),
+            wide_of(lats // 128, (rows + 2) * 8, 128),
+            wide_of(var_count, rows, lats),
+        ],
+        in_specs=[FAR] * 5,
+        scratch_shapes=[
+            padded_scratch(rows, lats),
+            pltpu.VMEM((24, hidden), F32),
+            pltpu.VMEM((3, (rows + 2) * 8, lats), F32),
+            pltpu.VMEM(state.shape, F32),
+            pltpu.VMEM(state.shape, F32),
+            pltpu.VMEM(first.shape, F32),
+            pltpu.VMEM(second.shape, F32),
+            pltpu.VMEM((1, hidden), F32),
+            pltpu.SemaphoreType.DMA((5,)),
+        ],
+        compiler_params=PARAMS,
+        cost_estimate=pl.CostEstimate(
+            flops=2_000_000_000, bytes_accessed=3_000_000, transcendentals=1_100_000
+        ),
+        name="prepare",
+    )(*[remote(value) for value in operands])
+
+
+def gradient_planes(
+    blocks, core, cot_planes, partner, neighbour, front, back, state_taps, cot_taps, partial
+):
+    var_count, rows, lats = cot_planes.shape
+    return pl.pallas_call(
+        gradient_kernel,
+        out_shape=shape_of(blocks, rows, lats),
+        in_specs=[SCALAR] + [NEAR] * 8,
+        scratch_shapes=[
+            padded_scratch(4, lats),
+            tap_scratch(4, lats),
+            tap_scratch(8, lats),
+            tap_scratch(8, lats),
+            pltpu.VMEM((3, (rows + 2) * 8, lats), F32),
+            padded_scratch(rows + 2, lats),
+        ],
+        compiler_params=PARAMS,
+        cost_estimate=pl.CostEstimate(
+            flops=400_000_000, bytes_accessed=1_500_000, transcendentals=200_000
+        ),
+        name="gradient",
+    )(core, cot_planes, partner, neighbour, front, back, state_taps, cot_taps, partial)
+
+
+def member_planes(core, members):
+    count, lons, var_count, lats = members.shape
+    results = pl.pallas_call(
+        planes_kernel,
+        in_specs=[SCALAR, FAR],
+        out_specs=[FAR] * (2 * count),
+        out_shape=[pltpu.HBM((lons, lats), BF)] * (2 * count),
+        scratch_shapes=[
+            pltpu.VMEM((count, lats // 128, lons * var_count, 128), BF),
+            pltpu.VMEM((lons * 2, 128), F32),
+            pltpu.VMEM((2 * count, lons, lats), BF),
+            pltpu.SemaphoreType.DMA((count * (lats // 128),)),
+            pltpu.SemaphoreType.DMA((2 * count,)),
+        ],
+        compiler_params=PARAMS,
+        cost_estimate=pl.CostEstimate(flops=0, bytes_accessed=10_000_000, transcendentals=0),
+        name="planes",
+    )(core, remote(members))
+    return list(results[:count]), list(results[count:])
+
+
+def hidden_slopes(core, partner, neighbour, front, state_taps):
+    rows = state_taps.shape[0] // GROUP
+    hidden, lats = front.shape[1], state_taps.shape[1]
+    return pl.pallas_call(
+        slopes_kernel,
+        out_shape=pltpu.HBM((rows + 2, hidden, lats), F32),
+        in_specs=[SCALAR] + [NEAR] * 4,
+        out_specs=NEAR,
+        scratch_shapes=[padded_scratch(4, lats), tap_scratch(4, lats), tap_scratch(8, lats)],
+        compiler_params=PARAMS,
+        cost_estimate=pl.CostEstimate(
+            flops=1_000_000_000, bytes_accessed=6_000_000, transcendentals=1_200_000
+        ),
+        name="slopes",
+    )(core, partner, neighbour, front, state_taps)
+
+
+def member_sums(blocks, kept, taken, field):
+    lons, lats = field.shape
+    rows = lons // blocks
+    span = 192
+    count = len(kept) + len(taken)
+    offsets = np.arange(lats)
+    lat_loc = jnp.asarray(taps(np.abs(offsets[:, None] - offsets[None, :])))
+    reaches = (((0, 256), (0, 384)), ((256, 384), (128, 384)))
+    lon_loc = jnp.asarray(
+        taps(np.abs(np.arange(span)[:, None] + HALF - np.arange(span + 2 * HALF)[None, :]))
+    )
+    return pl.pallas_call(
+        functools.partial(member_kernel, span, reaches),
+        in_specs=[FAR] * count + [NEAR] * 3,
+        out_shape=shape_of(blocks, rows + 4, lats),
+        scratch_shapes=[
+            pltpu.VMEM((lons, lats), F32),
+            pltpu.VMEM((lons + 2 * HALF, lats), BF),
+            pltpu.VMEM((lons + 16, lats), F32),
+            pltpu.VMEM((count, lons, lats), BF),
+            pltpu.SemaphoreType.DMA((count,)),
+        ],
+        compiler_params=PARAMS,
+        cost_estimate=pl.CostEstimate(
+            flops=4_000_000_000, bytes_accessed=6_000_000, transcendentals=0
+        ),
+        name="members",
+    )(*[remote(value) for value in kept + taken], field, lat_loc, lon_loc)
+
+
+def block_sums(groups, arrived):
+    lines = arrived[0].shape[1]
+    lats = sum(part.shape[2] for part in arrived)
+    return pl.pallas_call(
+        sum_kernel,
+        out_shape=shape_of(groups, 2 * lines, lats),
+        compiler_params=PARAMS,
+        name="block_sum",
+    )(*arrived)
+
+
+def responses(scale, copies, slopes, front, back):
+    rows = copies.shape[1] // 2 - 4
+    hidden, lats = slopes.shape[1:]
+    return pl.pallas_call(
+        functools.partial(response_kernel, scale),
+        out_shape=[wide_of(rows, 2, lats)] * 2,
+        in_specs=[NEAR, FAR, NEAR, NEAR],
+        scratch_shapes=[
+            padded_scratch(rows + 4, lats),
+            tap_scratch(rows + 4, lats),
+            pltpu.VMEM((3, (rows + 2) * 8, lats), F32),
+            padded_scratch(rows + 2, lats),
+            pltpu.VMEM((rows + 2, hidden, lats), F32),
+            pltpu.SemaphoreType.DMA((2,)),
+        ],
+        compiler_params=PARAMS,
+        name="response",
+    )(copies, remote(slopes), front, back)
 
 
 def per_device(members, state, cotangent, conv_in, conv_out, bias):
     blocks = lax.axis_size("space")
     groups = lax.axis_size("mem")
     held, lons, var_count, lats = members.shape
-    rows = state.shape[0]
-    tiles = lats // 128
     core = lax.axis_index("space") % 2
-    small = pltpu.CompilerParams(vmem_limit_bytes=24 << 20)
-    right = [(i, (i + 1) % blocks) for i in range(blocks)]
-    left = [((i + 1) % blocks, i) for i in range(blocks)]
     swap = [(i, i ^ 1) for i in range(blocks)]
+    chain = [(i, (i + 1 if i % 2 else i - 1) % blocks) for i in range(blocks)]
     tail = jnp.concatenate([state[-2:], cotangent[-2:]], axis=1)
     head = jnp.concatenate([state[:2], cotangent[:2]], axis=1)
-    before = lax.ppermute(tail, "space", right)
-    after = lax.ppermute(head, "space", left)
-    hidden = conv_in.shape[2]
-    shape = jax.ShapeDtypeStruct
-    padded = lambda count: pltpu.VMEM((tiles, count * 8, 128), F32)
-    tap = lambda count: pltpu.VMEM((count * GROUP, lats), BF)
-    product = pltpu.VMEM((3, (rows + 2) * 8, lats), F32)
+    neighbour = lax.ppermute(jnp.where(core == 0, head, tail), "space", chain)
+    partner = lax.ppermute(jnp.where(core == 0, tail, head), "space", swap)
+    core = core.reshape(1)
     first = jnp.transpose(conv_in, (0, 1, 3, 2))
-    far = pl.BlockSpec(memory_space=pltpu.HBM)
-    near = pl.BlockSpec(memory_space=pltpu.VMEM)
-    remote = lambda value: pltpu.with_memory_space_constraint(value, pltpu.HBM)
-    front, back, state_taps, cot_taps, partial, cot_planes = pl.pallas_call(
-        prepare_kernel,
-        out_shape=[
-            shape((2, hidden, 3 * GROUP), BF),
-            shape((2, 48, 2 * hidden), BF),
-            shape((rows * GROUP, lats), BF),
-            shape((rows * GROUP, lats), BF),
-            shape((tiles, (rows + 2) * 8, 128), F32),
-            shape((var_count, rows, lats), F32),
-        ],
-        in_specs=[far] * 5,
-        scratch_shapes=[
-            padded(rows),
-            pltpu.VMEM((24, hidden), F32),
-            product,
-            pltpu.VMEM(state.shape, F32),
-            pltpu.VMEM(state.shape, F32),
-            pltpu.VMEM(first.shape, F32),
-            pltpu.VMEM(conv_out.shape, F32),
-            pltpu.VMEM((1, hidden), F32),
-            pltpu.SemaphoreType.DMA((5,)),
-        ],
-        compiler_params=small,
-        cost_estimate=pl.CostEstimate(flops=2_000_000_000, bytes_accessed=3_000_000, transcendentals=1_100_000),
-        name="prepare",
-    )(*[remote(value) for value in (state, cotangent, first, conv_out, bias.reshape(1, hidden))])
-    outgoing = pl.pallas_call(
-        gradient_kernel,
-        out_shape=shape((blocks, rows, lats), BF),
-        scratch_shapes=[
-            padded(4), tap(4), tap(8), tap(8), product, padded(rows + 2)
-        ],
-        compiler_params=small,
-        cost_estimate=pl.CostEstimate(flops=400_000_000, bytes_accessed=1_500_000, transcendentals=200_000),
-        name="gradient",
-    )(cot_planes, before, after, front, back, state_taps, cot_taps, partial)
+    front, back, state_taps, cot_taps, partial, cot_planes = prepare(
+        state, cotangent, first, conv_out, bias
+    )
+    outgoing = gradient_planes(
+        blocks, core, cot_planes, partner, neighbour, front, back, state_taps, cot_taps, partial
+    )
     members, outgoing = lax.optimization_barrier((members, outgoing))
     gathered = lax.all_to_all(outgoing, "space", 0, 0, tiled=True)
-    kept, taken = [], []
-    members = remote(members)
-    for member in range(held):
-        keep, give = pl.pallas_call(
-            planes_kernel,
-            grid_spec=pltpu.PrefetchScalarGridSpec(
-                num_scalar_prefetch=1,
-                grid=(tiles,),
-                in_specs=[
-                    pl.BlockSpec((1, lons, var_count, 128), lambda j, c, member=member: (member, 0, 0, j))
-                ],
-                out_specs=[pl.BlockSpec((lons, 128), lambda j, c: (0, j))] * 2,
-                scratch_shapes=[pltpu.VMEM((lons * 2, 128), F32)],
-            ),
-            out_shape=[pltpu.HBM((lons, lats), BF)] * 2,
-            compiler_params=small,
-            cost_estimate=pl.CostEstimate(flops=0, bytes_accessed=10_000_000, transcendentals=0),
-            name="planes",
-        )(core.reshape(1), members)
-        kept.append(keep)
-        taken.append(lax.ppermute(give, "space", swap))
-    slopes = pl.pallas_call(
-        slopes_kernel,
-        out_shape=pltpu.HBM((rows + 2, hidden, lats), F32),
-        out_specs=near,
-        scratch_shapes=[padded(4), tap(4), tap(8)],
-        compiler_params=small,
-        cost_estimate=pl.CostEstimate(flops=1_000_000_000, bytes_accessed=6_000_000, transcendentals=1_200_000),
-        name="slopes",
-    )(before, after, front, state_taps)
-
-    span = 192
-    offsets = np.arange(lats)
-    lat_loc = jnp.asarray(taps(np.abs(offsets[:, None] - offsets[None, :])))
-    lon_loc = jnp.asarray(
-        taps(np.abs(np.arange(span)[:, None] + HALF - np.arange(span + 2 * HALF)[None, :]))
-    )
-    parts = pl.pallas_call(
-        functools.partial(member_kernel, span),
-        in_specs=[far] * (2 * held) + [near] * 3,
-        out_shape=jax.ShapeDtypeStruct((blocks, rows + 4, lats), BF),
-        scratch_shapes=[
-            pltpu.VMEM((lons, lats), F32),
-            pltpu.VMEM((lons + 2 * HALF, lats), BF),
-            pltpu.VMEM((lons + 16, lats), F32),
-            pltpu.VMEM((2 * held, lons, lats), BF),
-            pltpu.SemaphoreType.DMA((2 * held,)),
-        ],
-        compiler_params=small,
-        cost_estimate=pl.CostEstimate(flops=4_000_000_000, bytes_accessed=6_000_000, transcendentals=0),
-        name="members",
-    )(*[remote(value) for value in kept + taken], gathered.reshape(lons, lats), lat_loc, lon_loc)
-    arrived = lax.all_to_all(parts, "space", 0, 0, tiled=True)
-    spread = pl.pallas_call(
-        sum_kernel,
-        out_shape=jax.ShapeDtypeStruct((groups, 2 * (rows + 4), lats), BF),
-        compiler_params=small,
-        name="block_sum",
-    )(arrived)
+    kept, given = member_planes(core, members)
+    taken = [lax.ppermute(give, "space", swap) for give in given]
+    slopes = hidden_slopes(core, partner, neighbour, front, state_taps)
+    parts = member_sums(blocks, kept, taken, gathered.reshape(lons, lats))
+    arrived = [lax.all_to_all(parts, "space", 0, 0, tiled=True)]
+    spread = block_sums(groups, arrived)
     copies = lax.all_to_all(spread, "mem", 0, 0, tiled=True)
     member_count = held * blocks * groups
-    field = jax.ShapeDtypeStruct(state.shape, F32)
-    increment, response = pl.pallas_call(
-        functools.partial(response_kernel, 1.0 / (member_count - 1.0)),
-        out_shape=[field, field],
-        in_specs=[near, far, near, near],
-        scratch_shapes=[
-            padded(rows + 4),
-            tap(rows + 4),
-            product,
-            padded(rows + 2),
-            pltpu.VMEM((rows + 2, hidden, lats), F32),
-            pltpu.SemaphoreType.DMA((2,)),
-        ],
-        compiler_params=small,
-        name="response",
-    )(copies, remote(slopes), front, back)
+    increment, response = responses(1.0 / (member_count - 1.0), copies, slopes, front, back)
     return (increment, response)
 
 

time: 112 us -> 98.6 us (0.88)
  Pallas kernels: 48.5 us -> 32.9 us
  waiting for transfers between devices: 8.21 us -> 17.9 us
  blocking collectives: 31.4 us -> 26.6 us
  starting transfers between devices: 20.4 us -> 18.2 us
    pallas_call x10 -> x7, Pallas kernels: 48.5 us -> 32.9 us  [the longest x1 8.2 us: member_sums(): pl.pallas_call(functools.partial(member_kernel, span, reaches), in_specs=...]
    all_to_all x1, waiting for transfers between devices: 0.01 us -> 9.82 us  [per_device(): gathered = lax.all_to_all(outgoing, 'space', 0, 0, tiled=True)]
    all_to_all x1, blocking collectives: 31.4 us -> 26.6 us  [per_device(): arrived = [lax.all_to_all(parts, 'space', 0, 0, tiled=True)]]
    all_to_all x1, starting transfers between devices: 11.2 us -> 8.68 us  [per_device(): gathered = lax.all_to_all(outgoing, 'space', 0, 0, tiled=True)]
  transfers between devices with their start and end apart: 8 -> 8, of which waited for: 5 -> 5; matrix products, arithmetic and copies ran while one was open for 0% -> 0% of each run, Pallas kernels for 25% -> 15%
where the time goes in v2:
time: 98.6 us; the launch traced here: 98.2 us
  Pallas kernels  32.9 us (33%)
  blocking collectives  26.6 us (27%)
  starting transfers between devices  18.2 us (18%)
  waiting for transfers between devices  17.9 us (18%)
  local copies, waits for them, and re-layouts  1.59 us (2%)
    all_to_all x1, blocking collectives, per_device(): arrived = [lax.all_to_all(parts, 'space', 0, 0, tiled=True)]  26.6 us
    all_to_all x1, waiting for transfers between devices, per_device(): gathered = lax.all_to_all(outgoing, 'space', 0, 0, tiled=True)  9.82 us
    all_to_all x1, starting transfers between devices, per_device(): gathered = lax.all_to_all(outgoing, 'space', 0, 0, tiled=True)  8.68 us
    pallas_call x1, Pallas kernels, member_sums(): pl.pallas_call(functools.partial(member_kernel, span, reaches), in_specs=...  8.2 us
    pallas_call x1, Pallas kernels, responses(): pl.pallas_call(functools.partial(response_kernel, scale), out_shape=[wide...  7.31 us
    all_to_all x1, starting transfers between devices, per_device(): copies = lax.all_to_all(spread, 'mem', 0, 0, tiled=True)  6.06 us
    pallas_call x1, Pallas kernels, prepare(): pl.pallas_call(prepare_kernel, out_shape=[shape_of(2, hidden, 3 * GROUP),...  5.92 us
    pallas_call x1, Pallas kernels, hidden_slopes(): pl.pallas_call(slopes_kernel, out_shape=pltpu.HBM((rows + 2, hidden, lats...  4.86 us
  transfers between devices with their start and end apart: 8, of which 5 were waited for; matrix products, arithmetic and copies ran while one was open for 0% of the time, Pallas kernels for 15%

profile of v2, /device:TPU:8, one launch (start us, length us, event | category | flops | bytes accessed | tf_op | source)
XLA Modules:
  0.0 98.2 jit_solution(302071438137438984)
XLA Ops:
  0.6 0.8 fusion.2
  1.4 0.1 collective-permute-start
  1.5 2.3 %collective-permute-start.1 = (f32[2,4,384]{2,1,0:T(4,128)S(1)}, f32[2,4,384]{2,1,0:T(4,128)S(1)}, u32[]{:S(2)}, u32[]{:S(2)}) collective-permute-start(f32[2,4,384]{2,1,0:T(4,128)S(1)} %get-tuple-element.38), channel_id=1, source_target_pairs={{0,248},{8,16},{16,8},{24,32},{32,24},{40,48},{48,40},{56,64},{64,... | collective-permute-start | bytes 36872 | tf_op jit(solution)/shard_map/ppermute | solution.py:615
  3.8 5.9 %prepare.1 = (bf16[2,128,96]{2,1,0:T(8,128)(2,1)S(1)}, bf16[2,48,256]{2,1,0:T(8,128)(2,1)S(1)}, bf16[768,384]{1,0:T(8,128)(2,1)S(1)}, bf16[768,384]{1,0:T(8,128)...) custom-call(f32[24,2,384]{2,1,0:T(2,128)} %state_far.1, f32[24,2,384]{2,1,0:T(2,128)} %cot_far.1, ...), custom_call_target="tpu_custom_call" | custom-call | flops 2000000000 | bytes 3000000 | tf_op jit(solution)/shard_map/prepare/pallas_call | solution.py:453
  9.7 0.0 copy-start
  9.7 0.0 copy-start.1
  9.8 0.0 collective-permute-done.partner_ref
  9.8 0.0 collective-permute-done.1.neighbour_ref
  9.8 2.0 %gradient.1 = bf16[32,24,384]{2,1,0:T(8,128)(2,1)} custom-call(s32[1]{0:T(128)} %bitcast.core_ref, f32[2,24,384]{2,1,0:T(8,128)S(1)} %get-tuple-element.18.cot_planes, f32[2,4,384]{2,1,0:T(4,128)S(1)} %collective-permute-done.partner_ref, f32[2,4,384]{2,1,0:T(4,128)S(1)} %collective-permute-done.1.neighbour_ref, ...), custom_call_target="tpu_custom_call" | custom-call | flops 400000000 | bytes 1500000 | tf_op jit(solution)/shard_map/gradient/pallas_call | solution.py:487
  11.8 8.7 %all-to-all-start = ((bf16[32,24,384]{2,1,0:T(8,128)(2,1)}), bf16[32,24,384]{2,1,0:T(8,128)(2,1)S(1)}, u32[]{:S(2)}, u32[]{:S(2)}) async-start(bf16[32,24,384]{2,1,0:T(8,128)(2,1)} %gradient.1), calls=%async_computation | async-start | bytes 1179648 | tf_op jit(solution)/shard_map/all_to_all | solution.py:626
  20.5 3.7 %planes.1 = (bf16[768,384]{1,0:T(8,128)(2,1)}, bf16[768,384]{1,0:T(8,128)(2,1)}, bf16[768,384]{1,0:T(8,128)(2,1)}, bf16[768,384]{1,0:T(8,128)(2,1)}, bf16[768,38...) custom-call(s32[1]{0:T(128)} %bitcast.core_ref, ...), custom_call_target="tpu_custom_call" | custom-call | bytes 10000000 | tf_op jit(solution)/shard_map/planes/pallas_call | solution.py:509
  24.2 0.2 collective-permute-start.2
  24.5 0.4 collective-permute-start.3
  24.8 0.1 collective-permute-start.4
  25.0 0.4 collective-permute-start.5
  25.3 1.2 %collective-permute-done.2.refs_4_ = bf16[768,384]{1,0:T(8,128)(2,1)S(1)} collective-permute-done((bf16[768,384]{1,0:T(8,128)(2,1)}, bf16[768,384]{1,0:T(8,128)(2,1)S(1)}, u32[]{:S(2)}, u32[]{:S(2)}) %collective-permute-start.2) | collective-permute-done | bytes 589856 | tf_op jit(solution)/shard_map/ppermute | solution.py:628
  26.5 0.0 copy-start.2
  26.5 1.7 %collective-permute-done.3.refs_5_ = bf16[768,384]{1,0:T(8,128)(2,1)S(1)} collective-permute-done((bf16[768,384]{1,0:T(8,128)(2,1)}, bf16[768,384]{1,0:T(8,128)(2,1)S(1)}, u32[]{:S(2)}, u32[]{:S(2)}) %collective-permute-start.3) | collective-permute-done | bytes 589856 | tf_op jit(solution)/shard_map/ppermute | solution.py:628
  28.2 0.0 copy-start.3
  28.2 0.8 collective-permute-done.4.refs_6_
  29.1 0.0 copy-start.4
  29.1 0.8 copy-done.4
  29.9 0.0 collective-permute-done.5.refs_7_
  29.9 9.8 %all-to-all-done = bf16[32,24,384]{2,1,0:T(8,128)(2,1)S(1)} async-done(((bf16[32,24,384]{2,1,0:T(8,128)(2,1)}), bf16[32,24,384]{2,1,0:T(8,128)(2,1)S(1)}, u32[]{:S(2)}, u32[]{:S(2)}) %all-to-all-start) | async-done | bytes 589856 | tf_op jit(solution)/shard_map/all_to_all | solution.py:626
  39.7 0.0 copy-done.2
  39.7 0.0 copy-done.3
  39.7 0.0 copy-done
  39.7 0.0 copy-done.1
  39.7 8.2 %members.1 = bf16[32,28,384]{2,1,0:T(8,128)(2,1)S(1)} custom-call(bf16[768,384]{1,0:T(8,128)(2,1)} %get-tuple-element.25.refs_0_, bf16[768,384]{1,0:T(8,128)(2,1)} %get-tuple-element.26.refs_1_, bf16[768,384]{1,0:T(8,128)(2,1)} %get-tuple-element.27.refs_2_, bf16[768,384]{1,0:T(8,128)(2,1)} %get-tuple-element.28.refs_3_, bf16[768,384]{1,0:T(8,128)(2,1)} %copy-done.2, ...), custom_call_target="tpu_custom_call" | custom-call | flops 4000000000 | bytes 6000000 | tf_op jit(solution)/shard_map/members/pallas_call | solution.py:556
  47.9 26.6 %all_to_all.15.refs_0_ = bf16[32,28,384]{2,1,0:T(8,128)(2,1)S(1)} all-to-all(bf16[32,28,384]{2,1,0:T(8,128)(2,1)S(1)} %members.1), channel_id=1, replica_groups=mesh['space'=32,'mem'=8] {'space'}, dimensions={0} | all-to-all | bytes 1376256 | tf_op jit(solution)/shard_map/all_to_all | solution.py:631
  74.6 0.9 block_sum.1
  75.4 6.1 %all-to-all-start.2 = ((bf16[8,56,384]{2,1,0:T(8,128)(2,1)}), bf16[8,56,384]{2,1,0:T(8,128)(2,1)S(1)}, u32[]{:S(2)}, u32[]{:S(2)}) async-start(bf16[8,56,384]{2,1,0:T(8,128)(2,1)} %block_sum.1), calls=%async_computation.2 | async-start | bytes 688128 | tf_op jit(solution)/shard_map/all_to_all | solution.py:633
  81.5 4.9 %slopes.1.slopes_far = f32[26,128,384]{2,1,0:T(8,128)} custom-call(s32[1]{0:T(128)} %bitcast.core_ref, f32[2,4,384]{2,1,0:T(4,128)S(1)} %collective-permute-done.partner_ref, f32[2,4,384]{2,1,0:T(4,128)S(1)} %collective-permute-done.1.neighbour_ref, bf16[2,128,96]{2,1,0:T(8,128)(2,1)S(1)} %get-tuple-element.19.front_ref, ...), custom_call_target="tpu_custom_call" | custom-call | flops 1000000000 | bytes 6000000 | tf_op jit(solution)/shard_map/slopes/pallas_call | solution.py:531
  86.3 4.4 %all-to-all-done.2.copies_ref = bf16[8,56,384]{2,1,0:T(8,128)(2,1)S(1)} async-done(((bf16[8,56,384]{2,1,0:T(8,128)(2,1)}), bf16[8,56,384]{2,1,0:T(8,128)(2,1)S(1)}, u32[]{:S(2)}, u32[]{:S(2)}) %all-to-all-start.2) | async-done | bytes 344096 | tf_op jit(solution)/shard_map/all_to_all | solution.py:633
  90.7 7.3 %response.1 = (f32[24,2,384]{2,1,0:T(2,128)}, f32[24,2,384]{2,1,0:T(2,128)}) custom-call(bf16[8,56,384]{2,1,0:T(8,128)(2,1)S(1)} %all-to-all-done.2.copies_ref, f32[26,128,384]{2,1,0:T(8,128)} %slopes.1.slopes_far, bf16[2,128,96]{2,1,0:T(8,128)(2,1)S(1)} %get-tuple-element.19.front_ref, bf16[2,48,256]{2,1,0:T(8,128)(2,1)S(1)} %get-tuple-element.20.back_ref), custom_call_target="tpu_custom_call" | custom-call | tf_op jit(solution)/shard_map/response/pallas_call | solution.py:589
  (1 shorter events, 0.0 us)
Async XLA Ops:
  1.4 8.3 %collective-permute-start = (f32[2,4,384]{2,1,0:T(4,128)S(1)}, f32[2,4,384]{2,1,0:T(4,128)S(1)}, u32[]{:S(2)}, u32[]{:S(2)}) collective-permute-start(f32[2,4,384]{2,1,0:T(4,128)S(1)} %get-tuple-element.39), channel_id=1, source_target_pairs={{0,8},{8,0},{16,24},{24,16},{32,40},{40,32},{48,56},{56,48},{64,72... | collective-permute-start | bytes 36872 | tf_op jit(solution)/shard_map/ppermute | solution.py:616
  1.5 8.3 %collective-permute-start.1 = (f32[2,4,384]{2,1,0:T(4,128)S(1)}, f32[2,4,384]{2,1,0:T(4,128)S(1)}, u32[]{:S(2)}, u32[]{:S(2)}) collective-permute-start(f32[2,4,384]{2,1,0:T(4,128)S(1)} %get-tuple-element.38), channel_id=1, source_target_pairs={{0,248},{8,16},{16,8},{24,32},{32,24},{40,48},{48,40},{56,64},{64,... | collective-permute-start | bytes 36872 | tf_op jit(solution)/shard_map/ppermute | solution.py:615
  9.7 30.0 %copy-start = (bf16[384,384]{1,0:T(8,128)(2,1)S(1)}, bf16[384,384]{1,0:T(8,128)(2,1)}, u32[]{:S(2)}) copy-start(bf16[384,384]{1,0:T(8,128)(2,1)} %constant.24.clone.refs_9_) | copy-start | bytes 884740
  9.7 30.0 %copy-start.1 = (bf16[192,224]{1,0:T(8,128)(2,1)S(1)}, bf16[192,224]{1,0:T(8,128)(2,1)}, u32[]{:S(2)}) copy-start(bf16[192,224]{1,0:T(8,128)(2,1)} %constant.25.clone.refs_10_) | copy-start | bytes 258052
  11.8 27.9 %all-to-all-start = ((bf16[32,24,384]{2,1,0:T(8,128)(2,1)}), bf16[32,24,384]{2,1,0:T(8,128)(2,1)S(1)}, u32[]{:S(2)}, u32[]{:S(2)}) async-start(bf16[32,24,384]{2,1,0:T(8,128)(2,1)} %gradient.1), calls=%async_computation | async-start | bytes 1179648 | tf_op jit(solution)/shard_map/all_to_all | solution.py:626
  24.2 2.3 %collective-permute-start.2 = (bf16[768,384]{1,0:T(8,128)(2,1)}, bf16[768,384]{1,0:T(8,128)(2,1)S(1)}, u32[]{:S(2)}, u32[]{:S(2)}) collective-permute-start(bf16[768,384]{1,0:T(8,128)(2,1)} %get-tuple-element.29), channel_id=1, source_target_pairs={{0,8},{8,0},{16,24},{24,16},{32,40},{40,32},{48,56},{56,48},{64,72... | collective-permute-start | bytes 1769480 | tf_op jit(solution)/shard_map/ppermute | solution.py:628
  24.5 3.8 %collective-permute-start.3 = (bf16[768,384]{1,0:T(8,128)(2,1)}, bf16[768,384]{1,0:T(8,128)(2,1)S(1)}, u32[]{:S(2)}, u32[]{:S(2)}) collective-permute-start(bf16[768,384]{1,0:T(8,128)(2,1)} %get-tuple-element.30), channel_id=1, source_target_pairs={{0,8},{8,0},{16,24},{24,16},{32,40},{40,32},{48,56},{56,48},{64,72... | collective-permute-start | bytes 1769480 | tf_op jit(solution)/shard_map/ppermute | solution.py:628
  24.8 4.2 %collective-permute-start.4 = (bf16[768,384]{1,0:T(8,128)(2,1)}, bf16[768,384]{1,0:T(8,128)(2,1)S(1)}, u32[]{:S(2)}, u32[]{:S(2)}) collective-permute-start(bf16[768,384]{1,0:T(8,128)(2,1)} %get-tuple-element.31), channel_id=1, source_target_pairs={{0,8},{8,0},{16,24},{24,16},{32,40},{40,32},{48,56},{56,48},{64,72... | collective-permute-start | bytes 1769480 | tf_op jit(solution)/shard_map/ppermute | solution.py:628
  25.0 4.9 %collective-permute-start.5 = (bf16[768,384]{1,0:T(8,128)(2,1)}, bf16[768,384]{1,0:T(8,128)(2,1)}, u32[]{:S(2)}, u32[]{:S(2)}) collective-permute-start(bf16[768,384]{1,0:T(8,128)(2,1)} %get-tuple-element.32), channel_id=1, source_target_pairs={{0,8},{8,0},{16,24},{24,16},{32,40},{40,32},{48,56},{56,48},{64,72... | collective-permute-start | bytes 1769480 | tf_op jit(solution)/shard_map/ppermute | solution.py:628
  26.5 13.2 %copy-start.2 = (bf16[768,384]{1,0:T(8,128)(2,1)}, bf16[768,384]{1,0:T(8,128)(2,1)S(1)}, u32[]{:S(2)}) copy-start(bf16[768,384]{1,0:T(8,128)(2,1)S(1)} %collective-permute-done.2.refs_4_) | copy-start | bytes 1769476
  28.2 11.5 %copy-start.3 = (bf16[768,384]{1,0:T(8,128)(2,1)}, bf16[768,384]{1,0:T(8,128)(2,1)S(1)}, u32[]{:S(2)}) copy-start(bf16[768,384]{1,0:T(8,128)(2,1)S(1)} %collective-permute-done.3.refs_5_) | copy-start | bytes 1769476
  29.1 0.8 copy-start.4
  75.4 15.3 %all-to-all-start.2 = ((bf16[8,56,384]{2,1,0:T(8,128)(2,1)}), bf16[8,56,384]{2,1,0:T(8,128)(2,1)S(1)}, u32[]{:S(2)}, u32[]{:S(2)}) async-start(bf16[8,56,384]{2,1,0:T(8,128)(2,1)} %block_sum.1), calls=%async_computation.2 | async-start | bytes 688128 | tf_op jit(solution)/shard_map/all_to_all | solution.py:633

commit v3 on v2

--- a/solution.py
+++ b/solution.py
@@ -11,7 +11,7 @@
 
 HALF = 16
 GROUP = 32
-UNROLL = True
+BATCH = 11
 BF = jnp.bfloat16
 F32 = jnp.float32
 
@@ -66,14 +66,31 @@
         wide_ref[tile, pl.ds(7, rows, stride=8), :] = jnp.zeros((rows, 128), F32)
 
 
-def fold_hidden(hidden, back_weight, product_ref, row):
-    high, low = split_high_low(hidden)
+def fold_rows(hiddens, back_weight, product_ref, rows):
+    lats = hiddens[0].shape[1]
+    high, low = split_high_low(jnp.concatenate(hiddens, axis=1))
     product = jnp.dot(
         back_weight, jnp.concatenate([high, low], axis=0), preferred_element_type=F32
     )
     product = product[:24] + product[24:]
-    for step in range(3):
-        product_ref[step, pl.ds(pl.multiple_of(row * 8, 8), 8), :] = product[8 * step : 8 * step + 8]
+    for at, row in enumerate(rows):
+        for step in range(3):
+            product_ref[step, pl.ds(row * 8, 8), :] = product[
+                8 * step : 8 * step + 8, at * lats : (at + 1) * lats
+            ]
+
+
+def backward_rows(front_ref, windows):
+    activity = [jnp.dot(front_ref[0], state(), preferred_element_type=F32) for state, _ in windows]
+    hidden = [jnp.dot(front_ref[1], cot(), preferred_element_type=F32) for _, cot in windows]
+    for at in range(len(windows)):
+        active = jnp.tanh(activity[at])
+        hidden[at] = (1.0 - active * active) * hidden[at]
+    return hidden
+
+
+def window_of(ref, row):
+    return lambda: ref[pl.ds(row * GROUP, 3 * GROUP), :]
 
 
 def fold_lats(product_ref, fold_ref, first, count):
@@ -110,10 +127,6 @@
         for row in range(2):
             put_taps(wide_ref, before_ref[row, line : line + 1, :], row, var)
             put_taps(wide_ref, after_ref[row, line : line + 1, :], 2 + row, var)
-
-
-def tap_window(row):
-    return pl.ds(pl.multiple_of(row * GROUP, GROUP), 3 * GROUP)
 
 
 def bands(tap_ref, edge_ref, frame_ref):
@@ -213,18 +226,12 @@
             put_taps(wide, plane, 0, var)
         stack_taps(wide, tap_ref)
 
-    def step(row, carry):
-        activity = jnp.tanh(
-            jnp.dot(front_ref[0], state_taps[tap_window(row), :], preferred_element_type=F32)
+    for first in range(0, rows - 2, BATCH):
+        batch = range(first, min(first + BATCH, rows - 2))
+        hidden = backward_rows(
+            front_ref, [(window_of(state_taps, row), window_of(cot_taps, row)) for row in batch]
         )
-        slopes = 1.0 - activity * activity
-        hidden = slopes * jnp.dot(
-            front_ref[1], cot_taps[tap_window(row), :], preferred_element_type=F32
-        )
-        fold_hidden(hidden, back_ref[0], product, row + 2)
-        return carry
-
-    lax.fori_loop(0, rows - 2, step, 0, unroll=UNROLL)
+        fold_rows(hidden, back_ref[0], product, [row + 2 for row in batch])
     fold_lats(product, fold, 2, rows - 2)
 
 
@@ -254,16 +261,10 @@
         stack_taps(wide, edge)
         bands(tap_ref, edge, frame_ref)
     fold[...] = fold_ref[...]
-    for start, row in ((0, 0), (1, 1), (4, rows), (5, rows + 1)):
-        window = pl.ds(start * GROUP, 3 * GROUP)
-        activity = jnp.tanh(
-            jnp.dot(front_ref[0], state_frame[window, :], preferred_element_type=F32)
-        )
-        slopes = 1.0 - activity * activity
-        hidden = slopes * jnp.dot(
-            front_ref[1], cot_frame[window, :], preferred_element_type=F32
-        )
-        fold_hidden(hidden, back_ref[0], product, row)
+    hidden = backward_rows(
+        front_ref, [(window_of(state_frame, at), window_of(cot_frame, at)) for at in (0, 1, 4, 5)]
+    )
+    fold_rows(hidden, back_ref[0], product, (0, 1, rows, rows + 1))
     fold_lats(product, fold, 0, 2)
     fold_lats(product, fold, rows, 2)
     for var in range(2):
@@ -282,18 +283,15 @@
     stack_taps(wide, edge)
     bands(state_taps, edge, frame)
 
-    def slopes(window):
-        activity = jnp.tanh(jnp.dot(front_ref[0], window, preferred_element_type=F32))
-        return 1.0 - activity * activity
-
-    for start, row in ((0, 0), (1, 1), (4, rows), (5, rows + 1)):
-        out_ref[row] = slopes(frame[pl.ds(start * GROUP, 3 * GROUP), :])
-
-    def step(row, carry):
-        out_ref[row + 2] = slopes(state_taps[tap_window(row), :])
-        return carry
-
-    lax.fori_loop(0, rows - 2, step, 0, unroll=2)
+    windows = [window_of(frame, at) for at in (0, 1)]
+    windows += [window_of(state_taps, row) for row in range(rows - 2)]
+    windows += [window_of(frame, at) for at in (4, 5)]
+    for first in range(0, rows + 2, BATCH):
+        batch = range(first, min(first + BATCH, rows + 2))
+        dots = [jnp.dot(front_ref[0], windows[row](), preferred_element_type=F32) for row in batch]
+        for row, value in zip(batch, dots):
+            active = jnp.tanh(value)
+            out_ref[row] = 1.0 - active * active
 
 
 def response_kernel(
@@ -327,17 +325,15 @@
         put_taps(wide, plane, 0, var)
     stack_taps(wide, incr_taps)
 
-    def step(row, carry):
-        hidden = slopes_ref[row] * jnp.dot(
-            front_ref[0], incr_taps[tap_window(row), :], preferred_element_type=F32
-        )
-        fold_hidden(hidden, back_ref[1], product, row)
-        return carry
-
-    copies[0].wait()
-    lax.fori_loop(0, half, step, 0, unroll=UNROLL)
-    copies[1].wait()
-    lax.fori_loop(half, rows + 2, step, 0, unroll=UNROLL)
+    for part in range(2):
+        batch = range(part * half, (part + 1) * half)
+        hidden = [
+            jnp.dot(front_ref[0], window_of(incr_taps, row)(), preferred_element_type=F32)
+            for row in batch
+        ]
+        copies[part].wait()
+        hidden = [slopes_ref[row] * value for row, value in zip(batch, hidden)]
+        fold_rows(hidden, back_ref[1], product, batch)
     fold_lats(product, fold, 0, rows + 2)
     for var in range(2):
         increment = planes[var][2 : 2 + rows]
@@ -381,24 +377,32 @@
     member_refs = [held.at[index] for index in range(len(far_refs))]
     copies = fetch(zip(far_refs, member_refs), semaphores)
     field[...] = field_ref[...].astype(F32)
+    lats = field_ref.shape[1]
+    chunk = 2 * span
     for index, member_ref in enumerate(member_refs):
         copies[index].wait()
-        for start in range(0, lons, span):
-            window = pl.ds(start, span)
+        at = index * lats
+        for start in range(0, lons, chunk):
+            window = pl.ds(start, chunk)
             product = (member_ref[window, :].astype(F32) * field[window, :]).astype(BF)
             for (first, last), (low, high) in reaches:
-                banded[pl.ds(HALF + start, span), first:last] = jnp.dot(
+                banded[pl.ds(HALF + start, chunk), at + first : at + last] = jnp.dot(
                     product[:, low:high], lat_ref[low:high, first:last], preferred_element_type=F32
                 ).astype(BF)
-        banded[pl.ds(0, HALF), :] = banded[pl.ds(lons, HALF), :]
-        banded[pl.ds(HALF + lons, HALF), :] = banded[pl.ds(HALF, HALF), :]
-        for start in range(0, lons, span):
+    banded[pl.ds(0, HALF), :] = banded[pl.ds(lons, HALF), :]
+    banded[pl.ds(HALF + lons, HALF), :] = banded[pl.ds(HALF, HALF), :]
+    for start in range(0, lons, span):
+        value = None
+        for index, member_ref in enumerate(member_refs):
+            at = index * lats
             spread = jnp.dot(
-                lon_ref[...], banded[pl.ds(start, span + 2 * HALF), :], preferred_element_type=F32
+                lon_ref[...],
+                banded[pl.ds(start, span + 2 * HALF), at : at + lats],
+                preferred_element_type=F32,
             )
-            window = pl.ds(8 + start, span)
-            value = member_ref[pl.ds(start, span), :].astype(F32) * spread
-            total[window, :] = value if index == 0 else total[window, :] + value
+            term = member_ref[pl.ds(start, span), :].astype(F32) * spread
+            value = term if value is None else value + term
+        total[pl.ds(8 + start, span), :] = value
     total[pl.ds(0, 8), :] = total[pl.ds(lons, 8), :]
     total[pl.ds(lons + 8, 8), :] = total[pl.ds(8, 8), :]
     for block in range(blocks):
@@ -545,7 +549,7 @@
 def member_sums(blocks, kept, taken, field):
     lons, lats = field.shape
     rows = lons // blocks
-    span = 192
+    span = 96
     count = len(kept) + len(taken)
     offsets = np.arange(lats)
     lat_loc = jnp.asarray(taps(np.abs(offsets[:, None] - offsets[None, :])))
@@ -555,11 +559,11 @@
     )
     return pl.pallas_call(
         functools.partial(member_kernel, span, reaches),
-        in_specs=[FAR] * count + [NEAR] * 3,
+        in_specs=[FAR] * len(kept) + [pl.BlockSpec(memory_space=pl.ANY)] * len(taken) + [NEAR] * 3,
         out_shape=shape_of(blocks, rows + 4, lats),
         scratch_shapes=[
             pltpu.VMEM((lons, lats), F32),
-            pltpu.VMEM((lons + 2 * HALF, lats), BF),
+            pltpu.VMEM((lons + 2 * HALF, count * lats), BF),
             pltpu.VMEM((lons + 16, lats), F32),
             pltpu.VMEM((count, lons, lats), BF),
             pltpu.SemaphoreType.DMA((count,)),
@@ -569,7 +573,7 @@
             flops=4_000_000_000, bytes_accessed=6_000_000, transcendentals=0
         ),
         name="members",
-    )(*[remote(value) for value in kept + taken], field, lat_loc, lon_loc)
+    )(*[remote(value) for value in kept], *taken, field, lat_loc, lon_loc)
 
 
 def block_sums(groups, arrived):
@@ -627,6 +631,7 @@
     kept, given = member_planes(core, members)
     taken = [lax.ppermute(give, "space", swap) for give in given]
     slopes = hidden_slopes(core, partner, neighbour, front, state_taps)
+    gathered, slopes = lax.optimization_barrier((gathered, slopes))
     parts = member_sums(blocks, kept, taken, gathered.reshape(lons, lats))
     arrived = [lax.all_to_all(parts, "space", 0, 0, tiled=True)]
     spread = block_sums(groups, arrived)

time: 98.6 us -> 90.6 us (0.919)
  blocking collectives: 26.6 us -> 42.3 us
  Pallas kernels: 32.9 us -> 23 us
  waiting for transfers between devices: 17.9 us -> 11 us
  starting transfers between devices: 18.2 us -> 12.3 us
    all_to_all x0 -> x1, blocking collectives: none -> 15.6 us  [per_device(): copies = lax.all_to_all(spread, 'mem', 0, 0, tiled=True)]
    all_to_all x1 -> x0, starting transfers between devices: 6.06 us -> none  [per_device(): copies = lax.all_to_all(spread, 'mem', 0, 0, tiled=True)]
    all_to_all x1 -> x0, waiting for transfers between devices: 4.37 us -> none  [per_device(): copies = lax.all_to_all(spread, 'mem', 0, 0, tiled=True)]
    ppermute x4, waiting for transfers between devices: 3.72 us -> 0.01 us  [per_device(): taken = [lax.ppermute(give, 'space', swap) for give in given]]
    pallas_call x1, Pallas kernels: 7.31 us -> 4.2 us  [responses(): pl.pallas_call(functools.partial(response_kernel, scale), out_shape=[wide...]
    pallas_call x1, Pallas kernels: 5.92 us -> 3.54 us  [prepare(): pl.pallas_call(prepare_kernel, out_shape=[shape_of(2, hidden, 3 * GROUP),...]
    ppermute x1, starting transfers between devices: 2.29 us -> 0.09 us  [per_device(): neighbour = lax.ppermute(jnp.where(core == 0, head, tail), 'space', chain)]
    ppermute x1, starting transfers between devices: 0.09 us -> 1.91 us  [per_device(): partner = lax.ppermute(jnp.where(core == 0, tail, head), 'space', swap)]
  transfers between devices with their start and end apart: 8 -> 7, of which waited for: 5 -> 1; matrix products, arithmetic and copies ran while one was open for 0% -> 0% of each run, Pallas kernels for 15% -> 12%
where the time goes in v3:
time: 90.6 us; the launch traced here: 90.3 us
  blocking collectives  42.3 us (47%)
  Pallas kernels  23 us (25%)
  starting transfers between devices  12.3 us (14%)
  waiting for transfers between devices  11 us (12%)
  between operations  0.91 us (1%)
    all_to_all x1, blocking collectives, per_device(): arrived = [lax.all_to_all(parts, 'space', 0, 0, tiled=True)]  26.6 us
    all_to_all x1, blocking collectives, per_device(): copies = lax.all_to_all(spread, 'mem', 0, 0, tiled=True)  15.6 us
    all_to_all x1, waiting for transfers between devices, per_device(): gathered = lax.all_to_all(outgoing, 'space', 0, 0, tiled=True)  11 us
    all_to_all x1, starting transfers between devices, per_device(): gathered = lax.all_to_all(outgoing, 'space', 0, 0, tiled=True)  9.18 us
    pallas_call x1, Pallas kernels, member_sums(): pl.pallas_call(functools.partial(member_kernel, span, reaches), in_specs=...  6.59 us
    pallas_call x1, Pallas kernels, responses(): pl.pallas_call(functools.partial(response_kernel, scale), out_shape=[wide...  4.2 us
    pallas_call x1, Pallas kernels, member_planes(): pl.pallas_call(planes_kernel, in_specs=[SCALAR, FAR], out_specs=[FAR] * (...  3.76 us
    pallas_call x1, Pallas kernels, prepare(): pl.pallas_call(prepare_kernel, out_shape=[shape_of(2, hidden, 3 * GROUP),...  3.54 us
  transfers between devices with their start and end apart: 7, of which 1 were waited for; matrix products, arithmetic and copies ran while one was open for 0% of the time, Pallas kernels for 12%

profile of v3, /device:TPU:8, one launch (start us, length us, event | category | flops | bytes accessed | tf_op | source)
XLA Modules:
  0.0 90.3 jit_solution(17465027377874515105)
XLA Ops:
  0.6 0.8 fusion.2
  1.4 0.1 collective-permute-start.1
  1.5 1.9 %collective-permute-start = (f32[2,4,384]{2,1,0:T(4,128)S(1)}, f32[2,4,384]{2,1,0:T(4,128)S(1)}, u32[]{:S(2)}, u32[]{:S(2)}) collective-permute-start(f32[2,4,384]{2,1,0:T(4,128)S(1)} %get-tuple-element.43), channel_id=1, source_target_pairs={{0,8},{8,0},{16,24},{24,16},{32,40},{40,32},{48,56},{56,48},{64,72... | collective-permute-start | bytes 36872 | tf_op jit(solution)/shard_map/ppermute | solution.py:620
  3.4 3.5 %prepare.1 = (bf16[2,128,96]{2,1,0:T(8,128)(2,1)S(1)}, bf16[2,48,256]{2,1,0:T(8,128)(2,1)S(1)}, bf16[768,384]{1,0:T(8,128)(2,1)S(1)}, bf16[768,384]{1,0:T(8,128)...) custom-call(f32[24,2,384]{2,1,0:T(2,128)} %state_far.1, f32[24,2,384]{2,1,0:T(2,128)} %cot_far.1, ...), custom_call_target="tpu_custom_call" | custom-call | flops 2000000000 | bytes 3000000 | tf_op jit(solution)/shard_map/prepare/pallas_call | solution.py:457
  7.0 0.0 collective-permute-done.1.neighbour_ref
  7.0 0.0 collective-permute-done.partner_ref
  7.0 1.6 %gradient.1 = bf16[32,24,384]{2,1,0:T(8,128)(2,1)} custom-call(s32[1]{0:T(128)} %bitcast.core_ref, f32[2,24,384]{2,1,0:T(8,128)S(1)} %get-tuple-element.20.cot_planes, f32[2,4,384]{2,1,0:T(4,128)S(1)} %collective-permute-done.partner_ref, f32[2,4,384]{2,1,0:T(4,128)S(1)} %collective-permute-done.1.neighbour_ref, ...), custom_call_target="tpu_custom_call" | custom-call | flops 400000000 | bytes 1500000 | tf_op jit(solution)/shard_map/gradient/pallas_call | solution.py:491
  8.6 9.2 %all-to-all-start = ((bf16[32,24,384]{2,1,0:T(8,128)(2,1)}), bf16[32,24,384]{2,1,0:T(8,128)(2,1)S(1)}, u32[]{:S(2)}, u32[]{:S(2)}) async-start(bf16[32,24,384]{2,1,0:T(8,128)(2,1)} %gradient.1), calls=%async_computation | async-start | bytes 1179648 | tf_op jit(solution)/shard_map/all_to_all | solution.py:630
  17.8 0.0 copy-start
  17.8 0.0 copy-start.1
  17.8 3.8 %planes.1 = (bf16[768,384]{1,0:T(8,128)(2,1)}, bf16[768,384]{1,0:T(8,128)(2,1)}, bf16[768,384]{1,0:T(8,128)(2,1)}, bf16[768,384]{1,0:T(8,128)(2,1)}, bf16[768,38...) custom-call(s32[1]{0:T(128)} %bitcast.core_ref, ...), custom_call_target="tpu_custom_call" | custom-call | bytes 10000000 | tf_op jit(solution)/shard_map/planes/pallas_call | solution.py:513
  21.6 0.2 collective-permute-start.2
  21.8 0.4 collective-permute-start.3
  22.2 0.1 collective-permute-start.4
  22.3 0.4 collective-permute-start.5
  22.7 3.2 %slopes.1.slopes_far = f32[26,128,384]{2,1,0:T(8,128)} custom-call(s32[1]{0:T(128)} %bitcast.core_ref, f32[2,4,384]{2,1,0:T(4,128)S(1)} %collective-permute-done.partner_ref, f32[2,4,384]{2,1,0:T(4,128)S(1)} %collective-permute-done.1.neighbour_ref, bf16[2,128,96]{2,1,0:T(8,128)(2,1)S(1)} %get-tuple-element.21.front_ref, ...), custom_call_target="tpu_custom_call" | custom-call | flops 1000000000 | bytes 6000000 | tf_op jit(solution)/shard_map/slopes/pallas_call | solution.py:535
  25.9 11.0 %all-to-all-done = bf16[32,24,384]{2,1,0:T(8,128)(2,1)S(1)} async-done(((bf16[32,24,384]{2,1,0:T(8,128)(2,1)}), bf16[32,24,384]{2,1,0:T(8,128)(2,1)S(1)}, u32[]{:S(2)}, u32[]{:S(2)}) %all-to-all-start) | async-done | bytes 589856 | tf_op jit(solution)/shard_map/all_to_all | solution.py:630
  36.9 0.0 collective-permute-done.2.refs_4_
  36.9 0.0 collective-permute-done.3.refs_5_
  36.9 0.0 collective-permute-done.4.refs_6_
  36.9 0.0 collective-permute-done.5.refs_7_
  36.9 0.0 copy-done
  36.9 0.0 copy-done.1
  37.0 6.6 %members.1 = bf16[32,28,384]{2,1,0:T(8,128)(2,1)S(1)} custom-call(bf16[768,384]{1,0:T(8,128)(2,1)} %get-tuple-element.27.refs_0_, bf16[768,384]{1,0:T(8,128)(2,1)} %get-tuple-element.28.refs_1_, bf16[768,384]{1,0:T(8,128)(2,1)} %get-tuple-element.29.refs_2_, bf16[768,384]{1,0:T(8,128)(2,1)} %get-tuple-element.30.refs_3_, ...), custom_call_target="tpu_custom_call" | custom-call | flops 4000000000 | bytes 6000000 | tf_op jit(solution)/shard_map/members/pallas_call | solution.py:560
  43.6 26.6 %all_to_all.15.refs_0_ = bf16[32,28,384]{2,1,0:T(8,128)(2,1)S(1)} all-to-all(bf16[32,28,384]{2,1,0:T(8,128)(2,1)S(1)} %members.1), channel_id=1, replica_groups=mesh['space'=32,'mem'=8] {'space'}, dimensions={0} | all-to-all | bytes 1376256 | tf_op jit(solution)/shard_map/all_to_all | solution.py:636
  70.2 0.1 block_sum.1
  70.3 15.6 %all_to_all.16.copies_ref = bf16[8,56,384]{2,1,0:T(8,128)(2,1)S(1)} all-to-all(bf16[8,56,384]{2,1,0:T(8,128)(2,1)S(1)} %block_sum.1), channel_id=1, replica_groups=mesh['space'=32,'mem'=8] {'mem'}, dimensions={0} | all-to-all | bytes 688128 | tf_op jit(solution)/shard_map/all_to_all | solution.py:638
  85.9 4.2 %response.1 = (f32[24,2,384]{2,1,0:T(2,128)}, f32[24,2,384]{2,1,0:T(2,128)}) custom-call(bf16[8,56,384]{2,1,0:T(8,128)(2,1)S(1)} %all_to_all.16.copies_ref, f32[26,128,384]{2,1,0:T(8,128)} %slopes.1.slopes_far, bf16[2,128,96]{2,1,0:T(8,128)(2,1)S(1)} %get-tuple-element.21.front_ref, bf16[2,48,256]{2,1,0:T(8,128)(2,1)S(1)} %get-tuple-element.22.back_ref), custom_call_target="tpu_custom_call" | custom-call | tf_op jit(solution)/shard_map/response/pallas_call | solution.py:593
  (1 shorter events, 0.0 us)
Async XLA Ops:
  1.4 5.6 %collective-permute-start.1 = (f32[2,4,384]{2,1,0:T(4,128)S(1)}, f32[2,4,384]{2,1,0:T(4,128)S(1)}, u32[]{:S(2)}, u32[]{:S(2)}) collective-permute-start(f32[2,4,384]{2,1,0:T(4,128)S(1)} %get-tuple-element.42), channel_id=1, source_target_pairs={{0,248},{8,16},{16,8},{24,32},{32,24},{40,48},{48,40},{56,64},{64,... | collective-permute-start | bytes 36872 | tf_op jit(solution)/shard_map/ppermute | solution.py:619
  1.5 5.5 %collective-permute-start = (f32[2,4,384]{2,1,0:T(4,128)S(1)}, f32[2,4,384]{2,1,0:T(4,128)S(1)}, u32[]{:S(2)}, u32[]{:S(2)}) collective-permute-start(f32[2,4,384]{2,1,0:T(4,128)S(1)} %get-tuple-element.43), channel_id=1, source_target_pairs={{0,8},{8,0},{16,24},{24,16},{32,40},{40,32},{48,56},{56,48},{64,72... | collective-permute-start | bytes 36872 | tf_op jit(solution)/shard_map/ppermute | solution.py:620
  8.6 28.3 %all-to-all-start = ((bf16[32,24,384]{2,1,0:T(8,128)(2,1)}), bf16[32,24,384]{2,1,0:T(8,128)(2,1)S(1)}, u32[]{:S(2)}, u32[]{:S(2)}) async-start(bf16[32,24,384]{2,1,0:T(8,128)(2,1)} %gradient.1), calls=%async_computation | async-start | bytes 1179648 | tf_op jit(solution)/shard_map/all_to_all | solution.py:630
  17.8 19.1 %copy-start = (bf16[384,384]{1,0:T(8,128)(2,1)S(1)}, bf16[384,384]{1,0:T(8,128)(2,1)}, u32[]{:S(2)}) copy-start(bf16[384,384]{1,0:T(8,128)(2,1)} %constant.24.clone.refs_9_) | copy-start | bytes 884740
  17.8 19.1 %copy-start.1 = (bf16[96,128]{1,0:T(8,128)(2,1)S(1)}, bf16[96,128]{1,0:T(8,128)(2,1)}, u32[]{:S(2)}) copy-start(bf16[96,128]{1,0:T(8,128)(2,1)} %constant.25.clone.refs_10_) | copy-start | bytes 73732
  21.6 15.3 %collective-permute-start.2 = (bf16[768,384]{1,0:T(8,128)(2,1)}, bf16[768,384]{1,0:T(8,128)(2,1)S(1)}, u32[]{:S(2)}, u32[]{:S(2)}) collective-permute-start(bf16[768,384]{1,0:T(8,128)(2,1)} %get-tuple-element.31), channel_id=1, source_target_pairs={{0,8},{8,0},{16,24},{24,16},{32,40},{40,32},{48,56},{56,48},{64,72... | collective-permute-start | bytes 1769480 | tf_op jit(solution)/shard_map/ppermute | solution.py:632
  21.8 15.1 %collective-permute-start.3 = (bf16[768,384]{1,0:T(8,128)(2,1)}, bf16[768,384]{1,0:T(8,128)(2,1)S(1)}, u32[]{:S(2)}, u32[]{:S(2)}) collective-permute-start(bf16[768,384]{1,0:T(8,128)(2,1)} %get-tuple-element.32), channel_id=1, source_target_pairs={{0,8},{8,0},{16,24},{24,16},{32,40},{40,32},{48,56},{56,48},{64,72... | collective-permute-start | bytes 1769480 | tf_op jit(solution)/shard_map/ppermute | solution.py:632
  22.2 14.7 %collective-permute-start.4 = (bf16[768,384]{1,0:T(8,128)(2,1)}, bf16[768,384]{1,0:T(8,128)(2,1)S(1)}, u32[]{:S(2)}, u32[]{:S(2)}) collective-permute-start(bf16[768,384]{1,0:T(8,128)(2,1)} %get-tuple-element.33), channel_id=1, source_target_pairs={{0,8},{8,0},{16,24},{24,16},{32,40},{40,32},{48,56},{56,48},{64,72... | collective-permute-start | bytes 1769480 | tf_op jit(solution)/shard_map/ppermute | solution.py:632
  22.3 14.6 %collective-permute-start.5 = (bf16[768,384]{1,0:T(8,128)(2,1)}, bf16[768,384]{1,0:T(8,128)(2,1)}, u32[]{:S(2)}, u32[]{:S(2)}) collective-permute-start(bf16[768,384]{1,0:T(8,128)(2,1)} %get-tuple-element.34), channel_id=1, source_target_pairs={{0,8},{8,0},{16,24},{24,16},{32,40},{40,32},{48,56},{56,48},{64,72... | collective-permute-start | bytes 1769480 | tf_op jit(solution)/shard_map/ppermute | solution.py:632

commit v4 on v3

--- a/solution.py
+++ b/solution.py
@@ -307,6 +307,7 @@
     product,
     fold,
     slopes_ref,
+    tail,
     semaphores,
 ):
     rows = incr_out.shape[0]
@@ -315,11 +316,28 @@
     copies = fetch([(slopes_far.at[part], slopes_ref.at[part]) for part in halves], semaphores)
     planes = []
     put_ones(wide, 0.0)
+    groups = copies_ref.shape[0]
+    lane = lax.broadcasted_iota(jnp.int32, (rows + 4, 128), 1)
     for var in range(2):
-        window = pl.ds(var * (rows + 4), rows + 4)
-        plane = copies_ref[0, window, :].astype(F32)
-        for group in range(1, copies_ref.shape[0]):
-            plane = plane + copies_ref[group, window, :].astype(F32)
+        fronts, tails = [], []
+        for half_of in range(2):
+            window = pl.ds(var * 48, 48)
+            members = [group for group in range(groups) if (group // 2) % 2 == half_of]
+            value = sum(copies_ref[group, window, :].astype(F32) for group in members)
+            fronts.append(value[0 : rows + 4])
+            packed = value[32:46]
+            tail[pl.ds(0, 14), :] = packed
+            tail[pl.ds(14, 14), :] = pltpu.roll(packed, 64, 1)
+            tails.append(tail[pl.ds(0, rows + 4), :])
+        middle = pltpu.roll(fronts[1], 64, 1)
+        plane = jnp.concatenate(
+            [
+                fronts[0],
+                jnp.where(lane < 64, tails[0], middle),
+                jnp.where(lane < 64, middle, pltpu.roll(tails[1], 64, 1)),
+            ],
+            axis=1,
+        )
         plane = plane * scale
         planes.append(plane)
         put_taps(wide, plane, 0, var)
@@ -369,44 +387,56 @@
         copy.wait()
 
 
-def member_kernel(span, reaches, *refs):
+def member_kernel(span, half_ref, *refs):
     *far_refs, field_ref, lat_ref, lon_ref, out_ref, field, banded, total, held, semaphores = refs
     lons = field_ref.shape[0]
     blocks = out_ref.shape[0]
     rows = lons // blocks
+    wide = 2 * 128
+    half = half_ref[0]
+    reach = pl.ds(pl.multiple_of(half * 128, 128), wide)
     member_refs = [held.at[index] for index in range(len(far_refs))]
-    copies = fetch(zip(far_refs, member_refs), semaphores)
-    field[...] = field_ref[...].astype(F32)
-    lats = field_ref.shape[1]
+    copies = fetch([(far.at[:, reach], near) for far, near in zip(far_refs, member_refs)], semaphores)
+    field[...] = field_ref[:, reach].astype(F32)
+    lat_loc = lat_ref[half]
     chunk = 2 * span
     for index, member_ref in enumerate(member_refs):
         copies[index].wait()
-        at = index * lats
+        at = index * wide
         for start in range(0, lons, chunk):
             window = pl.ds(start, chunk)
             product = (member_ref[window, :].astype(F32) * field[window, :]).astype(BF)
-            for (first, last), (low, high) in reaches:
-                banded[pl.ds(HALF + start, chunk), at + first : at + last] = jnp.dot(
-                    product[:, low:high], lat_ref[low:high, first:last], preferred_element_type=F32
-                ).astype(BF)
+            banded[pl.ds(HALF + start, chunk), at : at + wide] = jnp.dot(
+                product, lat_loc, preferred_element_type=F32
+            ).astype(BF)
     banded[pl.ds(0, HALF), :] = banded[pl.ds(lons, HALF), :]
     banded[pl.ds(HALF + lons, HALF), :] = banded[pl.ds(HALF, HALF), :]
     for start in range(0, lons, span):
         value = None
         for index, member_ref in enumerate(member_refs):
-            at = index * lats
+            at = index * wide
             spread = jnp.dot(
                 lon_ref[...],
-                banded[pl.ds(start, span + 2 * HALF), at : at + lats],
+                banded[pl.ds(start, span + 2 * HALF), at : at + wide],
                 preferred_element_type=F32,
             )
             term = member_ref[pl.ds(start, span), :].astype(F32) * spread
             value = term if value is None else value + term
-        total[pl.ds(8 + start, span), :] = value
+        total[pl.ds(8 + start, span), :] = jnp.where(half == 0, value, pltpu.roll(value, 192, 1))
     total[pl.ds(0, 8), :] = total[pl.ds(lons, 8), :]
     total[pl.ds(lons + 8, 8), :] = total[pl.ds(8, 8), :]
+    lane = lax.broadcasted_iota(jnp.int32, (16, 128), 1)
     for block in range(blocks):
-        out_ref[block] = total[pl.ds(6 + block * rows, rows + 4), :].astype(BF)
+        top = 6 + block * rows
+        out_ref[block, 0:32, :] = total[pl.ds(top, 32), 0:128].astype(out_ref.dtype)
+        near = total[pl.ds(top, 16), 128:256]
+        next_rows = total[pl.ds(top + 14, 16), 128:256]
+        packed = jnp.where(lane < 64, near, pltpu.roll(next_rows, 64, 1))
+        out_ref[block, 32:48, :] = packed.astype(out_ref.dtype)
+
+
+def add_kernel(own_ref, other_ref, out_ref):
+    out_ref[...] = (own_ref[...] + other_ref[...].astype(F32)).astype(BF)
 
 
 def sum_kernel(*refs):
@@ -546,34 +576,54 @@
     )(core, partner, neighbour, front, state_taps)
 
 
-def member_sums(blocks, kept, taken, field):
-    lons, lats = field.shape
-    rows = lons // blocks
+def member_sums(blocks, half, kept, taken, field, kind):
+    lons = field.shape[0]
     span = 96
     count = len(kept) + len(taken)
-    offsets = np.arange(lats)
-    lat_loc = jnp.asarray(taps(np.abs(offsets[:, None] - offsets[None, :])))
-    reaches = (((0, 256), (0, 384)), ((256, 384), (128, 384)))
+    wide = 2 * 128
+    offsets = np.arange(wide)
+    lat_band = taps(np.abs(offsets[:, None] - offsets[None, :]))
+    zero = np.zeros_like(lat_band)
+    lat_loc = jnp.asarray(
+        np.stack(
+            [
+                np.where(offsets[None, :] < 192, lat_band, zero),
+                np.where(offsets[None, :] >= 64, lat_band, zero),
+            ]
+        )
+    )
     lon_loc = jnp.asarray(
         taps(np.abs(np.arange(span)[:, None] + HALF - np.arange(span + 2 * HALF)[None, :]))
     )
     return pl.pallas_call(
-        functools.partial(member_kernel, span, reaches),
-        in_specs=[FAR] * len(kept) + [pl.BlockSpec(memory_space=pl.ANY)] * len(taken) + [NEAR] * 3,
-        out_shape=shape_of(blocks, rows + 4, lats),
+        functools.partial(member_kernel, span),
+        in_specs=[SCALAR]
+        + [FAR] * len(kept)
+        + [pl.BlockSpec(memory_space=pl.ANY)] * len(taken)
+        + [NEAR] * 3,
+        out_shape=jax.ShapeDtypeStruct((blocks, 48, 128), kind),
         scratch_shapes=[
-            pltpu.VMEM((lons, lats), F32),
-            pltpu.VMEM((lons + 2 * HALF, count * lats), BF),
-            pltpu.VMEM((lons + 16, lats), F32),
-            pltpu.VMEM((count, lons, lats), BF),
+            pltpu.VMEM((lons, wide), F32),
+            pltpu.VMEM((lons + 2 * HALF, count * wide), BF),
+            pltpu.VMEM((lons + 16, wide), F32),
+            pltpu.VMEM((count, lons, wide), BF),
             pltpu.SemaphoreType.DMA((count,)),
         ],
         compiler_params=PARAMS,
         cost_estimate=pl.CostEstimate(
-            flops=4_000_000_000, bytes_accessed=6_000_000, transcendentals=0
+            flops=2_000_000_000, bytes_accessed=4_000_000, transcendentals=0
         ),
         name="members",
-    )(*[remote(value) for value in kept], *taken, field, lat_loc, lon_loc)
+    )(half, *[remote(value) for value in kept], *taken, field, lat_loc, lon_loc)
+
+
+def add_parts(own, other):
+    return pl.pallas_call(
+        add_kernel,
+        out_shape=jax.ShapeDtypeStruct(own.shape, BF),
+        compiler_params=PARAMS,
+        name="add_parts",
+    )(own, other)
 
 
 def block_sums(groups, arrived):
@@ -588,7 +638,7 @@
 
 
 def responses(scale, copies, slopes, front, back):
-    rows = copies.shape[1] // 2 - 4
+    rows = slopes.shape[0] - 2
     hidden, lats = slopes.shape[1:]
     return pl.pallas_call(
         functools.partial(response_kernel, scale),
@@ -600,6 +650,7 @@
             pltpu.VMEM((3, (rows + 2) * 8, lats), F32),
             padded_scratch(rows + 2, lats),
             pltpu.VMEM((rows + 2, hidden, lats), F32),
+            pltpu.VMEM((32, 128), F32),
             pltpu.SemaphoreType.DMA((2,)),
         ],
         compiler_params=PARAMS,
@@ -632,8 +683,14 @@
     taken = [lax.ppermute(give, "space", swap) for give in given]
     slopes = hidden_slopes(core, partner, neighbour, front, state_taps)
     gathered, slopes = lax.optimization_barrier((gathered, slopes))
-    parts = member_sums(blocks, kept, taken, gathered.reshape(lons, lats))
-    arrived = [lax.all_to_all(parts, "space", 0, 0, tiled=True)]
+    half = (lax.axis_index("mem") // 2) % 2
+    half = half.reshape(1)
+    field = gathered.reshape(lons, lats)
+    theirs = member_sums(blocks, 1 - half, kept, taken, field, BF)
+    theirs, field = lax.optimization_barrier((theirs, field))
+    other = lax.ppermute(theirs, "mem", [(i, i ^ 2) for i in range(groups)])
+    own = member_sums(blocks, half, kept, taken, field, F32)
+    arrived = [lax.all_to_all(add_parts(own, other), "space", 0, 0, tiled=True)]
     spread = block_sums(groups, arrived)
     copies = lax.all_to_all(spread, "mem", 0, 0, tiled=True)
     member_count = held * blocks * groups

time: 90.6 us -> 90.1 us (level)
  blocking collectives: 42.3 us -> 32.6 us
  waiting for transfers between devices: 11 us -> 15.7 us
  Pallas kernels: 23 us -> 25.9 us
  starting transfers between devices: 12.3 us -> 13.9 us
    all_to_all x1, blocking collectives: 26.6 us -> 18.3 us  [per_device(): arrived = [lax.all_to_all(add_parts(own, other), 'space', 0, 0, tiled=True)]]
    ppermute x0 -> x1, waiting for transfers between devices: none -> 4.67 us  [per_device(): other = lax.ppermute(theirs, 'mem', [(i, i ^ 2) for i in range(groups)])]
    pallas_call x1 -> x3, Pallas kernels: 6.59 us -> 9.17 us  [the longest x2 9.08 us: member_sums(): pl.pallas_call(functools.partial(member_kernel, span), in_specs=[SCALAR]...]
    ppermute x0 -> x1, starting transfers between devices: none -> 1.58 us  [per_device(): other = lax.ppermute(theirs, 'mem', [(i, i ^ 2) for i in range(groups)])]
    all_to_all x1, blocking collectives: 15.6 us -> 14.3 us  [per_device(): copies = lax.all_to_all(spread, 'mem', 0, 0, tiled=True)]
  transfers between devices with their start and end apart: 7 -> 8, of which waited for: 1 -> 2; matrix products, arithmetic and copies ran while one was open for 0% -> 0% of each run, Pallas kernels for 12% -> 17%
where the time goes in v4:
time: 90.1 us; the launch traced here: 89.7 us
  blocking collectives  32.6 us (36%)
  Pallas kernels  25.9 us (29%)
  waiting for transfers between devices  15.7 us (17%)
  starting transfers between devices  13.9 us (15%)
  between operations  0.93 us (1%)
    all_to_all x1, blocking collectives, per_device(): arrived = [lax.all_to_all(add_parts(own, other), 'space', 0, 0, tiled=True)]  18.3 us
    all_to_all x1, blocking collectives, per_device(): copies = lax.all_to_all(spread, 'mem', 0, 0, tiled=True)  14.3 us
    all_to_all x1, waiting for transfers between devices, per_device(): gathered = lax.all_to_all(outgoing, 'space', 0, 0, tiled=True)  11 us
    all_to_all x1, starting transfers between devices, per_device(): gathered = lax.all_to_all(outgoing, 'space', 0, 0, tiled=True)  9.19 us
    pallas_call x2, Pallas kernels, member_sums(): pl.pallas_call(functools.partial(member_kernel, span), in_specs=[SCALAR]...  9.08 us
    ppermute x1, waiting for transfers between devices, per_device(): other = lax.ppermute(theirs, 'mem', [(i, i ^ 2) for i in range(groups)])  4.67 us
    pallas_call x1, Pallas kernels, responses(): pl.pallas_call(functools.partial(response_kernel, scale), out_shape=[wide...  4.49 us
    pallas_call x1, Pallas kernels, member_planes(): pl.pallas_call(planes_kernel, in_specs=[SCALAR, FAR], out_specs=[FAR] * (...  3.76 us
  transfers between devices with their start and end apart: 8, of which 2 were waited for; matrix products, arithmetic and copies ran while one was open for 0% of the time, Pallas kernels for 17%

profile of v4, /device:TPU:8, one launch (start us, length us, event | category | flops | bytes accessed | tf_op | source)
XLA Modules:
  0.0 89.7 jit_solution(884072724370949905)
XLA Ops:
  0.6 0.8 fusion.2
  1.4 0.1 collective-permute-start.1
  1.5 1.9 %collective-permute-start = (f32[2,4,384]{2,1,0:T(4,128)S(1)}, f32[2,4,384]{2,1,0:T(4,128)S(1)}, u32[]{:S(2)}, u32[]{:S(2)}) collective-permute-start(f32[2,4,384]{2,1,0:T(4,128)S(1)} %get-tuple-element.47), channel_id=1, source_target_pairs={{0,8},{8,0},{16,24},{24,16},{32,40},{40,32},{48,56},{56,48},{64,72... | collective-permute-start | bytes 36872 | tf_op jit(solution)/shard_map/ppermute | solution.py:671
  3.4 3.5 %prepare.1 = (bf16[2,128,96]{2,1,0:T(8,128)(2,1)S(1)}, bf16[2,48,256]{2,1,0:T(8,128)(2,1)S(1)}, bf16[768,384]{1,0:T(8,128)(2,1)S(1)}, bf16[768,384]{1,0:T(8,128)...) custom-call(f32[24,2,384]{2,1,0:T(2,128)} %state_far.1, f32[24,2,384]{2,1,0:T(2,128)} %cot_far.1, ...), custom_call_target="tpu_custom_call" | custom-call | flops 2000000000 | bytes 3000000 | tf_op jit(solution)/shard_map/prepare/pallas_call | solution.py:487
  7.0 0.0 collective-permute-done.1.neighbour_ref
  7.0 0.0 collective-permute-done.partner_ref
  7.0 1.6 %gradient.1 = bf16[32,24,384]{2,1,0:T(8,128)(2,1)} custom-call(s32[1]{0:T(128)} %bitcast.1.core_ref, f32[2,24,384]{2,1,0:T(8,128)S(1)} %get-tuple-element.22.cot_planes, f32[2,4,384]{2,1,0:T(4,128)S(1)} %collective-permute-done.partner_ref, f32[2,4,384]{2,1,0:T(4,128)S(1)} %collective-permute-done.1.neighbour_ref, ...), custom_call_target="tpu_custom_call" | custom-call | flops 400000000 | bytes 1500000 | tf_op jit(solution)/shard_map/gradient/pallas_call | solution.py:521
  8.6 9.2 %all-to-all-start = ((bf16[32,24,384]{2,1,0:T(8,128)(2,1)}), bf16[32,24,384]{2,1,0:T(8,128)(2,1)S(1)}, u32[]{:S(2)}, u32[]{:S(2)}) async-start(bf16[32,24,384]{2,1,0:T(8,128)(2,1)} %gradient.1), calls=%async_computation | async-start | bytes 1179648 | tf_op jit(solution)/shard_map/all_to_all | solution.py:681
  17.8 0.0 copy-start
  17.8 0.0 copy-start.1
  17.8 3.8 %planes.1 = (bf16[768,384]{1,0:T(8,128)(2,1)}, bf16[768,384]{1,0:T(8,128)(2,1)}, bf16[768,384]{1,0:T(8,128)(2,1)}, bf16[768,384]{1,0:T(8,128)(2,1)}, bf16[768,38...) custom-call(s32[1]{0:T(128)} %bitcast.1.core_ref, ...), custom_call_target="tpu_custom_call" | custom-call | bytes 10000000 | tf_op jit(solution)/shard_map/planes/pallas_call | solution.py:543
  21.6 0.2 collective-permute-start.2
  21.8 0.4 collective-permute-start.3
  22.2 0.1 collective-permute-start.4
  22.3 0.4 collective-permute-start.5
  22.7 3.2 %slopes.1.slopes_far = f32[26,128,384]{2,1,0:T(8,128)} custom-call(s32[1]{0:T(128)} %bitcast.1.core_ref, f32[2,4,384]{2,1,0:T(4,128)S(1)} %collective-permute-done.partner_ref, f32[2,4,384]{2,1,0:T(4,128)S(1)} %collective-permute-done.1.neighbour_ref, bf16[2,128,96]{2,1,0:T(8,128)(2,1)S(1)} %get-tuple-element.23.front_ref, ...), custom_call_target="tpu_custom_call" | custom-call | flops 1000000000 | bytes 6000000 | tf_op jit(solution)/shard_map/slopes/pallas_call | solution.py:565
  25.9 11.0 %all-to-all-done = bf16[32,24,384]{2,1,0:T(8,128)(2,1)S(1)} async-done(((bf16[32,24,384]{2,1,0:T(8,128)(2,1)}), bf16[32,24,384]{2,1,0:T(8,128)(2,1)S(1)}, u32[]{:S(2)}, u32[]{:S(2)}) %all-to-all-start) | async-done | bytes 589856 | tf_op jit(solution)/shard_map/all_to_all | solution.py:681
  36.9 0.0 collective-permute-done.2.refs_4_
  36.9 0.0 collective-permute-done.3.refs_5_
  36.9 0.0 collective-permute-done.4.refs_6_
  36.9 0.0 collective-permute-done.5.refs_7_
  36.9 0.0 copy-done
  36.9 0.0 copy-done.1
  37.0 4.6 %members.2 = bf16[32,48,128]{2,1,0:T(8,128)(2,1)S(1)} custom-call(s32[1]{0:T(128)S(6)} %sub.8.half_ref, bf16[768,384]{1,0:T(8,128)(2,1)} %get-tuple-element.29.refs_0_, bf16[768,384]{1,0:T(8,128)(2,1)} %get-tuple-element.30.refs_1_, bf16[768,384]{1,0:T(8,128)(2,1)} %get-tuple-element.31.refs_2_, bf16[768,384]{1,0:T(8,128)(2,1)} %get-tuple-element.32.refs_3_, ...), custom_call_target="tpu_custom_call" | custom-call | flops 2000000000 | bytes 4000000 | tf_op jit(solution)/shard_map/members/pallas_call | solution.py:598
  41.6 1.6 %collective-permute-start.6 = (bf16[32,48,128]{2,1,0:T(8,128)(2,1)S(1)}, bf16[32,48,128]{2,1,0:T(8,128)(2,1)S(1)}, u32[]{:S(2)}, u32[]{:S(2)}) collective-permute-start(bf16[32,48,128]{2,1,0:T(8,128)(2,1)S(1)} %members.2), channel_id=1, source_target_pairs={{0,2},{1,3},{2,0},{3,1},{4,6},{5,7},{6,4},{7,5},{8,10},{9,11},{10,... | collective-permute-start | bytes 1179656 | tf_op jit(solution)/shard_map/ppermute | solution.py:691
  43.2 4.5 %members.3.own_ref = f32[32,48,128]{2,1,0:T(8,128)S(1)} custom-call(s32[1]{0:T(128)} %bitcast.half_ref, bf16[768,384]{1,0:T(8,128)(2,1)} %get-tuple-element.29.refs_0_, bf16[768,384]{1,0:T(8,128)(2,1)} %get-tuple-element.30.refs_1_, bf16[768,384]{1,0:T(8,128)(2,1)} %get-tuple-element.31.refs_2_, bf16[768,384]{1,0:T(8,128)(2,1)} %get-tuple-element.32.refs_3_, ...), custom_call_target="tpu_custom_call" | custom-call | flops 2000000000 | bytes 4000000 | tf_op jit(solution)/shard_map/members/pallas_call | solution.py:598
  47.6 4.7 %collective-permute-done.6.other_ref = bf16[32,48,128]{2,1,0:T(8,128)(2,1)S(1)} collective-permute-done((bf16[32,48,128]{2,1,0:T(8,128)(2,1)S(1)}, bf16[32,48,128]{2,1,0:T(8,128)(2,1)S(1)}, u32[]{:S(2)}, u32[]{:S(2)}) %collective-permute-start.6) | collective-permute-done | bytes 393248 | tf_op jit(solution)/shard_map/ppermute | solution.py:691
  52.3 0.1 add_parts.1
  52.4 18.3 %all_to_all.15.refs_0_ = bf16[32,48,128]{2,1,0:T(8,128)(2,1)S(1)} all-to-all(bf16[32,48,128]{2,1,0:T(8,128)(2,1)S(1)} %add_parts.1), channel_id=1, replica_groups=mesh['space'=32,'mem'=8] {'space'}, dimensions={0} | all-to-all | bytes 786432 | tf_op jit(solution)/shard_map/all_to_all | solution.py:693
  70.7 0.1 block_sum.1
  70.8 14.3 %all_to_all.16.copies_ref = bf16[8,96,128]{2,1,0:T(8,128)(2,1)S(1)} all-to-all(bf16[8,96,128]{2,1,0:T(8,128)(2,1)S(1)} %block_sum.1), channel_id=1, replica_groups=mesh['space'=32,'mem'=8] {'mem'}, dimensions={0} | all-to-all | bytes 393216 | tf_op jit(solution)/shard_map/all_to_all | solution.py:695
  85.1 4.5 %response.1 = (f32[24,2,384]{2,1,0:T(2,128)}, f32[24,2,384]{2,1,0:T(2,128)}) custom-call(bf16[8,96,128]{2,1,0:T(8,128)(2,1)S(1)} %all_to_all.16.copies_ref, f32[26,128,384]{2,1,0:T(8,128)} %slopes.1.slopes_far, bf16[2,128,96]{2,1,0:T(8,128)(2,1)S(1)} %get-tuple-element.23.front_ref, bf16[2,48,256]{2,1,0:T(8,128)(2,1)S(1)} %get-tuple-element.24.back_ref), custom_call_target="tpu_custom_call" | custom-call | tf_op jit(solution)/shard_map/response/pallas_call | solution.py:643
  (1 shorter events, 0.0 us)
Async XLA Ops:
  1.4 5.6 %collective-permute-start.1 = (f32[2,4,384]{2,1,0:T(4,128)S(1)}, f32[2,4,384]{2,1,0:T(4,128)S(1)}, u32[]{:S(2)}, u32[]{:S(2)}) collective-permute-start(f32[2,4,384]{2,1,0:T(4,128)S(1)} %get-tuple-element.46), channel_id=1, source_target_pairs={{0,248},{8,16},{16,8},{24,32},{32,24},{40,48},{48,40},{56,64},{64,... | collective-permute-start | bytes 36872 | tf_op jit(solution)/shard_map/ppermute | solution.py:670
  1.5 5.5 %collective-permute-start = (f32[2,4,384]{2,1,0:T(4,128)S(1)}, f32[2,4,384]{2,1,0:T(4,128)S(1)}, u32[]{:S(2)}, u32[]{:S(2)}) collective-permute-start(f32[2,4,384]{2,1,0:T(4,128)S(1)} %get-tuple-element.47), channel_id=1, source_target_pairs={{0,8},{8,0},{16,24},{24,16},{32,40},{40,32},{48,56},{56,48},{64,72... | collective-permute-start | bytes 36872 | tf_op jit(solution)/shard_map/ppermute | solution.py:671
  8.6 28.3 %all-to-all-start = ((bf16[32,24,384]{2,1,0:T(8,128)(2,1)}), bf16[32,24,384]{2,1,0:T(8,128)(2,1)S(1)}, u32[]{:S(2)}, u32[]{:S(2)}) async-start(bf16[32,24,384]{2,1,0:T(8,128)(2,1)} %gradient.1), calls=%async_computation | async-start | bytes 1179648 | tf_op jit(solution)/shard_map/all_to_all | solution.py:681
  17.8 19.1 %copy-start = (bf16[2,256,256]{2,1,0:T(8,128)(2,1)S(1)}, bf16[2,256,256]{2,1,0:T(8,128)(2,1)}, u32[]{:S(2)}) copy-start(bf16[2,256,256]{2,1,0:T(8,128)(2,1)} %constant.44.clone.refs_9_) | copy-start | bytes 786436
  17.8 19.1 %copy-start.1 = (bf16[96,128]{1,0:T(8,128)(2,1)S(1)}, bf16[96,128]{1,0:T(8,128)(2,1)}, u32[]{:S(2)}) copy-start(bf16[96,128]{1,0:T(8,128)(2,1)} %constant.45.clone.refs_10_) | copy-start | bytes 73732
  21.6 15.3 %collective-permute-start.2 = (bf16[768,384]{1,0:T(8,128)(2,1)}, bf16[768,384]{1,0:T(8,128)(2,1)S(1)}, u32[]{:S(2)}, u32[]{:S(2)}) collective-permute-start(bf16[768,384]{1,0:T(8,128)(2,1)} %get-tuple-element.33), channel_id=1, source_target_pairs={{0,8},{8,0},{16,24},{24,16},{32,40},{40,32},{48,56},{56,48},{64,72... | collective-permute-start | bytes 1769480 | tf_op jit(solution)/shard_map/ppermute | solution.py:683
  21.8 15.1 %collective-permute-start.3 = (bf16[768,384]{1,0:T(8,128)(2,1)}, bf16[768,384]{1,0:T(8,128)(2,1)S(1)}, u32[]{:S(2)}, u32[]{:S(2)}) collective-permute-start(bf16[768,384]{1,0:T(8,128)(2,1)} %get-tuple-element.34), channel_id=1, source_target_pairs={{0,8},{8,0},{16,24},{24,16},{32,40},{40,32},{48,56},{56,48},{64,72... | collective-permute-start | bytes 1769480 | tf_op jit(solution)/shard_map/ppermute | solution.py:683
  22.2 14.7 %collective-permute-start.4 = (bf16[768,384]{1,0:T(8,128)(2,1)}, bf16[768,384]{1,0:T(8,128)(2,1)S(1)}, u32[]{:S(2)}, u32[]{:S(2)}) collective-permute-start(bf16[768,384]{1,0:T(8,128)(2,1)} %get-tuple-element.35), channel_id=1, source_target_pairs={{0,8},{8,0},{16,24},{24,16},{32,40},{40,32},{48,56},{56,48},{64,72... | collective-permute-start | bytes 1769480 | tf_op jit(solution)/shard_map/ppermute | solution.py:683
  22.3 14.6 %collective-permute-start.5 = (bf16[768,384]{1,0:T(8,128)(2,1)}, bf16[768,384]{1,0:T(8,128)(2,1)}, u32[]{:S(2)}, u32[]{:S(2)}) collective-permute-start(bf16[768,384]{1,0:T(8,128)(2,1)} %get-tuple-element.36), channel_id=1, source_target_pairs={{0,8},{8,0},{16,24},{24,16},{32,40},{40,32},{48,56},{56,48},{64,72... | collective-permute-start | bytes 1769480 | tf_op jit(solution)/shard_map/ppermute | solution.py:683
  41.6 10.7 %collective-permute-start.6 = (bf16[32,48,128]{2,1,0:T(8,128)(2,1)S(1)}, bf16[32,48,128]{2,1,0:T(8,128)(2,1)S(1)}, u32[]{:S(2)}, u32[]{:S(2)}) collective-permute-start(bf16[32,48,128]{2,1,0:T(8,128)(2,1)S(1)} %members.2), channel_id=1, source_target_pairs={{0,2},{1,3},{2,0},{3,1},{4,6},{5,7},{6,4},{7,5},{8,10},{9,11},{10,... | collective-permute-start | bytes 1179656 | tf_op jit(solution)/shard_map/ppermute | solution.py:691

commit v5 on v4

--- a/solution.py
+++ b/solution.py
@@ -307,7 +307,6 @@
     product,
     fold,
     slopes_ref,
-    tail,
     semaphores,
 ):
     rows = incr_out.shape[0]
@@ -317,27 +316,16 @@
     planes = []
     put_ones(wide, 0.0)
     groups = copies_ref.shape[0]
-    lane = lax.broadcasted_iota(jnp.int32, (rows + 4, 128), 1)
+    lines = rows + 4
     for var in range(2):
-        fronts, tails = [], []
-        for half_of in range(2):
-            window = pl.ds(var * 48, 48)
-            members = [group for group in range(groups) if (group // 2) % 2 == half_of]
-            value = sum(copies_ref[group, window, :].astype(F32) for group in members)
-            fronts.append(value[0 : rows + 4])
-            packed = value[32:46]
-            tail[pl.ds(0, 14), :] = packed
-            tail[pl.ds(14, 14), :] = pltpu.roll(packed, 64, 1)
-            tails.append(tail[pl.ds(0, rows + 4), :])
-        middle = pltpu.roll(fronts[1], 64, 1)
-        plane = jnp.concatenate(
-            [
-                fronts[0],
-                jnp.where(lane < 64, tails[0], middle),
-                jnp.where(lane < 64, middle, pltpu.roll(tails[1], 64, 1)),
-            ],
-            axis=1,
-        )
+        values = [
+            copies_ref[group, pl.ds(2 * var * lines, 2 * lines), :].astype(F32)
+            for group in range(groups)
+        ]
+        lower = sum(value for group, value in enumerate(values) if (group // 2) % 2 == 0)
+        upper = sum(value for group, value in enumerate(values) if (group // 2) % 2 == 1)
+        middle = (lower + upper)[lines:]
+        plane = jnp.concatenate([lower[:lines], middle, upper[:lines]], axis=1)
         plane = plane * scale
         planes.append(plane)
         put_taps(wide, plane, 0, var)
@@ -392,12 +380,17 @@
     lons = field_ref.shape[0]
     blocks = out_ref.shape[0]
     rows = lons // blocks
-    wide = 2 * 128
+    reach, wide = lat_ref.shape[1:]
     half = half_ref[0]
-    reach = pl.ds(pl.multiple_of(half * 128, 128), wide)
+    offset = pl.multiple_of(half * 128, 128)
+    if reach < field_ref.shape[1]:
+        source = pl.ds(offset, reach)
+    else:
+        source = pl.ds(0, reach)
+    target = pl.ds(offset, wide)
     member_refs = [held.at[index] for index in range(len(far_refs))]
-    copies = fetch([(far.at[:, reach], near) for far, near in zip(far_refs, member_refs)], semaphores)
-    field[...] = field_ref[:, reach].astype(F32)
+    copies = fetch([(far.at[:, source], near) for far, near in zip(far_refs, member_refs)], semaphores)
+    field[...] = field_ref[:, source].astype(F32)
     lat_loc = lat_ref[half]
     chunk = 2 * span
     for index, member_ref in enumerate(member_refs):
@@ -420,23 +413,28 @@
                 banded[pl.ds(start, span + 2 * HALF), at : at + wide],
                 preferred_element_type=F32,
             )
-            term = member_ref[pl.ds(start, span), :].astype(F32) * spread
+            term = member_ref[pl.ds(start, span), target].astype(F32) * spread
             value = term if value is None else value + term
-        total[pl.ds(8 + start, span), :] = jnp.where(half == 0, value, pltpu.roll(value, 192, 1))
+        if wide > 128:
+            value = jnp.where(half == 0, value, pltpu.roll(value, 128, 1))
+        total[pl.ds(8 + start, span), :] = value
     total[pl.ds(0, 8), :] = total[pl.ds(lons, 8), :]
     total[pl.ds(lons + 8, 8), :] = total[pl.ds(8, 8), :]
-    lane = lax.broadcasted_iota(jnp.int32, (16, 128), 1)
+    row = lax.broadcasted_iota(jnp.int32, (32, 128), 0)
     for block in range(blocks):
         top = 6 + block * rows
-        out_ref[block, 0:32, :] = total[pl.ds(top, 32), 0:128].astype(out_ref.dtype)
-        near = total[pl.ds(top, 16), 128:256]
-        next_rows = total[pl.ds(top + 14, 16), 128:256]
-        packed = jnp.where(lane < 64, near, pltpu.roll(next_rows, 64, 1))
-        out_ref[block, 32:48, :] = packed.astype(out_ref.dtype)
+        if wide > 128:
+            out_ref[block, pl.ds(0, rows + 4), :] = total[pl.ds(top, rows + 4), 0:128]
+            out_ref[block, pl.ds(rows + 4, rows + 4), :] = total[pl.ds(top, rows + 4), 128:256]
+        else:
+            value = jnp.where(row < rows + 4, total[pl.ds(top, 32), :], 0.0)
+            out_ref[block] = value.astype(BF)
 
 
 def add_kernel(own_ref, other_ref, out_ref):
-    out_ref[...] = (own_ref[...] + other_ref[...].astype(F32)).astype(BF)
+    for block in range(own_ref.shape[0]):
+        outer = own_ref[block, 0:32, :] + other_ref[block].astype(F32)
+        out_ref[block] = jnp.concatenate([outer, own_ref[block, 32:, :]], axis=0).astype(BF)
 
 
 def sum_kernel(*refs):
@@ -576,42 +574,37 @@
     )(core, partner, neighbour, front, state_taps)
 
 
-def member_sums(blocks, half, kept, taken, field, kind):
-    lons = field.shape[0]
+def member_sums(blocks, half, kept, taken, field, wide):
+    lons, lats = field.shape
+    rows = lons // blocks
     span = 96
     count = len(kept) + len(taken)
-    wide = 2 * 128
-    offsets = np.arange(wide)
-    lat_band = taps(np.abs(offsets[:, None] - offsets[None, :]))
-    zero = np.zeros_like(lat_band)
+    reach = 256 if wide == 128 else lats
+    source, target = np.arange(reach), np.arange(wide)
     lat_loc = jnp.asarray(
-        np.stack(
-            [
-                np.where(offsets[None, :] < 192, lat_band, zero),
-                np.where(offsets[None, :] >= 64, lat_band, zero),
-            ]
-        )
+        np.stack([taps(np.abs(source[:, None] - 128 * at - target[None, :])) for at in range(2)])
     )
     lon_loc = jnp.asarray(
         taps(np.abs(np.arange(span)[:, None] + HALF - np.arange(span + 2 * HALF)[None, :]))
     )
+    out_shape = shape_of(blocks, 32, 128) if wide == 128 else wide_of(blocks, 2 * (rows + 4), 128)
     return pl.pallas_call(
         functools.partial(member_kernel, span),
         in_specs=[SCALAR]
         + [FAR] * len(kept)
         + [pl.BlockSpec(memory_space=pl.ANY)] * len(taken)
         + [NEAR] * 3,
-        out_shape=jax.ShapeDtypeStruct((blocks, 48, 128), kind),
+        out_shape=out_shape,
         scratch_shapes=[
-            pltpu.VMEM((lons, wide), F32),
+            pltpu.VMEM((lons, reach), F32),
             pltpu.VMEM((lons + 2 * HALF, count * wide), BF),
             pltpu.VMEM((lons + 16, wide), F32),
-            pltpu.VMEM((count, lons, wide), BF),
+            pltpu.VMEM((count, lons, reach), BF),
             pltpu.SemaphoreType.DMA((count,)),
         ],
         compiler_params=PARAMS,
         cost_estimate=pl.CostEstimate(
-            flops=2_000_000_000, bytes_accessed=4_000_000, transcendentals=0
+            flops=wide * 16_000_000, bytes_accessed=4_000_000, transcendentals=0
         ),
         name="members",
     )(half, *[remote(value) for value in kept], *taken, field, lat_loc, lon_loc)
@@ -620,7 +613,7 @@
 def add_parts(own, other):
     return pl.pallas_call(
         add_kernel,
-        out_shape=jax.ShapeDtypeStruct(own.shape, BF),
+        out_shape=shape_of(*own.shape),
         compiler_params=PARAMS,
         name="add_parts",
     )(own, other)
@@ -650,7 +643,6 @@
             pltpu.VMEM((3, (rows + 2) * 8, lats), F32),
             padded_scratch(rows + 2, lats),
             pltpu.VMEM((rows + 2, hidden, lats), F32),
-            pltpu.VMEM((32, 128), F32),
             pltpu.SemaphoreType.DMA((2,)),
         ],
         compiler_params=PARAMS,
@@ -686,10 +678,10 @@
     half = (lax.axis_index("mem") // 2) % 2
     half = half.reshape(1)
     field = gathered.reshape(lons, lats)
-    theirs = member_sums(blocks, 1 - half, kept, taken, field, BF)
+    theirs = member_sums(blocks, 1 - half, kept, taken, field, 128)
     theirs, field = lax.optimization_barrier((theirs, field))
     other = lax.ppermute(theirs, "mem", [(i, i ^ 2) for i in range(groups)])
-    own = member_sums(blocks, half, kept, taken, field, F32)
+    own = member_sums(blocks, half, kept, taken, field, 256)
     arrived = [lax.all_to_all(add_parts(own, other), "space", 0, 0, tiled=True)]
     spread = block_sums(groups, arrived)
     copies = lax.all_to_all(spread, "mem", 0, 0, tiled=True)

time: 90.1 us -> 88.4 us (0.981)
  waiting for transfers between devices: 15.7 us -> 12.1 us
  blocking collectives: 32.6 us -> 34.2 us
    ppermute x1, waiting for transfers between devices: 4.67 us -> 1.09 us  [per_device(): other = lax.ppermute(theirs, 'mem', [(i, i ^ 2) for i in range(groups)])]
    all_to_all x1, blocking collectives: 18.3 us -> 19.8 us  [per_device(): arrived = [lax.all_to_all(add_parts(own, other), 'space', 0, 0, tiled=True)]]
  transfers between devices with their start and end apart: 8 -> 8, of which waited for: 2 -> 2; matrix products, arithmetic and copies ran while one was open for 0% -> 0% of each run, Pallas kernels for 17% -> 18%
where the time goes in v5:
time: 88.4 us; the launch traced here: 88 us
  blocking collectives  34.2 us (39%)
  Pallas kernels  26 us (29%)
  starting transfers between devices  14 us (16%)
  waiting for transfers between devices  12.1 us (14%)
  between operations  0.93 us (1%)
    all_to_all x1, blocking collectives, per_device(): arrived = [lax.all_to_all(add_parts(own, other), 'space', 0, 0, tiled=True)]  19.8 us
    all_to_all x1, blocking collectives, per_device(): copies = lax.all_to_all(spread, 'mem', 0, 0, tiled=True)  14.4 us
    all_to_all x1, waiting for transfers between devices, per_device(): gathered = lax.all_to_all(outgoing, 'space', 0, 0, tiled=True)  11 us
    all_to_all x1, starting transfers between devices, per_device(): gathered = lax.all_to_all(outgoing, 'space', 0, 0, tiled=True)  9.19 us
    pallas_call x2, Pallas kernels, member_sums(): pl.pallas_call(functools.partial(member_kernel, span), in_specs=[SCALAR]...  9.1 us
    pallas_call x1, Pallas kernels, responses(): pl.pallas_call(functools.partial(response_kernel, scale), out_shape=[wide...  4.62 us
    pallas_call x1, Pallas kernels, member_planes(): pl.pallas_call(planes_kernel, in_specs=[SCALAR, FAR], out_specs=[FAR] * (...  3.75 us
    pallas_call x1, Pallas kernels, prepare(): pl.pallas_call(prepare_kernel, out_shape=[shape_of(2, hidden, 3 * GROUP),...  3.54 us
  transfers between devices with their start and end apart: 8, of which 2 were waited for; matrix products, arithmetic and copies ran while one was open for 0% of the time, Pallas kernels for 18%

profile of v5, /device:TPU:8, one launch (start us, length us, event | category | flops | bytes accessed | tf_op | source)
XLA Modules:
  0.0 88.0 jit_solution(2952010268704937941)
XLA Ops:
  0.6 0.8 fusion.2
  1.4 0.1 collective-permute-start.1
  1.5 1.9 %collective-permute-start = (f32[2,4,384]{2,1,0:T(4,128)S(1)}, f32[2,4,384]{2,1,0:T(4,128)S(1)}, u32[]{:S(2)}, u32[]{:S(2)}) collective-permute-start(f32[2,4,384]{2,1,0:T(4,128)S(1)} %get-tuple-element.47), channel_id=1, source_target_pairs={{0,8},{8,0},{16,24},{24,16},{32,40},{40,32},{48,56},{56,48},{64,72... | collective-permute-start | bytes 36872 | tf_op jit(solution)/shard_map/ppermute | solution.py:663
  3.4 3.5 %prepare.1 = (bf16[2,128,96]{2,1,0:T(8,128)(2,1)S(1)}, bf16[2,48,256]{2,1,0:T(8,128)(2,1)S(1)}, bf16[768,384]{1,0:T(8,128)(2,1)S(1)}, bf16[768,384]{1,0:T(8,128)...) custom-call(f32[24,2,384]{2,1,0:T(2,128)} %state_far.1, f32[24,2,384]{2,1,0:T(2,128)} %cot_far.1, ...), custom_call_target="tpu_custom_call" | custom-call | flops 2000000000 | bytes 3000000 | tf_op jit(solution)/shard_map/prepare/pallas_call | solution.py:485
  7.0 0.0 collective-permute-done.1.neighbour_ref
  7.0 0.0 collective-permute-done.partner_ref
  7.0 1.6 %gradient.1 = bf16[32,24,384]{2,1,0:T(8,128)(2,1)} custom-call(s32[1]{0:T(128)} %bitcast.1.core_ref, f32[2,24,384]{2,1,0:T(8,128)S(1)} %get-tuple-element.22.cot_planes, f32[2,4,384]{2,1,0:T(4,128)S(1)} %collective-permute-done.partner_ref, f32[2,4,384]{2,1,0:T(4,128)S(1)} %collective-permute-done.1.neighbour_ref, ...), custom_call_target="tpu_custom_call" | custom-call | flops 400000000 | bytes 1500000 | tf_op jit(solution)/shard_map/gradient/pallas_call | solution.py:519
  8.6 9.2 %all-to-all-start = ((bf16[32,24,384]{2,1,0:T(8,128)(2,1)}), bf16[32,24,384]{2,1,0:T(8,128)(2,1)S(1)}, u32[]{:S(2)}, u32[]{:S(2)}) async-start(bf16[32,24,384]{2,1,0:T(8,128)(2,1)} %gradient.1), calls=%async_computation | async-start | bytes 1179648 | tf_op jit(solution)/shard_map/all_to_all | solution.py:673
  17.8 0.0 copy-start.1
  17.8 0.0 copy-start.2
  17.8 3.8 %planes.1 = (bf16[768,384]{1,0:T(8,128)(2,1)}, bf16[768,384]{1,0:T(8,128)(2,1)}, bf16[768,384]{1,0:T(8,128)(2,1)}, bf16[768,384]{1,0:T(8,128)(2,1)}, bf16[768,38...) custom-call(s32[1]{0:T(128)} %bitcast.1.core_ref, ...), custom_call_target="tpu_custom_call" | custom-call | bytes 10000000 | tf_op jit(solution)/shard_map/planes/pallas_call | solution.py:541
  21.6 0.2 collective-permute-start.2
  21.8 0.4 collective-permute-start.3
  22.2 0.1 collective-permute-start.4
  22.3 0.4 collective-permute-start.5
  22.7 3.2 %slopes.1.slopes_far = f32[26,128,384]{2,1,0:T(8,128)} custom-call(s32[1]{0:T(128)} %bitcast.1.core_ref, f32[2,4,384]{2,1,0:T(4,128)S(1)} %collective-permute-done.partner_ref, f32[2,4,384]{2,1,0:T(4,128)S(1)} %collective-permute-done.1.neighbour_ref, bf16[2,128,96]{2,1,0:T(8,128)(2,1)S(1)} %get-tuple-element.23.front_ref, ...), custom_call_target="tpu_custom_call" | custom-call | flops 1000000000 | bytes 6000000 | tf_op jit(solution)/shard_map/slopes/pallas_call | solution.py:563
  25.9 0.0 copy-start
  25.9 11.0 %all-to-all-done = bf16[32,24,384]{2,1,0:T(8,128)(2,1)S(1)} async-done(((bf16[32,24,384]{2,1,0:T(8,128)(2,1)}), bf16[32,24,384]{2,1,0:T(8,128)(2,1)S(1)}, u32[]{:S(2)}, u32[]{:S(2)}) %all-to-all-start) | async-done | bytes 589856 | tf_op jit(solution)/shard_map/all_to_all | solution.py:673
  36.9 0.0 collective-permute-done.2.refs_4_
  36.9 0.0 collective-permute-done.3.refs_5_
  36.9 0.0 collective-permute-done.4.refs_6_
  36.9 0.0 collective-permute-done.5.refs_7_
  36.9 0.0 copy-done.1
  36.9 0.0 copy-done.2
  36.9 3.9 %members.2 = bf16[32,32,128]{2,1,0:T(8,128)(2,1)S(1)} custom-call(s32[1]{0:T(128)S(6)} %sub.8.half_ref, bf16[768,384]{1,0:T(8,128)(2,1)} %get-tuple-element.29.refs_0_, bf16[768,384]{1,0:T(8,128)(2,1)} %get-tuple-element.30.refs_1_, bf16[768,384]{1,0:T(8,128)(2,1)} %get-tuple-element.31.refs_2_, bf16[768,384]{1,0:T(8,128)(2,1)} %get-tuple-element.32.refs_3_, ...), custom_call_target="tpu_custom_call" | custom-call | flops 2048000000 | bytes 4000000 | tf_op jit(solution)/shard_map/members/pallas_call | solution.py:591
  40.8 1.7 %collective-permute-start.6 = (bf16[32,32,128]{2,1,0:T(8,128)(2,1)S(1)}, bf16[32,32,128]{2,1,0:T(8,128)(2,1)S(1)}, u32[]{:S(2)}, u32[]{:S(2)}) collective-permute-start(bf16[32,32,128]{2,1,0:T(8,128)(2,1)S(1)} %members.2), channel_id=1, source_target_pairs={{0,2},{1,3},{2,0},{3,1},{4,6},{5,7},{6,4},{7,5},{8,10},{9,11},{10,... | collective-permute-start | bytes 786440 | tf_op jit(solution)/shard_map/ppermute | solution.py:683
  42.6 0.0 copy-done
  42.6 5.2 %members.3.own_ref = f32[32,56,128]{2,1,0:T(8,128)S(1)} custom-call(s32[1]{0:T(128)} %bitcast.half_ref, bf16[768,384]{1,0:T(8,128)(2,1)} %get-tuple-element.29.refs_0_, bf16[768,384]{1,0:T(8,128)(2,1)} %get-tuple-element.30.refs_1_, bf16[768,384]{1,0:T(8,128)(2,1)} %get-tuple-element.31.refs_2_, bf16[768,384]{1,0:T(8,128)(2,1)} %get-tuple-element.32.refs_3_, ...), custom_call_target="tpu_custom_call" | custom-call | flops 4096000000 | bytes 4000000 | tf_op jit(solution)/shard_map/members/pallas_call | solution.py:591
  47.8 1.1 %collective-permute-done.6.other_ref = bf16[32,32,128]{2,1,0:T(8,128)(2,1)S(1)} collective-permute-done((bf16[32,32,128]{2,1,0:T(8,128)(2,1)S(1)}, bf16[32,32,128]{2,1,0:T(8,128)(2,1)S(1)}, u32[]{:S(2)}, u32[]{:S(2)}) %collective-permute-start.6) | collective-permute-done | bytes 262176 | tf_op jit(solution)/shard_map/ppermute | solution.py:683
  48.9 0.1 add_parts.1
  49.0 19.8 %all_to_all.15.refs_0_ = bf16[32,56,128]{2,1,0:T(8,128)(2,1)S(1)} all-to-all(bf16[32,56,128]{2,1,0:T(8,128)(2,1)S(1)} %add_parts.1), channel_id=1, replica_groups=mesh['space'=32,'mem'=8] {'space'}, dimensions={0} | all-to-all | bytes 917504 | tf_op jit(solution)/shard_map/all_to_all | solution.py:685
  68.8 0.1 block_sum.1
  68.8 14.4 %all_to_all.16.copies_ref = bf16[8,112,128]{2,1,0:T(8,128)(2,1)S(1)} all-to-all(bf16[8,112,128]{2,1,0:T(8,128)(2,1)S(1)} %block_sum.1), channel_id=1, replica_groups=mesh['space'=32,'mem'=8] {'mem'}, dimensions={0} | all-to-all | bytes 458752 | tf_op jit(solution)/shard_map/all_to_all | solution.py:687
  83.3 4.6 %response.1 = (f32[24,2,384]{2,1,0:T(2,128)}, f32[24,2,384]{2,1,0:T(2,128)}) custom-call(bf16[8,112,128]{2,1,0:T(8,128)(2,1)S(1)} %all_to_all.16.copies_ref, f32[26,128,384]{2,1,0:T(8,128)} %slopes.1.slopes_far, bf16[2,128,96]{2,1,0:T(8,128)(2,1)S(1)} %get-tuple-element.23.front_ref, bf16[2,48,256]{2,1,0:T(8,128)(2,1)S(1)} %get-tuple-element.24.back_ref), custom_call_target="tpu_custom_call" | custom-call | tf_op jit(solution)/shard_map/response/pallas_call | solution.py:636
  (1 shorter events, 0.0 us)
Async XLA Ops:
  1.4 5.6 %collective-permute-start.1 = (f32[2,4,384]{2,1,0:T(4,128)S(1)}, f32[2,4,384]{2,1,0:T(4,128)S(1)}, u32[]{:S(2)}, u32[]{:S(2)}) collective-permute-start(f32[2,4,384]{2,1,0:T(4,128)S(1)} %get-tuple-element.46), channel_id=1, source_target_pairs={{0,248},{8,16},{16,8},{24,32},{32,24},{40,48},{48,40},{56,64},{64,... | collective-permute-start | bytes 36872 | tf_op jit(solution)/shard_map/ppermute | solution.py:662
  1.5 5.5 %collective-permute-start = (f32[2,4,384]{2,1,0:T(4,128)S(1)}, f32[2,4,384]{2,1,0:T(4,128)S(1)}, u32[]{:S(2)}, u32[]{:S(2)}) collective-permute-start(f32[2,4,384]{2,1,0:T(4,128)S(1)} %get-tuple-element.47), channel_id=1, source_target_pairs={{0,8},{8,0},{16,24},{24,16},{32,40},{40,32},{48,56},{56,48},{64,72... | collective-permute-start | bytes 36872 | tf_op jit(solution)/shard_map/ppermute | solution.py:663
  8.6 28.3 %all-to-all-start = ((bf16[32,24,384]{2,1,0:T(8,128)(2,1)}), bf16[32,24,384]{2,1,0:T(8,128)(2,1)S(1)}, u32[]{:S(2)}, u32[]{:S(2)}) async-start(bf16[32,24,384]{2,1,0:T(8,128)(2,1)} %gradient.1), calls=%async_computation | async-start | bytes 1179648 | tf_op jit(solution)/shard_map/all_to_all | solution.py:673
  17.8 19.1 %copy-start.1 = (bf16[2,256,128]{2,1,0:T(8,128)(2,1)S(1)}, bf16[2,256,128]{2,1,0:T(8,128)(2,1)}, u32[]{:S(2)}) copy-start(bf16[2,256,128]{2,1,0:T(8,128)(2,1)} %constant.46.clone.refs_9_) | copy-start | bytes 393220
  17.8 19.1 %copy-start.2 = (bf16[96,128]{1,0:T(8,128)(2,1)S(1)}, bf16[96,128]{1,0:T(8,128)(2,1)}, u32[]{:S(2)}) copy-start(bf16[96,128]{1,0:T(8,128)(2,1)} %constant.47.clone.refs_10_) | copy-start | bytes 73732
  21.6 15.3 %collective-permute-start.2 = (bf16[768,384]{1,0:T(8,128)(2,1)}, bf16[768,384]{1,0:T(8,128)(2,1)S(1)}, u32[]{:S(2)}, u32[]{:S(2)}) collective-permute-start(bf16[768,384]{1,0:T(8,128)(2,1)} %get-tuple-element.33), channel_id=1, source_target_pairs={{0,8},{8,0},{16,24},{24,16},{32,40},{40,32},{48,56},{56,48},{64,72... | collective-permute-start | bytes 1769480 | tf_op jit(solution)/shard_map/ppermute | solution.py:675
  21.8 15.1 %collective-permute-start.3 = (bf16[768,384]{1,0:T(8,128)(2,1)}, bf16[768,384]{1,0:T(8,128)(2,1)S(1)}, u32[]{:S(2)}, u32[]{:S(2)}) collective-permute-start(bf16[768,384]{1,0:T(8,128)(2,1)} %get-tuple-element.34), channel_id=1, source_target_pairs={{0,8},{8,0},{16,24},{24,16},{32,40},{40,32},{48,56},{56,48},{64,72... | collective-permute-start | bytes 1769480 | tf_op jit(solution)/shard_map/ppermute | solution.py:675
  22.2 14.7 %collective-permute-start.4 = (bf16[768,384]{1,0:T(8,128)(2,1)}, bf16[768,384]{1,0:T(8,128)(2,1)S(1)}, u32[]{:S(2)}, u32[]{:S(2)}) collective-permute-start(bf16[768,384]{1,0:T(8,128)(2,1)} %get-tuple-element.35), channel_id=1, source_target_pairs={{0,8},{8,0},{16,24},{24,16},{32,40},{40,32},{48,56},{56,48},{64,72... | collective-permute-start | bytes 1769480 | tf_op jit(solution)/shard_map/ppermute | solution.py:675
  22.3 14.6 %collective-permute-start.5 = (bf16[768,384]{1,0:T(8,128)(2,1)}, bf16[768,384]{1,0:T(8,128)(2,1)}, u32[]{:S(2)}, u32[]{:S(2)}) collective-permute-start(bf16[768,384]{1,0:T(8,128)(2,1)} %get-tuple-element.36), channel_id=1, source_target_pairs={{0,8},{8,0},{16,24},{24,16},{32,40},{40,32},{48,56},{56,48},{64,72... | collective-permute-start | bytes 1769480 | tf_op jit(solution)/shard_map/ppermute | solution.py:675
  25.9 16.6 %copy-start = (bf16[2,384,256]{2,1,0:T(8,128)(2,1)S(1)}, bf16[2,384,256]{2,1,0:T(8,128)(2,1)}, u32[]{:S(2)}) copy-start(bf16[2,384,256]{2,1,0:T(8,128)(2,1)} %constant.48.clone.refs_9_) | copy-start | bytes 1179652
  40.8 8.1 %collective-permute-start.6 = (bf16[32,32,128]{2,1,0:T(8,128)(2,1)S(1)}, bf16[32,32,128]{2,1,0:T(8,128)(2,1)S(1)}, u32[]{:S(2)}, u32[]{:S(2)}) collective-permute-start(bf16[32,32,128]{2,1,0:T(8,128)(2,1)S(1)} %members.2), channel_id=1, source_target_pairs={{0,2},{1,3},{2,0},{3,1},{4,6},{5,7},{6,4},{7,5},{8,10},{9,11},{10,... | collective-permute-start | bytes 786440 | tf_op jit(solution)/shard_map/ppermute | solution.py:683

commit v6 on v5

--- a/solution.py
+++ b/solution.py
@@ -237,6 +237,7 @@
 
 def gradient_kernel(
     core_ref,
+    half_ref,
     cot_planes,
     partner_ref,
     neighbour_ref,
@@ -268,7 +269,8 @@
     fold_lats(product, fold, 0, 2)
     fold_lats(product, fold, rows, 2)
     for var in range(2):
-        plane = (cot_planes[var] + folded(fold, rows, var)).astype(BF)
+        plane = cot_planes[var] + folded(fold, rows, var)
+        plane = jnp.where(half_ref[0] == 0, plane[:, 128:], plane[:, :256]).astype(BF)
         for pair in range(out_ref.shape[0] // 2):
             out_ref[2 * pair + var] = plane
 
@@ -297,7 +299,7 @@
 def response_kernel(
     scale,
     copies_ref,
-    slopes_far,
+    slopes_ref,
     front_ref,
     back_ref,
     incr_out,
@@ -306,13 +308,9 @@
     incr_taps,
     product,
     fold,
-    slopes_ref,
-    semaphores,
 ):
     rows = incr_out.shape[0]
     half = (rows + 2) // 2
-    halves = [pl.ds(0, half), pl.ds(half, half)]
-    copies = fetch([(slopes_far.at[part], slopes_ref.at[part]) for part in halves], semaphores)
     planes = []
     put_ones(wide, 0.0)
     groups = copies_ref.shape[0]
@@ -337,7 +335,6 @@
             jnp.dot(front_ref[0], window_of(incr_taps, row)(), preferred_element_type=F32)
             for row in batch
         ]
-        copies[part].wait()
         hidden = [slopes_ref[row] * value for row, value in zip(batch, hidden)]
         fold_rows(hidden, back_ref[1], product, batch)
     fold_lats(product, fold, 0, rows + 2)
@@ -375,22 +372,27 @@
         copy.wait()
 
 
-def member_kernel(span, half_ref, *refs):
-    *far_refs, field_ref, lat_ref, lon_ref, out_ref, field, banded, total, held, semaphores = refs
-    lons = field_ref.shape[0]
+def member_kernel(span, count, half_ref, *refs):
+    far_refs = refs[:count]
+    *field_refs, lat_ref, lon_ref, out_ref, field, banded, total, held, semaphores = refs[count:]
+    lons = field.shape[0]
     blocks = out_ref.shape[0]
     rows = lons // blocks
     reach, wide = lat_ref.shape[1:]
     half = half_ref[0]
     offset = pl.multiple_of(half * 128, 128)
-    if reach < field_ref.shape[1]:
+    if reach == 256:
         source = pl.ds(offset, reach)
     else:
         source = pl.ds(0, reach)
     target = pl.ds(offset, wide)
     member_refs = [held.at[index] for index in range(len(far_refs))]
     copies = fetch([(far.at[:, source], near) for far, near in zip(far_refs, member_refs)], semaphores)
-    field[...] = field_ref[:, source].astype(F32)
+    if reach == 256:
+        field[...] = field_refs[0][...].astype(F32)
+    else:
+        field[:, pl.ds(pl.multiple_of(128 - half * 128, 128), 256)] = field_refs[0][...].astype(F32)
+        field[:, pl.ds(pl.multiple_of(half * 256, 128), 128)] = field_refs[1][...].astype(F32)
     lat_loc = lat_ref[half]
     chunk = 2 * span
     for index, member_ref in enumerate(member_refs):
@@ -513,13 +515,13 @@
 
 
 def gradient_planes(
-    blocks, core, cot_planes, partner, neighbour, front, back, state_taps, cot_taps, partial
+    blocks, core, half, cot_planes, partner, neighbour, front, back, state_taps, cot_taps, partial
 ):
     var_count, rows, lats = cot_planes.shape
     return pl.pallas_call(
         gradient_kernel,
-        out_shape=shape_of(blocks, rows, lats),
-        in_specs=[SCALAR] + [NEAR] * 8,
+        out_shape=shape_of(blocks, rows, 256),
+        in_specs=[SCALAR] * 2 + [NEAR] * 8,
         scratch_shapes=[
             padded_scratch(4, lats),
             tap_scratch(4, lats),
@@ -533,7 +535,7 @@
             flops=400_000_000, bytes_accessed=1_500_000, transcendentals=200_000
         ),
         name="gradient",
-    )(core, cot_planes, partner, neighbour, front, back, state_taps, cot_taps, partial)
+    )(core, half, cot_planes, partner, neighbour, front, back, state_taps, cot_taps, partial)
 
 
 def member_planes(core, members):
@@ -574,8 +576,8 @@
     )(core, partner, neighbour, front, state_taps)
 
 
-def member_sums(blocks, half, kept, taken, field, wide):
-    lons, lats = field.shape
+def member_sums(blocks, half, kept, taken, fields, wide):
+    lons, lats = kept[0].shape
     rows = lons // blocks
     span = 96
     count = len(kept) + len(taken)
@@ -589,11 +591,11 @@
     )
     out_shape = shape_of(blocks, 32, 128) if wide == 128 else wide_of(blocks, 2 * (rows + 4), 128)
     return pl.pallas_call(
-        functools.partial(member_kernel, span),
+        functools.partial(member_kernel, span, count),
         in_specs=[SCALAR]
         + [FAR] * len(kept)
         + [pl.BlockSpec(memory_space=pl.ANY)] * len(taken)
-        + [NEAR] * 3,
+        + [NEAR] * (2 + len(fields)),
         out_shape=out_shape,
         scratch_shapes=[
             pltpu.VMEM((lons, reach), F32),
@@ -607,7 +609,7 @@
             flops=wide * 16_000_000, bytes_accessed=4_000_000, transcendentals=0
         ),
         name="members",
-    )(half, *[remote(value) for value in kept], *taken, field, lat_loc, lon_loc)
+    )(half, *[remote(value) for value in kept], *taken, *fields, lat_loc, lon_loc)
 
 
 def add_parts(own, other):
@@ -636,18 +638,16 @@
     return pl.pallas_call(
         functools.partial(response_kernel, scale),
         out_shape=[wide_of(rows, 2, lats)] * 2,
-        in_specs=[NEAR, FAR, NEAR, NEAR],
+        in_specs=[NEAR] * 4,
         scratch_shapes=[
             padded_scratch(rows + 4, lats),
             tap_scratch(rows + 4, lats),
             pltpu.VMEM((3, (rows + 2) * 8, lats), F32),
             padded_scratch(rows + 2, lats),
-            pltpu.VMEM((rows + 2, hidden, lats), F32),
-            pltpu.SemaphoreType.DMA((2,)),
         ],
         compiler_params=PARAMS,
         name="response",
-    )(copies, remote(slopes), front, back)
+    )(copies, slopes, front, back)
 
 
 def per_device(members, state, cotangent, conv_in, conv_out, bias):
@@ -662,12 +662,14 @@
     neighbour = lax.ppermute(jnp.where(core == 0, head, tail), "space", chain)
     partner = lax.ppermute(jnp.where(core == 0, tail, head), "space", swap)
     core = core.reshape(1)
+    parity = (lax.axis_index("mem") // 2) % 2
+    half = parity.reshape(1)
     first = jnp.transpose(conv_in, (0, 1, 3, 2))
     front, back, state_taps, cot_taps, partial, cot_planes = prepare(
         state, cotangent, first, conv_out, bias
     )
     outgoing = gradient_planes(
-        blocks, core, cot_planes, partner, neighbour, front, back, state_taps, cot_taps, partial
+        blocks, core, half, cot_planes, partner, neighbour, front, back, state_taps, cot_taps, partial
     )
     members, outgoing = lax.optimization_barrier((members, outgoing))
     gathered = lax.all_to_all(outgoing, "space", 0, 0, tiled=True)
@@ -675,13 +677,13 @@
     taken = [lax.ppermute(give, "space", swap) for give in given]
     slopes = hidden_slopes(core, partner, neighbour, front, state_taps)
     gathered, slopes = lax.optimization_barrier((gathered, slopes))
-    half = (lax.axis_index("mem") // 2) % 2
-    half = half.reshape(1)
-    field = gathered.reshape(lons, lats)
-    theirs = member_sums(blocks, 1 - half, kept, taken, field, 128)
-    theirs, field = lax.optimization_barrier((theirs, field))
-    other = lax.ppermute(theirs, "mem", [(i, i ^ 2) for i in range(groups)])
-    own = member_sums(blocks, half, kept, taken, field, 256)
+    across = [(i, i ^ 2) for i in range(groups)]
+    inner = gathered.reshape(lons, 256)
+    outer = lax.ppermute(jnp.where(parity == 0, inner[:, 128:], inner[:, :128]), "mem", across)
+    theirs = member_sums(blocks, 1 - half, kept, taken, [inner], 128)
+    theirs, inner = lax.optimization_barrier((theirs, inner))
+    other = lax.ppermute(theirs, "mem", across)
+    own = member_sums(blocks, half, kept, taken, [inner, outer], 256)
     arrived = [lax.all_to_all(add_parts(own, other), "space", 0, 0, tiled=True)]
     spread = block_sums(groups, arrived)
     copies = lax.all_to_all(spread, "mem", 0, 0, tiled=True)

time: 88.4 us -> 84 us (0.950)
  waiting for transfers between devices: 12.1 us -> 8.23 us
  Pallas kernels: 26 us -> 23.9 us
  local copies, waits for them, and re-layouts: 0.77 us -> 1.67 us
    all_to_all x1, waiting for transfers between devices: 11 us -> 6.81 us  [per_device(): gathered = lax.all_to_all(outgoing, 'space', 0, 0, tiled=True)]
    pallas_call x1, Pallas kernels: 4.62 us -> 2.57 us  [responses(): pl.pallas_call(functools.partial(response_kernel, scale), out_shape=[wide...]
    unnamed x6 -> x10, local copies, waits for them, and re-layouts: 0.02 us -> 0.92 us
    ppermute x1 -> x2, starting transfers between devices: 1.74 us -> 2.36 us  [the longest x1 1.75 us: per_device(): lax.ppermute(jnp.where(parity == 0, inner[:, 128:], inner[:, :128]), 'mem...]
  transfers between devices with their start and end apart: 8 -> 9, of which waited for: 2 -> 2; matrix products, arithmetic and copies ran while one was open for 0% -> 0% of each run, Pallas kernels for 18% -> 24%
where the time goes in v6:
time: 84 us; the launch traced here: 83.6 us
  blocking collectives  34.3 us (41%)
  Pallas kernels  23.9 us (28%)
  starting transfers between devices  14.7 us (18%)
  waiting for transfers between devices  8.23 us (10%)
  local copies, waits for them, and re-layouts  1.67 us (2%)
    all_to_all x1, blocking collectives, per_device(): arrived = [lax.all_to_all(add_parts(own, other), 'space', 0, 0, tiled=True)]  20.1 us
    all_to_all x1, blocking collectives, per_device(): copies = lax.all_to_all(spread, 'mem', 0, 0, tiled=True)  14.1 us
    pallas_call x2, Pallas kernels, member_sums(): pl.pallas_call(functools.partial(member_kernel, span, count), in_specs=[S...  9.23 us
    all_to_all x1, starting transfers between devices, per_device(): gathered = lax.all_to_all(outgoing, 'space', 0, 0, tiled=True)  9.19 us
    all_to_all x1, waiting for transfers between devices, per_device(): gathered = lax.all_to_all(outgoing, 'space', 0, 0, tiled=True)  6.81 us
    pallas_call x1, Pallas kernels, member_planes(): pl.pallas_call(planes_kernel, in_specs=[SCALAR, FAR], out_specs=[FAR] * (...  3.73 us
    pallas_call x1, Pallas kernels, prepare(): pl.pallas_call(prepare_kernel, out_shape=[shape_of(2, hidden, 3 * GROUP),...  3.51 us
    pallas_call x1, Pallas kernels, hidden_slopes(): pl.pallas_call(slopes_kernel, out_shape=pltpu.HBM((rows + 2, hidden, lats...  3.22 us
  transfers between devices with their start and end apart: 9, of which 2 were waited for; matrix products, arithmetic and copies ran while one was open for 0% of the time, Pallas kernels for 24%

profile of v6, /device:TPU:8, one launch (start us, length us, event | category | flops | bytes accessed | tf_op | source)
XLA Modules:
  0.0 83.6 jit_solution(2810696744527346324)
XLA Ops:
  0.6 0.8 fusion.2
  1.4 0.1 collective-permute-start.1
  1.5 1.9 %collective-permute-start = (f32[2,4,384]{2,1,0:T(4,128)S(1)}, f32[2,4,384]{2,1,0:T(4,128)S(1)}, u32[]{:S(2)}, u32[]{:S(2)}) collective-permute-start(f32[2,4,384]{2,1,0:T(4,128)S(1)} %get-tuple-element.47), channel_id=1, source_target_pairs={{0,8},{8,0},{16,24},{24,16},{32,40},{40,32},{48,56},{56,48},{64,72... | collective-permute-start | bytes 36872 | tf_op jit(solution)/shard_map/ppermute | solution.py:663
  3.4 3.5 %prepare.1 = (bf16[2,128,96]{2,1,0:T(8,128)(2,1)S(1)}, bf16[2,48,256]{2,1,0:T(8,128)(2,1)S(1)}, bf16[768,384]{1,0:T(8,128)(2,1)S(1)}, bf16[768,384]{1,0:T(8,128)...) custom-call(f32[24,2,384]{2,1,0:T(2,128)} %state_far.1, f32[24,2,384]{2,1,0:T(2,128)} %cot_far.1, ...), custom_call_target="tpu_custom_call" | custom-call | flops 2000000000 | bytes 3000000 | tf_op jit(solution)/shard_map/prepare/pallas_call | solution.py:487
  7.0 0.0 collective-permute-done.1.neighbour_ref
  7.0 0.0 collective-permute-done.partner_ref
  7.0 1.5 %gradient.1 = bf16[32,24,256]{2,1,0:T(8,128)(2,1)} custom-call(s32[1]{0:T(128)} %bitcast.1.core_ref, s32[1]{0:T(128)} %bitcast.half_ref, f32[2,24,384]{2,1,0:T(8,128)S(1)} %get-tuple-element.22.cot_planes, f32[2,4,384]{2,1,0:T(4,128)S(1)} %collective-permute-done.partner_ref, f32[2,4,384]{2,1,0:T(4,128)S(1)} %collective-permute-done.1.neighbour_ref, ...), custom_call_target="tpu_custom_call" | custom-call | flops 400000000 | bytes 1500000 | tf_op jit(solution)/shard_map/gradient/pallas_call | solution.py:521
  8.5 9.2 %all-to-all-start = ((bf16[32,24,256]{2,1,0:T(8,128)(2,1)}), bf16[32,24,256]{2,1,0:T(8,128)(2,1)S(1)}, u32[]{:S(2)}, u32[]{:S(2)}) async-start(bf16[32,24,256]{2,1,0:T(8,128)(2,1)} %gradient.1), calls=%async_computation | async-start | bytes 786432 | tf_op jit(solution)/shard_map/all_to_all | solution.py:675
  17.7 0.0 copy-start.2
  17.7 3.7 %planes.1 = (bf16[768,384]{1,0:T(8,128)(2,1)}, bf16[768,384]{1,0:T(8,128)(2,1)}, bf16[768,384]{1,0:T(8,128)(2,1)}, bf16[768,384]{1,0:T(8,128)(2,1)}, bf16[768,38...) custom-call(s32[1]{0:T(128)} %bitcast.1.core_ref, ...), custom_call_target="tpu_custom_call" | custom-call | bytes 10000000 | tf_op jit(solution)/shard_map/planes/pallas_call | solution.py:543
  21.5 0.2 collective-permute-start.2
  21.7 0.4 collective-permute-start.3
  22.1 0.1 collective-permute-start.4
  22.2 0.4 collective-permute-start.5
  22.6 3.2 %slopes.1.slopes_ref = f32[26,128,384]{2,1,0:T(8,128)} custom-call(s32[1]{0:T(128)} %bitcast.1.core_ref, f32[2,4,384]{2,1,0:T(4,128)S(1)} %collective-permute-done.partner_ref, f32[2,4,384]{2,1,0:T(4,128)S(1)} %collective-permute-done.1.neighbour_ref, bf16[2,128,96]{2,1,0:T(8,128)(2,1)S(1)} %get-tuple-element.23.front_ref, ...), custom_call_target="tpu_custom_call" | custom-call | flops 1000000000 | bytes 6000000 | tf_op jit(solution)/shard_map/slopes/pallas_call | solution.py:565
  25.8 0.0 copy-start
  25.8 6.8 %all-to-all-done = bf16[32,24,256]{2,1,0:T(8,128)(2,1)S(1)} async-done(((bf16[32,24,256]{2,1,0:T(8,128)(2,1)}), bf16[32,24,256]{2,1,0:T(8,128)(2,1)S(1)}, u32[]{:S(2)}, u32[]{:S(2)}) %all-to-all-start) | async-done | bytes 393248 | tf_op jit(solution)/shard_map/all_to_all | solution.py:675
  32.6 1.8 %collective-permute-start.6 = (bf16[768,128]{1,0:T(8,128)(2,1)S(1)}, bf16[768,128]{1,0:T(8,128)(2,1)S(1)}, u32[]{:S(2)}, u32[]{:S(2)}) collective-permute-start(bf16[768,128]{1,0:T(8,128)(2,1)S(1)} %slice_select_fusion), channel_id=1, source_target_pairs={{0,2},{1,3},{2,0},{3,1},{4,6},{5,7},{6,4},{7,5},{8,10},{9,11},{10,... | collective-permute-start | bytes 589832 | tf_op jit(solution)/shard_map/ppermute | solution.py:682
  34.4 0.0 collective-permute-done.2.refs_4_
  34.4 0.0 collective-permute-done.3.refs_5_
  34.4 0.0 collective-permute-done.4.refs_6_
  34.4 0.0 collective-permute-done.5.refs_7_
  34.4 0.0 copy-done.2
  34.4 0.0 copy-start.1
  34.4 0.9 %copy-done.1 = bf16[2,256,128]{2,1,0:T(8,128)(2,1)S(1)} copy-done((bf16[2,256,128]{2,1,0:T(8,128)(2,1)S(1)}, bf16[2,256,128]{2,1,0:T(8,128)(2,1)}, u32[]{:S(2)}) %copy-start.1) | copy-done | bytes 131096
  35.3 0.0 slice-start
  35.3 4.0 %members.2 = bf16[32,32,128]{2,1,0:T(8,128)(2,1)S(1)} custom-call(s32[1]{0:T(128)S(6)} %sub.8.half_ref, bf16[768,384]{1,0:T(8,128)(2,1)} %get-tuple-element.29.refs_0_, bf16[768,384]{1,0:T(8,128)(2,1)} %get-tuple-element.30.refs_1_, bf16[768,384]{1,0:T(8,128)(2,1)} %get-tuple-element.31.refs_2_, bf16[768,384]{1,0:T(8,128)(2,1)} %get-tuple-element.32.refs_3_, ...), custom_call_target="tpu_custom_call" | custom-call | flops 2048000000 | bytes 4000000 | tf_op jit(solution)/shard_map/members/pallas_call | solution.py:593
  39.3 0.0 slice-start.1
  39.4 0.6 collective-permute-start.7
  40.0 0.0 collective-permute-done.6.refs_9_
  40.0 0.0 copy-done
  40.0 5.2 %members.3.own_ref = f32[32,56,128]{2,1,0:T(8,128)S(1)} custom-call(s32[1]{0:T(128)} %bitcast.half_ref, bf16[768,384]{1,0:T(8,128)(2,1)} %get-tuple-element.29.refs_0_, bf16[768,384]{1,0:T(8,128)(2,1)} %get-tuple-element.30.refs_1_, bf16[768,384]{1,0:T(8,128)(2,1)} %get-tuple-element.31.refs_2_, bf16[768,384]{1,0:T(8,128)(2,1)} %get-tuple-element.32.refs_3_, ...), custom_call_target="tpu_custom_call" | custom-call | flops 4096000000 | bytes 4000000 | tf_op jit(solution)/shard_map/members/pallas_call | solution.py:593
  45.2 1.4 %collective-permute-done.7.other_ref = bf16[32,32,128]{2,1,0:T(8,128)(2,1)S(1)} collective-permute-done((bf16[32,32,128]{2,1,0:T(8,128)(2,1)S(1)}, bf16[32,32,128]{2,1,0:T(8,128)(2,1)S(1)}, u32[]{:S(2)}, u32[]{:S(2)}) %collective-permute-start.7) | collective-permute-done | bytes 262176 | tf_op jit(solution)/shard_map/ppermute | solution.py:685
  46.6 0.1 add_parts.1
  46.7 20.1 %all_to_all.15.refs_0_ = bf16[32,56,128]{2,1,0:T(8,128)(2,1)S(1)} all-to-all(bf16[32,56,128]{2,1,0:T(8,128)(2,1)S(1)} %add_parts.1), channel_id=1, replica_groups=mesh['space'=32,'mem'=8] {'space'}, dimensions={0} | all-to-all | bytes 917504 | tf_op jit(solution)/shard_map/all_to_all | solution.py:687
  66.8 0.1 block_sum.1
  66.9 14.1 %all_to_all.16.copies_ref = bf16[8,112,128]{2,1,0:T(8,128)(2,1)S(1)} all-to-all(bf16[8,112,128]{2,1,0:T(8,128)(2,1)S(1)} %block_sum.1), channel_id=1, replica_groups=mesh['space'=32,'mem'=8] {'mem'}, dimensions={0} | all-to-all | bytes 458752 | tf_op jit(solution)/shard_map/all_to_all | solution.py:689
  81.0 0.0 slice-done
  81.0 0.0 slice-done.1
  81.0 2.6 %response.1 = (f32[24,2,384]{2,1,0:T(2,128)}, f32[24,2,384]{2,1,0:T(2,128)}) custom-call(bf16[8,112,128]{2,1,0:T(8,128)(2,1)S(1)} %all_to_all.16.copies_ref, f32[26,128,384]{2,1,0:T(8,128)S(1)} %bitcast.6, bf16[2,128,96]{2,1,0:T(8,128)(2,1)S(1)} %get-tuple-element.23.front_ref, bf16[2,48,256]{2,1,0:T(8,128)(2,1)S(1)} %get-tuple-element.24.back_ref), custom_call_target="tpu_custom_call" | custom-call | tf_op jit(solution)/shard_map/response/pallas_call | solution.py:638
  (3 shorter events, 0.0 us)
Async XLA Ops:
  1.4 5.6 %collective-permute-start.1 = (f32[2,4,384]{2,1,0:T(4,128)S(1)}, f32[2,4,384]{2,1,0:T(4,128)S(1)}, u32[]{:S(2)}, u32[]{:S(2)}) collective-permute-start(f32[2,4,384]{2,1,0:T(4,128)S(1)} %get-tuple-element.46), channel_id=1, source_target_pairs={{0,248},{8,16},{16,8},{24,32},{32,24},{40,48},{48,40},{56,64},{64,... | collective-permute-start | bytes 36872 | tf_op jit(solution)/shard_map/ppermute | solution.py:662
  1.5 5.5 %collective-permute-start = (f32[2,4,384]{2,1,0:T(4,128)S(1)}, f32[2,4,384]{2,1,0:T(4,128)S(1)}, u32[]{:S(2)}, u32[]{:S(2)}) collective-permute-start(f32[2,4,384]{2,1,0:T(4,128)S(1)} %get-tuple-element.47), channel_id=1, source_target_pairs={{0,8},{8,0},{16,24},{24,16},{32,40},{40,32},{48,56},{56,48},{64,72... | collective-permute-start | bytes 36872 | tf_op jit(solution)/shard_map/ppermute | solution.py:663
  8.5 24.1 %all-to-all-start = ((bf16[32,24,256]{2,1,0:T(8,128)(2,1)}), bf16[32,24,256]{2,1,0:T(8,128)(2,1)S(1)}, u32[]{:S(2)}, u32[]{:S(2)}) async-start(bf16[32,24,256]{2,1,0:T(8,128)(2,1)} %gradient.1), calls=%async_computation | async-start | bytes 786432 | tf_op jit(solution)/shard_map/all_to_all | solution.py:675
  17.7 16.7 %copy-start.2 = (bf16[96,128]{1,0:T(8,128)(2,1)S(1)}, bf16[96,128]{1,0:T(8,128)(2,1)}, u32[]{:S(2)}) copy-start(bf16[96,128]{1,0:T(8,128)(2,1)} %constant.47.clone.refs_10_.refs_11_) | copy-start | bytes 73732
  21.5 12.9 %collective-permute-start.2 = (bf16[768,384]{1,0:T(8,128)(2,1)}, bf16[768,384]{1,0:T(8,128)(2,1)S(1)}, u32[]{:S(2)}, u32[]{:S(2)}) collective-permute-start(bf16[768,384]{1,0:T(8,128)(2,1)} %get-tuple-element.33), channel_id=1, source_target_pairs={{0,8},{8,0},{16,24},{24,16},{32,40},{40,32},{48,56},{56,48},{64,72... | collective-permute-start | bytes 1769480 | tf_op jit(solution)/shard_map/ppermute | solution.py:677
  21.7 12.7 %collective-permute-start.3 = (bf16[768,384]{1,0:T(8,128)(2,1)}, bf16[768,384]{1,0:T(8,128)(2,1)S(1)}, u32[]{:S(2)}, u32[]{:S(2)}) collective-permute-start(bf16[768,384]{1,0:T(8,128)(2,1)} %get-tuple-element.34), channel_id=1, source_target_pairs={{0,8},{8,0},{16,24},{24,16},{32,40},{40,32},{48,56},{56,48},{64,72... | collective-permute-start | bytes 1769480 | tf_op jit(solution)/shard_map/ppermute | solution.py:677
  22.1 12.3 %collective-permute-start.4 = (bf16[768,384]{1,0:T(8,128)(2,1)}, bf16[768,384]{1,0:T(8,128)(2,1)S(1)}, u32[]{:S(2)}, u32[]{:S(2)}) collective-permute-start(bf16[768,384]{1,0:T(8,128)(2,1)} %get-tuple-element.35), channel_id=1, source_target_pairs={{0,8},{8,0},{16,24},{24,16},{32,40},{40,32},{48,56},{56,48},{64,72... | collective-permute-start | bytes 1769480 | tf_op jit(solution)/shard_map/ppermute | solution.py:677
  22.2 12.2 %collective-permute-start.5 = (bf16[768,384]{1,0:T(8,128)(2,1)}, bf16[768,384]{1,0:T(8,128)(2,1)S(1)}, u32[]{:S(2)}, u32[]{:S(2)}) collective-permute-start(bf16[768,384]{1,0:T(8,128)(2,1)} %get-tuple-element.36), channel_id=1, source_target_pairs={{0,8},{8,0},{16,24},{24,16},{32,40},{40,32},{48,56},{56,48},{64,72... | collective-permute-start | bytes 1769480 | tf_op jit(solution)/shard_map/ppermute | solution.py:677
  25.8 14.2 %copy-start = (bf16[2,384,256]{2,1,0:T(8,128)(2,1)S(1)}, bf16[2,384,256]{2,1,0:T(8,128)(2,1)}, u32[]{:S(2)}) copy-start(bf16[2,384,256]{2,1,0:T(8,128)(2,1)} %constant.48.clone.refs_10_) | copy-start | bytes 1179652
  32.6 7.3 %collective-permute-start.6 = (bf16[768,128]{1,0:T(8,128)(2,1)S(1)}, bf16[768,128]{1,0:T(8,128)(2,1)S(1)}, u32[]{:S(2)}, u32[]{:S(2)}) collective-permute-start(bf16[768,128]{1,0:T(8,128)(2,1)S(1)} %slice_select_fusion), channel_id=1, source_target_pairs={{0,2},{1,3},{2,0},{3,1},{4,6},{5,7},{6,4},{7,5},{8,10},{9,11},{10,... | collective-permute-start | bytes 589832 | tf_op jit(solution)/shard_map/ppermute | solution.py:682
  34.4 0.9 %copy-start.1 = (bf16[2,256,128]{2,1,0:T(8,128)(2,1)S(1)}, bf16[2,256,128]{2,1,0:T(8,128)(2,1)}, u32[]{:S(2)}) copy-start(bf16[2,256,128]{2,1,0:T(8,128)(2,1)} %constant.46.clone.refs_9_) | copy-start | bytes 393220
  35.3 45.7 %slice-start = ((s8[5111808]{0:T(1024)(128)(4,1)}), s8[4194304]{0:T(1024)(128)(4,1)S(1)}, s32[]{:S(2)}) async-start(s8[5111808]{0:T(1024)(128)(4,1)} %bitcast.5), calls=%async_computation.3 | async-start | bytes 8388608
  39.3 41.7 %slice-start.1 = ((s8[5111808]{0:T(1024)(128)(4,1)}), s8[917504]{0:T(1024)(128)(4,1)S(1)}, s32[]{:S(2)}) async-start(s8[5111808]{0:T(1024)(128)(4,1)} %bitcast.5), calls=%async_computation.4 | async-start | bytes 1835008
  39.4 7.2 %collective-permute-start.7 = (bf16[32,32,128]{2,1,0:T(8,128)(2,1)S(1)}, bf16[32,32,128]{2,1,0:T(8,128)(2,1)S(1)}, u32[]{:S(2)}, u32[]{:S(2)}) collective-permute-start(bf16[32,32,128]{2,1,0:T(8,128)(2,1)S(1)} %members.2), channel_id=1, source_target_pairs={{0,2},{1,3},{2,0},{3,1},{4,6},{5,7},{6,4},{7,5},{8,10},{9,11},{10,... | collective-permute-start | bytes 786440 | tf_op jit(solution)/shard_map/ppermute | solution.py:685

commit v7 on v6

--- a/solution.py
+++ b/solution.py
@@ -374,11 +374,11 @@
 
 def member_kernel(span, count, half_ref, *refs):
     far_refs = refs[:count]
-    *field_refs, lat_ref, lon_ref, out_ref, field, banded, total, held, semaphores = refs[count:]
+    *field_refs, lat_far, lon_far, out_ref, field, banded, total, held, lat_ref, lon_ref, semaphores = refs[count:]
     lons = field.shape[0]
     blocks = out_ref.shape[0]
     rows = lons // blocks
-    reach, wide = lat_ref.shape[1:]
+    reach, wide = lat_ref.shape
     half = half_ref[0]
     offset = pl.multiple_of(half * 128, 128)
     if reach == 256:
@@ -387,13 +387,18 @@
         source = pl.ds(0, reach)
     target = pl.ds(offset, wide)
     member_refs = [held.at[index] for index in range(len(far_refs))]
-    copies = fetch([(far.at[:, source], near) for far, near in zip(far_refs, member_refs)], semaphores)
+    pairs = [(lat_far.at[half], lat_ref), (lon_far, lon_ref)]
+    pairs += [(far.at[:, source], near) for far, near in zip(far_refs, member_refs)]
+    copies = fetch(pairs, semaphores)
+    bands_here, copies = copies[:2], copies[2:]
     if reach == 256:
         field[...] = field_refs[0][...].astype(F32)
     else:
         field[:, pl.ds(pl.multiple_of(128 - half * 128, 128), 256)] = field_refs[0][...].astype(F32)
         field[:, pl.ds(pl.multiple_of(half * 256, 128), 128)] = field_refs[1][...].astype(F32)
-    lat_loc = lat_ref[half]
+    for copy in bands_here:
+        copy.wait()
+    lat_loc = lat_ref[...]
     chunk = 2 * span
     for index, member_ref in enumerate(member_refs):
         copies[index].wait()
@@ -595,21 +600,24 @@
         in_specs=[SCALAR]
         + [FAR] * len(kept)
         + [pl.BlockSpec(memory_space=pl.ANY)] * len(taken)
-        + [NEAR] * (2 + len(fields)),
+        + [NEAR] * len(fields)
+        + [FAR] * 2,
         out_shape=out_shape,
         scratch_shapes=[
             pltpu.VMEM((lons, reach), F32),
             pltpu.VMEM((lons + 2 * HALF, count * wide), BF),
             pltpu.VMEM((lons + 16, wide), F32),
             pltpu.VMEM((count, lons, reach), BF),
-            pltpu.SemaphoreType.DMA((count,)),
+            pltpu.VMEM((reach, wide), BF),
+            pltpu.VMEM((span, span + 2 * HALF), BF),
+            pltpu.SemaphoreType.DMA((count + 2,)),
         ],
         compiler_params=PARAMS,
         cost_estimate=pl.CostEstimate(
             flops=wide * 16_000_000, bytes_accessed=4_000_000, transcendentals=0
         ),
         name="members",
-    )(half, *[remote(value) for value in kept], *taken, *fields, lat_loc, lon_loc)
+    )(half, *[remote(value) for value in kept], *taken, *fields, remote(lat_loc), remote(lon_loc))
 
 
 def add_parts(own, other):

time: 84 us -> 83.2 us (level)
  local copies, waits for them, and re-layouts: 1.67 us -> 0.76 us
    unnamed x10 -> x4, local copies, waits for them, and re-layouts: 0.92 us -> 0.01 us
where the time goes in v7:
time: 83.2 us; the launch traced here: 82.8 us
  blocking collectives  34.3 us (41%)
  Pallas kernels  24.1 us (29%)
  starting transfers between devices  14.7 us (18%)
  waiting for transfers between devices  8.15 us (10%)
    all_to_all x1, blocking collectives, per_device(): arrived = [lax.all_to_all(add_parts(own, other), 'space', 0, 0, tiled=True)]  20.1 us
    all_to_all x1, blocking collectives, per_device(): copies = lax.all_to_all(spread, 'mem', 0, 0, tiled=True)  14.1 us
    pallas_call x2, Pallas kernels, member_sums(): pl.pallas_call(functools.partial(member_kernel, span, count), in_specs=[S...  9.44 us
    all_to_all x1, starting transfers between devices, per_device(): gathered = lax.all_to_all(outgoing, 'space', 0, 0, tiled=True)  9.19 us
    all_to_all x1, waiting for transfers between devices, per_device(): gathered = lax.all_to_all(outgoing, 'space', 0, 0, tiled=True)  6.86 us
    pallas_call x1, Pallas kernels, member_planes(): pl.pallas_call(planes_kernel, in_specs=[SCALAR, FAR], out_specs=[FAR] * (...  3.7 us
    pallas_call x1, Pallas kernels, prepare(): pl.pallas_call(prepare_kernel, out_shape=[shape_of(2, hidden, 3 * GROUP),...  3.51 us
    pallas_call x1, Pallas kernels, hidden_slopes(): pl.pallas_call(slopes_kernel, out_shape=pltpu.HBM((rows + 2, hidden, lats...  3.21 us
  transfers between devices with their start and end apart: 9, of which 2 were waited for; matrix products, arithmetic and copies ran while one was open for 0% of the time, Pallas kernels for 24%

profile of v7, /device:TPU:8, one launch (start us, length us, event | category | flops | bytes accessed | tf_op | source)
XLA Modules:
  0.0 82.8 jit_solution(8261647233943235119)
XLA Ops:
  0.6 0.8 fusion.2
  1.4 0.1 collective-permute-start.1
  1.5 1.9 %collective-permute-start = (f32[2,4,384]{2,1,0:T(4,128)S(1)}, f32[2,4,384]{2,1,0:T(4,128)S(1)}, u32[]{:S(2)}, u32[]{:S(2)}) collective-permute-start(f32[2,4,384]{2,1,0:T(4,128)S(1)} %get-tuple-element.47), channel_id=1, source_target_pairs={{0,8},{8,0},{16,24},{24,16},{32,40},{40,32},{48,56},{56,48},{64,72... | collective-permute-start | bytes 36872 | tf_op jit(solution)/shard_map/ppermute | solution.py:671
  3.4 3.5 %prepare.1 = (bf16[2,128,96]{2,1,0:T(8,128)(2,1)S(1)}, bf16[2,48,256]{2,1,0:T(8,128)(2,1)S(1)}, bf16[768,384]{1,0:T(8,128)(2,1)S(1)}, bf16[768,384]{1,0:T(8,128)...) custom-call(f32[24,2,384]{2,1,0:T(2,128)} %state_far.1, f32[24,2,384]{2,1,0:T(2,128)} %cot_far.1, ...), custom_call_target="tpu_custom_call" | custom-call | flops 2000000000 | bytes 3000000 | tf_op jit(solution)/shard_map/prepare/pallas_call | solution.py:492
  7.0 0.0 collective-permute-done.1.neighbour_ref
  7.0 0.0 collective-permute-done.partner_ref
  7.0 1.5 %gradient.1 = bf16[32,24,256]{2,1,0:T(8,128)(2,1)} custom-call(s32[1]{0:T(128)} %bitcast.1.core_ref, s32[1]{0:T(128)} %bitcast.half_ref, f32[2,24,384]{2,1,0:T(8,128)S(1)} %get-tuple-element.22.cot_planes, f32[2,4,384]{2,1,0:T(4,128)S(1)} %collective-permute-done.partner_ref, f32[2,4,384]{2,1,0:T(4,128)S(1)} %collective-permute-done.1.neighbour_ref, ...), custom_call_target="tpu_custom_call" | custom-call | flops 400000000 | bytes 1500000 | tf_op jit(solution)/shard_map/gradient/pallas_call | solution.py:526
  8.5 9.2 %all-to-all-start = ((bf16[32,24,256]{2,1,0:T(8,128)(2,1)}), bf16[32,24,256]{2,1,0:T(8,128)(2,1)S(1)}, u32[]{:S(2)}, u32[]{:S(2)}) async-start(bf16[32,24,256]{2,1,0:T(8,128)(2,1)} %gradient.1), calls=%async_computation | async-start | bytes 786432 | tf_op jit(solution)/shard_map/all_to_all | solution.py:683
  17.7 3.7 %planes.1 = (bf16[768,384]{1,0:T(8,128)(2,1)}, bf16[768,384]{1,0:T(8,128)(2,1)}, bf16[768,384]{1,0:T(8,128)(2,1)}, bf16[768,384]{1,0:T(8,128)(2,1)}, bf16[768,38...) custom-call(s32[1]{0:T(128)} %bitcast.1.core_ref, ...), custom_call_target="tpu_custom_call" | custom-call | bytes 10000000 | tf_op jit(solution)/shard_map/planes/pallas_call | solution.py:548
  21.4 0.2 collective-permute-start.2
  21.7 0.4 collective-permute-start.3
  22.0 0.1 collective-permute-start.4
  22.2 0.4 collective-permute-start.5
  22.5 3.2 %slopes.1.slopes_ref = f32[26,128,384]{2,1,0:T(8,128)} custom-call(s32[1]{0:T(128)} %bitcast.1.core_ref, f32[2,4,384]{2,1,0:T(4,128)S(1)} %collective-permute-done.partner_ref, f32[2,4,384]{2,1,0:T(4,128)S(1)} %collective-permute-done.1.neighbour_ref, bf16[2,128,96]{2,1,0:T(8,128)(2,1)S(1)} %get-tuple-element.23.front_ref, ...), custom_call_target="tpu_custom_call" | custom-call | flops 1000000000 | bytes 6000000 | tf_op jit(solution)/shard_map/slopes/pallas_call | solution.py:570
  25.7 6.9 %all-to-all-done = bf16[32,24,256]{2,1,0:T(8,128)(2,1)S(1)} async-done(((bf16[32,24,256]{2,1,0:T(8,128)(2,1)}), bf16[32,24,256]{2,1,0:T(8,128)(2,1)S(1)}, u32[]{:S(2)}, u32[]{:S(2)}) %all-to-all-start) | async-done | bytes 393248 | tf_op jit(solution)/shard_map/all_to_all | solution.py:683
  32.6 1.8 %collective-permute-start.6 = (bf16[768,128]{1,0:T(8,128)(2,1)S(1)}, bf16[768,128]{1,0:T(8,128)(2,1)S(1)}, u32[]{:S(2)}, u32[]{:S(2)}) collective-permute-start(bf16[768,128]{1,0:T(8,128)(2,1)S(1)} %slice_select_fusion), channel_id=1, source_target_pairs={{0,2},{1,3},{2,0},{3,1},{4,6},{5,7},{6,4},{7,5},{8,10},{9,11},{10,... | collective-permute-start | bytes 589832 | tf_op jit(solution)/shard_map/ppermute | solution.py:690
  34.4 0.0 collective-permute-done.2.refs_4_
  34.4 0.0 collective-permute-done.3.refs_5_
  34.4 0.0 collective-permute-done.4.refs_6_
  34.4 0.0 collective-permute-done.5.refs_7_
  34.4 0.0 slice-start
  34.4 4.1 %members.2 = bf16[32,32,128]{2,1,0:T(8,128)(2,1)S(1)} custom-call(s32[1]{0:T(128)S(6)} %sub.8.half_ref, bf16[768,384]{1,0:T(8,128)(2,1)} %get-tuple-element.29.refs_0_, bf16[768,384]{1,0:T(8,128)(2,1)} %get-tuple-element.30.refs_1_, bf16[768,384]{1,0:T(8,128)(2,1)} %get-tuple-element.31.refs_2_, bf16[768,384]{1,0:T(8,128)(2,1)} %get-tuple-element.32.refs_3_, ...), custom_call_target="tpu_custom_call" | custom-call | flops 2048000000 | bytes 4000000 | tf_op jit(solution)/shard_map/members/pallas_call | solution.py:598
  38.5 0.0 slice-start.1
  38.5 0.6 collective-permute-start.7
  39.1 0.0 collective-permute-done.6.refs_9_
  39.1 5.4 %members.3.own_ref = f32[32,56,128]{2,1,0:T(8,128)S(1)} custom-call(s32[1]{0:T(128)} %bitcast.half_ref, bf16[768,384]{1,0:T(8,128)(2,1)} %get-tuple-element.29.refs_0_, bf16[768,384]{1,0:T(8,128)(2,1)} %get-tuple-element.30.refs_1_, bf16[768,384]{1,0:T(8,128)(2,1)} %get-tuple-element.31.refs_2_, bf16[768,384]{1,0:T(8,128)(2,1)} %get-tuple-element.32.refs_3_, ...), custom_call_target="tpu_custom_call" | custom-call | flops 4096000000 | bytes 4000000 | tf_op jit(solution)/shard_map/members/pallas_call | solution.py:598
  44.5 1.3 %collective-permute-done.7.other_ref = bf16[32,32,128]{2,1,0:T(8,128)(2,1)S(1)} collective-permute-done((bf16[32,32,128]{2,1,0:T(8,128)(2,1)S(1)}, bf16[32,32,128]{2,1,0:T(8,128)(2,1)S(1)}, u32[]{:S(2)}, u32[]{:S(2)}) %collective-permute-start.7) | collective-permute-done | bytes 262176 | tf_op jit(solution)/shard_map/ppermute | solution.py:693
  45.8 0.1 add_parts.1
  45.8 20.1 %all_to_all.15.refs_0_ = bf16[32,56,128]{2,1,0:T(8,128)(2,1)S(1)} all-to-all(bf16[32,56,128]{2,1,0:T(8,128)(2,1)S(1)} %add_parts.1), channel_id=1, replica_groups=mesh['space'=32,'mem'=8] {'space'}, dimensions={0} | all-to-all | bytes 917504 | tf_op jit(solution)/shard_map/all_to_all | solution.py:695
  66.0 0.1 block_sum.1
  66.1 14.1 %all_to_all.16.copies_ref = bf16[8,112,128]{2,1,0:T(8,128)(2,1)S(1)} all-to-all(bf16[8,112,128]{2,1,0:T(8,128)(2,1)S(1)} %block_sum.1), channel_id=1, replica_groups=mesh['space'=32,'mem'=8] {'mem'}, dimensions={0} | all-to-all | bytes 458752 | tf_op jit(solution)/shard_map/all_to_all | solution.py:697
  80.2 0.0 slice-done
  80.2 0.0 slice-done.1
  80.2 2.6 %response.1 = (f32[24,2,384]{2,1,0:T(2,128)}, f32[24,2,384]{2,1,0:T(2,128)}) custom-call(bf16[8,112,128]{2,1,0:T(8,128)(2,1)S(1)} %all_to_all.16.copies_ref, f32[26,128,384]{2,1,0:T(8,128)S(1)} %bitcast.6, bf16[2,128,96]{2,1,0:T(8,128)(2,1)S(1)} %get-tuple-element.23.front_ref, bf16[2,48,256]{2,1,0:T(8,128)(2,1)S(1)} %get-tuple-element.24.back_ref), custom_call_target="tpu_custom_call" | custom-call | tf_op jit(solution)/shard_map/response/pallas_call | solution.py:646
  (3 shorter events, 0.0 us)
Async XLA Ops:
  1.4 5.6 %collective-permute-start.1 = (f32[2,4,384]{2,1,0:T(4,128)S(1)}, f32[2,4,384]{2,1,0:T(4,128)S(1)}, u32[]{:S(2)}, u32[]{:S(2)}) collective-permute-start(f32[2,4,384]{2,1,0:T(4,128)S(1)} %get-tuple-element.46), channel_id=1, source_target_pairs={{0,248},{8,16},{16,8},{24,32},{32,24},{40,48},{48,40},{56,64},{64,... | collective-permute-start | bytes 36872 | tf_op jit(solution)/shard_map/ppermute | solution.py:670
  1.5 5.5 %collective-permute-start = (f32[2,4,384]{2,1,0:T(4,128)S(1)}, f32[2,4,384]{2,1,0:T(4,128)S(1)}, u32[]{:S(2)}, u32[]{:S(2)}) collective-permute-start(f32[2,4,384]{2,1,0:T(4,128)S(1)} %get-tuple-element.47), channel_id=1, source_target_pairs={{0,8},{8,0},{16,24},{24,16},{32,40},{40,32},{48,56},{56,48},{64,72... | collective-permute-start | bytes 36872 | tf_op jit(solution)/shard_map/ppermute | solution.py:671
  8.5 24.1 %all-to-all-start = ((bf16[32,24,256]{2,1,0:T(8,128)(2,1)}), bf16[32,24,256]{2,1,0:T(8,128)(2,1)S(1)}, u32[]{:S(2)}, u32[]{:S(2)}) async-start(bf16[32,24,256]{2,1,0:T(8,128)(2,1)} %gradient.1), calls=%async_computation | async-start | bytes 786432 | tf_op jit(solution)/shard_map/all_to_all | solution.py:683
  21.4 13.0 %collective-permute-start.2 = (bf16[768,384]{1,0:T(8,128)(2,1)}, bf16[768,384]{1,0:T(8,128)(2,1)S(1)}, u32[]{:S(2)}, u32[]{:S(2)}) collective-permute-start(bf16[768,384]{1,0:T(8,128)(2,1)} %get-tuple-element.33), channel_id=1, source_target_pairs={{0,8},{8,0},{16,24},{24,16},{32,40},{40,32},{48,56},{56,48},{64,72... | collective-permute-start | bytes 1769480 | tf_op jit(solution)/shard_map/ppermute | solution.py:685
  21.7 12.7 %collective-permute-start.3 = (bf16[768,384]{1,0:T(8,128)(2,1)}, bf16[768,384]{1,0:T(8,128)(2,1)S(1)}, u32[]{:S(2)}, u32[]{:S(2)}) collective-permute-start(bf16[768,384]{1,0:T(8,128)(2,1)} %get-tuple-element.34), channel_id=1, source_target_pairs={{0,8},{8,0},{16,24},{24,16},{32,40},{40,32},{48,56},{56,48},{64,72... | collective-permute-start | bytes 1769480 | tf_op jit(solution)/shard_map/ppermute | solution.py:685
  22.0 12.4 %collective-permute-start.4 = (bf16[768,384]{1,0:T(8,128)(2,1)}, bf16[768,384]{1,0:T(8,128)(2,1)S(1)}, u32[]{:S(2)}, u32[]{:S(2)}) collective-permute-start(bf16[768,384]{1,0:T(8,128)(2,1)} %get-tuple-element.35), channel_id=1, source_target_pairs={{0,8},{8,0},{16,24},{24,16},{32,40},{40,32},{48,56},{56,48},{64,72... | collective-permute-start | bytes 1769480 | tf_op jit(solution)/shard_map/ppermute | solution.py:685
  22.2 12.2 %collective-permute-start.5 = (bf16[768,384]{1,0:T(8,128)(2,1)}, bf16[768,384]{1,0:T(8,128)(2,1)S(1)}, u32[]{:S(2)}, u32[]{:S(2)}) collective-permute-start(bf16[768,384]{1,0:T(8,128)(2,1)} %get-tuple-element.36), channel_id=1, source_target_pairs={{0,8},{8,0},{16,24},{24,16},{32,40},{40,32},{48,56},{56,48},{64,72... | collective-permute-start | bytes 1769480 | tf_op jit(solution)/shard_map/ppermute | solution.py:685
  32.6 6.5 %collective-permute-start.6 = (bf16[768,128]{1,0:T(8,128)(2,1)S(1)}, bf16[768,128]{1,0:T(8,128)(2,1)S(1)}, u32[]{:S(2)}, u32[]{:S(2)}) collective-permute-start(bf16[768,128]{1,0:T(8,128)(2,1)S(1)} %slice_select_fusion), channel_id=1, source_target_pairs={{0,2},{1,3},{2,0},{3,1},{4,6},{5,7},{6,4},{7,5},{8,10},{9,11},{10,... | collective-permute-start | bytes 589832 | tf_op jit(solution)/shard_map/ppermute | solution.py:690
  34.4 45.8 %slice-start = ((s8[5111808]{0:T(1024)(128)(4,1)}), s8[4194304]{0:T(1024)(128)(4,1)S(1)}, s32[]{:S(2)}) async-start(s8[5111808]{0:T(1024)(128)(4,1)} %bitcast.5), calls=%async_computation.3 | async-start | bytes 8388608
  38.5 41.7 %slice-start.1 = ((s8[5111808]{0:T(1024)(128)(4,1)}), s8[917504]{0:T(1024)(128)(4,1)S(1)}, s32[]{:S(2)}) async-start(s8[5111808]{0:T(1024)(128)(4,1)} %bitcast.5), calls=%async_computation.4 | async-start | bytes 1835008
  38.5 7.3 %collective-permute-start.7 = (bf16[32,32,128]{2,1,0:T(8,128)(2,1)S(1)}, bf16[32,32,128]{2,1,0:T(8,128)(2,1)S(1)}, u32[]{:S(2)}, u32[]{:S(2)}) collective-permute-start(bf16[32,32,128]{2,1,0:T(8,128)(2,1)S(1)} %members.2), channel_id=1, source_target_pairs={{0,2},{1,3},{2,0},{3,1},{4,6},{5,7},{6,4},{7,5},{8,10},{9,11},{10,... | collective-permute-start | bytes 786440 | tf_op jit(solution)/shard_map/ppermute | solution.py:693

commit v8 on v7

--- a/solution.py
+++ b/solution.py
@@ -11,7 +11,7 @@
 
 HALF = 16
 GROUP = 32
-BATCH = 11
+BATCH = 6
 BF = jnp.bfloat16
 F32 = jnp.float32
 

time: 83.2 us -> 83.2 us (level)
  no operation moved by 1% of the time
where the time goes in v8:
time: 83.2 us; the launch traced here: 82.7 us
  blocking collectives  34.3 us (41%)
  Pallas kernels  24.1 us (29%)
  starting transfers between devices  14.7 us (18%)
  waiting for transfers between devices  8.15 us (10%)
    all_to_all x1, blocking collectives, per_device(): arrived = [lax.all_to_all(add_parts(own, other), 'space', 0, 0, tiled=True)]  20.1 us
    all_to_all x1, blocking collectives, per_device(): copies = lax.all_to_all(spread, 'mem', 0, 0, tiled=True)  14.1 us
    pallas_call x2, Pallas kernels, member_sums(): pl.pallas_call(functools.partial(member_kernel, span, count), in_specs=[S...  9.45 us
    all_to_all x1, starting transfers between devices, per_device(): gathered = lax.all_to_all(outgoing, 'space', 0, 0, tiled=True)  9.19 us
    all_to_all x1, waiting for transfers between devices, per_device(): gathered = lax.all_to_all(outgoing, 'space', 0, 0, tiled=True)  6.86 us
    pallas_call x1, Pallas kernels, member_planes(): pl.pallas_call(planes_kernel, in_specs=[SCALAR, FAR], out_specs=[FAR] * (...  3.7 us
    pallas_call x1, Pallas kernels, prepare(): pl.pallas_call(prepare_kernel, out_shape=[shape_of(2, hidden, 3 * GROUP),...  3.48 us
    pallas_call x1, Pallas kernels, hidden_slopes(): pl.pallas_call(slopes_kernel, out_shape=pltpu.HBM((rows + 2, hidden, lats...  3.21 us
  transfers between devices with their start and end apart: 9, of which 2 were waited for; matrix products, arithmetic and copies ran while one was open for 0% of the time, Pallas kernels for 24%

profile of v8, /device:TPU:8, one launch (start us, length us, event | category | flops | bytes accessed | tf_op | source)
XLA Modules:
  0.0 82.7 jit_solution(15146636938084291802)
XLA Ops:
  0.6 0.8 fusion.2
  1.4 0.1 collective-permute-start.1
  1.5 1.9 %collective-permute-start = (f32[2,4,384]{2,1,0:T(4,128)S(1)}, f32[2,4,384]{2,1,0:T(4,128)S(1)}, u32[]{:S(2)}, u32[]{:S(2)}) collective-permute-start(f32[2,4,384]{2,1,0:T(4,128)S(1)} %get-tuple-element.47), channel_id=1, source_target_pairs={{0,8},{8,0},{16,24},{24,16},{32,40},{40,32},{48,56},{56,48},{64,72... | collective-permute-start | bytes 36872 | tf_op jit(solution)/shard_map/ppermute | solution.py:671
  3.4 3.5 %prepare.1 = (bf16[2,128,96]{2,1,0:T(8,128)(2,1)S(1)}, bf16[2,48,256]{2,1,0:T(8,128)(2,1)S(1)}, bf16[768,384]{1,0:T(8,128)(2,1)S(1)}, bf16[768,384]{1,0:T(8,128)...) custom-call(f32[24,2,384]{2,1,0:T(2,128)} %state_far.1, f32[24,2,384]{2,1,0:T(2,128)} %cot_far.1, ...), custom_call_target="tpu_custom_call" | custom-call | flops 2000000000 | bytes 3000000 | tf_op jit(solution)/shard_map/prepare/pallas_call | solution.py:492
  6.9 0.0 collective-permute-done.1.neighbour_ref
  7.0 0.0 collective-permute-done.partner_ref
  7.0 1.5 %gradient.1 = bf16[32,24,256]{2,1,0:T(8,128)(2,1)} custom-call(s32[1]{0:T(128)} %bitcast.1.core_ref, s32[1]{0:T(128)} %bitcast.half_ref, f32[2,24,384]{2,1,0:T(8,128)S(1)} %get-tuple-element.22.cot_planes, f32[2,4,384]{2,1,0:T(4,128)S(1)} %collective-permute-done.partner_ref, f32[2,4,384]{2,1,0:T(4,128)S(1)} %collective-permute-done.1.neighbour_ref, ...), custom_call_target="tpu_custom_call" | custom-call | flops 400000000 | bytes 1500000 | tf_op jit(solution)/shard_map/gradient/pallas_call | solution.py:526
  8.5 9.2 %all-to-all-start = ((bf16[32,24,256]{2,1,0:T(8,128)(2,1)}), bf16[32,24,256]{2,1,0:T(8,128)(2,1)S(1)}, u32[]{:S(2)}, u32[]{:S(2)}) async-start(bf16[32,24,256]{2,1,0:T(8,128)(2,1)} %gradient.1), calls=%async_computation | async-start | bytes 786432 | tf_op jit(solution)/shard_map/all_to_all | solution.py:683
  17.7 3.7 %planes.1 = (bf16[768,384]{1,0:T(8,128)(2,1)}, bf16[768,384]{1,0:T(8,128)(2,1)}, bf16[768,384]{1,0:T(8,128)(2,1)}, bf16[768,384]{1,0:T(8,128)(2,1)}, bf16[768,38...) custom-call(s32[1]{0:T(128)} %bitcast.1.core_ref, ...), custom_call_target="tpu_custom_call" | custom-call | bytes 10000000 | tf_op jit(solution)/shard_map/planes/pallas_call | solution.py:548
  21.4 0.2 collective-permute-start.2
  21.6 0.4 collective-permute-start.3
  22.0 0.1 collective-permute-start.4
  22.1 0.4 collective-permute-start.5
  22.5 3.2 %slopes.1.slopes_ref = f32[26,128,384]{2,1,0:T(8,128)} custom-call(s32[1]{0:T(128)} %bitcast.1.core_ref, f32[2,4,384]{2,1,0:T(4,128)S(1)} %collective-permute-done.partner_ref, f32[2,4,384]{2,1,0:T(4,128)S(1)} %collective-permute-done.1.neighbour_ref, bf16[2,128,96]{2,1,0:T(8,128)(2,1)S(1)} %get-tuple-element.23.front_ref, ...), custom_call_target="tpu_custom_call" | custom-call | flops 1000000000 | bytes 6000000 | tf_op jit(solution)/shard_map/slopes/pallas_call | solution.py:570
  25.7 6.9 %all-to-all-done = bf16[32,24,256]{2,1,0:T(8,128)(2,1)S(1)} async-done(((bf16[32,24,256]{2,1,0:T(8,128)(2,1)}), bf16[32,24,256]{2,1,0:T(8,128)(2,1)S(1)}, u32[]{:S(2)}, u32[]{:S(2)}) %all-to-all-start) | async-done | bytes 393248 | tf_op jit(solution)/shard_map/all_to_all | solution.py:683
  32.6 1.8 %collective-permute-start.6 = (bf16[768,128]{1,0:T(8,128)(2,1)S(1)}, bf16[768,128]{1,0:T(8,128)(2,1)S(1)}, u32[]{:S(2)}, u32[]{:S(2)}) collective-permute-start(bf16[768,128]{1,0:T(8,128)(2,1)S(1)} %slice_select_fusion), channel_id=1, source_target_pairs={{0,2},{1,3},{2,0},{3,1},{4,6},{5,7},{6,4},{7,5},{8,10},{9,11},{10,... | collective-permute-start | bytes 589832 | tf_op jit(solution)/shard_map/ppermute | solution.py:690
  34.4 0.0 collective-permute-done.2.refs_4_
  34.4 0.0 collective-permute-done.3.refs_5_
  34.4 0.0 collective-permute-done.4.refs_6_
  34.4 0.0 collective-permute-done.5.refs_7_
  34.4 0.0 slice-start
  34.4 4.1 %members.2 = bf16[32,32,128]{2,1,0:T(8,128)(2,1)S(1)} custom-call(s32[1]{0:T(128)S(6)} %sub.8.half_ref, bf16[768,384]{1,0:T(8,128)(2,1)} %get-tuple-element.29.refs_0_, bf16[768,384]{1,0:T(8,128)(2,1)} %get-tuple-element.30.refs_1_, bf16[768,384]{1,0:T(8,128)(2,1)} %get-tuple-element.31.refs_2_, bf16[768,384]{1,0:T(8,128)(2,1)} %get-tuple-element.32.refs_3_, ...), custom_call_target="tpu_custom_call" | custom-call | flops 2048000000 | bytes 4000000 | tf_op jit(solution)/shard_map/members/pallas_call | solution.py:598
  38.5 0.0 slice-start.1
  38.5 0.6 collective-permute-start.7
  39.1 0.0 collective-permute-done.6.refs_9_
  39.1 5.4 %members.3.own_ref = f32[32,56,128]{2,1,0:T(8,128)S(1)} custom-call(s32[1]{0:T(128)} %bitcast.half_ref, bf16[768,384]{1,0:T(8,128)(2,1)} %get-tuple-element.29.refs_0_, bf16[768,384]{1,0:T(8,128)(2,1)} %get-tuple-element.30.refs_1_, bf16[768,384]{1,0:T(8,128)(2,1)} %get-tuple-element.31.refs_2_, bf16[768,384]{1,0:T(8,128)(2,1)} %get-tuple-element.32.refs_3_, ...), custom_call_target="tpu_custom_call" | custom-call | flops 4096000000 | bytes 4000000 | tf_op jit(solution)/shard_map/members/pallas_call | solution.py:598
  44.5 1.3 %collective-permute-done.7.other_ref = bf16[32,32,128]{2,1,0:T(8,128)(2,1)S(1)} collective-permute-done((bf16[32,32,128]{2,1,0:T(8,128)(2,1)S(1)}, bf16[32,32,128]{2,1,0:T(8,128)(2,1)S(1)}, u32[]{:S(2)}, u32[]{:S(2)}) %collective-permute-start.7) | collective-permute-done | bytes 262176 | tf_op jit(solution)/shard_map/ppermute | solution.py:693
  45.7 0.1 add_parts.1
  45.8 20.1 %all_to_all.15.refs_0_ = bf16[32,56,128]{2,1,0:T(8,128)(2,1)S(1)} all-to-all(bf16[32,56,128]{2,1,0:T(8,128)(2,1)S(1)} %add_parts.1), channel_id=1, replica_groups=mesh['space'=32,'mem'=8] {'space'}, dimensions={0} | all-to-all | bytes 917504 | tf_op jit(solution)/shard_map/all_to_all | solution.py:695
  65.9 0.1 block_sum.1
  66.0 14.1 %all_to_all.16.copies_ref = bf16[8,112,128]{2,1,0:T(8,128)(2,1)S(1)} all-to-all(bf16[8,112,128]{2,1,0:T(8,128)(2,1)S(1)} %block_sum.1), channel_id=1, replica_groups=mesh['space'=32,'mem'=8] {'mem'}, dimensions={0} | all-to-all | bytes 458752 | tf_op jit(solution)/shard_map/all_to_all | solution.py:697
  80.2 0.0 slice-done
  80.2 0.0 slice-done.1
  80.2 2.6 %response.1 = (f32[24,2,384]{2,1,0:T(2,128)}, f32[24,2,384]{2,1,0:T(2,128)}) custom-call(bf16[8,112,128]{2,1,0:T(8,128)(2,1)S(1)} %all_to_all.16.copies_ref, f32[26,128,384]{2,1,0:T(8,128)S(1)} %bitcast.6, bf16[2,128,96]{2,1,0:T(8,128)(2,1)S(1)} %get-tuple-element.23.front_ref, bf16[2,48,256]{2,1,0:T(8,128)(2,1)S(1)} %get-tuple-element.24.back_ref), custom_call_target="tpu_custom_call" | custom-call | tf_op jit(solution)/shard_map/response/pallas_call | solution.py:646
  (3 shorter events, 0.0 us)
Async XLA Ops:
  1.4 5.5 %collective-permute-start.1 = (f32[2,4,384]{2,1,0:T(4,128)S(1)}, f32[2,4,384]{2,1,0:T(4,128)S(1)}, u32[]{:S(2)}, u32[]{:S(2)}) collective-permute-start(f32[2,4,384]{2,1,0:T(4,128)S(1)} %get-tuple-element.46), channel_id=1, source_target_pairs={{0,248},{8,16},{16,8},{24,32},{32,24},{40,48},{48,40},{56,64},{64,... | collective-permute-start | bytes 36872 | tf_op jit(solution)/shard_map/ppermute | solution.py:670
  1.5 5.4 %collective-permute-start = (f32[2,4,384]{2,1,0:T(4,128)S(1)}, f32[2,4,384]{2,1,0:T(4,128)S(1)}, u32[]{:S(2)}, u32[]{:S(2)}) collective-permute-start(f32[2,4,384]{2,1,0:T(4,128)S(1)} %get-tuple-element.47), channel_id=1, source_target_pairs={{0,8},{8,0},{16,24},{24,16},{32,40},{40,32},{48,56},{56,48},{64,72... | collective-permute-start | bytes 36872 | tf_op jit(solution)/shard_map/ppermute | solution.py:671
  8.5 24.1 %all-to-all-start = ((bf16[32,24,256]{2,1,0:T(8,128)(2,1)}), bf16[32,24,256]{2,1,0:T(8,128)(2,1)S(1)}, u32[]{:S(2)}, u32[]{:S(2)}) async-start(bf16[32,24,256]{2,1,0:T(8,128)(2,1)} %gradient.1), calls=%async_computation | async-start | bytes 786432 | tf_op jit(solution)/shard_map/all_to_all | solution.py:683
  21.4 13.0 %collective-permute-start.2 = (bf16[768,384]{1,0:T(8,128)(2,1)}, bf16[768,384]{1,0:T(8,128)(2,1)S(1)}, u32[]{:S(2)}, u32[]{:S(2)}) collective-permute-start(bf16[768,384]{1,0:T(8,128)(2,1)} %get-tuple-element.33), channel_id=1, source_target_pairs={{0,8},{8,0},{16,24},{24,16},{32,40},{40,32},{48,56},{56,48},{64,72... | collective-permute-start | bytes 1769480 | tf_op jit(solution)/shard_map/ppermute | solution.py:685
  21.6 12.7 %collective-permute-start.3 = (bf16[768,384]{1,0:T(8,128)(2,1)}, bf16[768,384]{1,0:T(8,128)(2,1)S(1)}, u32[]{:S(2)}, u32[]{:S(2)}) collective-permute-start(bf16[768,384]{1,0:T(8,128)(2,1)} %get-tuple-element.34), channel_id=1, source_target_pairs={{0,8},{8,0},{16,24},{24,16},{32,40},{40,32},{48,56},{56,48},{64,72... | collective-permute-start | bytes 1769480 | tf_op jit(solution)/shard_map/ppermute | solution.py:685
  22.0 12.4 %collective-permute-start.4 = (bf16[768,384]{1,0:T(8,128)(2,1)}, bf16[768,384]{1,0:T(8,128)(2,1)S(1)}, u32[]{:S(2)}, u32[]{:S(2)}) collective-permute-start(bf16[768,384]{1,0:T(8,128)(2,1)} %get-tuple-element.35), channel_id=1, source_target_pairs={{0,8},{8,0},{16,24},{24,16},{32,40},{40,32},{48,56},{56,48},{64,72... | collective-permute-start | bytes 1769480 | tf_op jit(solution)/shard_map/ppermute | solution.py:685
  22.1 12.2 %collective-permute-start.5 = (bf16[768,384]{1,0:T(8,128)(2,1)}, bf16[768,384]{1,0:T(8,128)(2,1)S(1)}, u32[]{:S(2)}, u32[]{:S(2)}) collective-permute-start(bf16[768,384]{1,0:T(8,128)(2,1)} %get-tuple-element.36), channel_id=1, source_target_pairs={{0,8},{8,0},{16,24},{24,16},{32,40},{40,32},{48,56},{56,48},{64,72... | collective-permute-start | bytes 1769480 | tf_op jit(solution)/shard_map/ppermute | solution.py:685
  32.6 6.5 %collective-permute-start.6 = (bf16[768,128]{1,0:T(8,128)(2,1)S(1)}, bf16[768,128]{1,0:T(8,128)(2,1)S(1)}, u32[]{:S(2)}, u32[]{:S(2)}) collective-permute-start(bf16[768,128]{1,0:T(8,128)(2,1)S(1)} %slice_select_fusion), channel_id=1, source_target_pairs={{0,2},{1,3},{2,0},{3,1},{4,6},{5,7},{6,4},{7,5},{8,10},{9,11},{10,... | collective-permute-start | bytes 589832 | tf_op jit(solution)/shard_map/ppermute | solution.py:690
  34.4 45.8 %slice-start = ((s8[5111808]{0:T(1024)(128)(4,1)}), s8[4194304]{0:T(1024)(128)(4,1)S(1)}, s32[]{:S(2)}) async-start(s8[5111808]{0:T(1024)(128)(4,1)} %bitcast.5), calls=%async_computation.3 | async-start | bytes 8388608
  38.5 41.7 %slice-start.1 = ((s8[5111808]{0:T(1024)(128)(4,1)}), s8[917504]{0:T(1024)(128)(4,1)S(1)}, s32[]{:S(2)}) async-start(s8[5111808]{0:T(1024)(128)(4,1)} %bitcast.5), calls=%async_computation.4 | async-start | bytes 1835008
  38.5 7.2 %collective-permute-start.7 = (bf16[32,32,128]{2,1,0:T(8,128)(2,1)S(1)}, bf16[32,32,128]{2,1,0:T(8,128)(2,1)S(1)}, u32[]{:S(2)}, u32[]{:S(2)}) collective-permute-start(bf16[32,32,128]{2,1,0:T(8,128)(2,1)S(1)} %members.2), channel_id=1, source_target_pairs={{0,2},{1,3},{2,0},{3,1},{4,6},{5,7},{6,4},{7,5},{8,10},{9,11},{10,... | collective-permute-start | bytes 786440 | tf_op jit(solution)/shard_map/ppermute | solution.py:693
